TPU v7x, 32 devices: a whole 2x2x4 slice. The times are simulated.
32 devices in a mesh: seq: 4 (over z), ep: 8 (over y, x, core).
Axes of the slice: x: 2, y: 2, z: 4, core: 2. Of those that a mesh axis runs over, the one named last changes fastest.
Arguments:
- tokens: bfloat16 [4096, 2048], P(('seq', 'ep')), may hold values from -60 to 60
- expert_ids: int32 [4096, 8], P(('seq', 'ep')), may hold values from 0 to 31, all different within a row; in each aligned block of 128 rows (0 to 127, 128 to 255, ...) at most 48 rows name the same one
- route_weights: float32 [4096, 8], P(('seq', 'ep')), may hold values from 0.05 to 0.45
- norm_gain: float32 [2048], replicated, may hold values from 0.1 to 1.9
- gate_proj: bfloat16 [32, 2048, 768], P(('seq', 'ep')), may hold values from -0.125 to 0.125
- up_proj: bfloat16 [32, 2048, 768], P(('seq', 'ep')), may hold values from -0.125 to 0.125
- down_proj: bfloat16 [32, 768, 2048], P(('seq', 'ep')), may hold values from -0.21875 to 0.21875
- out_grad: bfloat16 [4096, 2048], P(('seq', 'ep')), may hold values from -6 to 6
Outputs:
- moe_out: bfloat16 [4096, 2048], P(('seq', 'ep'))
- in_grad: bfloat16 [4096, 2048], P(('seq', 'ep'))
Inputs may be any that keep to these rules, and one draw needn't show every extreme that they name: `expert_ids`: in the rows of one device no expert is named more than 48 times, and in every draw some device names some expert exactly 48 times.
All inputs are finite; a program needn't handle non-finite values.
Results may differ from a plain program's by a relative error of at most 0.0071.
Values may be sent and summed in bfloat16 or wider, within the bound.
No kernel may reach another device: no remote copies, remote signals or barrier semaphores. Data moves between devices by JAX's collectives and lax.ppermute only.
A program may use at most 192 MiB of HBM per device.

v0:
```python
import jax
import jax.numpy as jnp
from jax import lax
from jax.sharding import PartitionSpec as P

EPS = 1e-06


def scale_rows(values, norm_gain):
    mean_square = jnp.mean(values * values, axis=-1, keepdims=True)
    return values * lax.rsqrt(mean_square + EPS) * norm_gain


def expert_forward(inputs, gate_w, up_w, down_w):
    gate_act = jnp.dot(inputs, gate_w, preferred_element_type=jnp.float32)
    upward = jnp.dot(inputs, up_w, preferred_element_type=jnp.float32)
    hidden = (jax.nn.silu(gate_act) * upward).astype(jnp.bfloat16)
    result = jnp.dot(hidden, down_w, preferred_element_type=jnp.float32).astype(jnp.bfloat16)
    return (result, gate_act, upward)


def expert_backward(grads, gate_act, upward, gate_w, up_w, down_w):
    pairs = (((1,), (1,)), ((), ()))
    grad_hidden = lax.dot_general(grads, down_w, pairs, preferred_element_type=jnp.float32)
    sigmoid_gate = jax.nn.sigmoid(gate_act)
    grad_gate = (
        grad_hidden * upward * sigmoid_gate * (1.0 + gate_act * (1.0 - sigmoid_gate))
    ).astype(jnp.bfloat16)
    grad_up = (grad_hidden * (gate_act * sigmoid_gate)).astype(jnp.bfloat16)
    summed = lax.dot_general(grad_gate, gate_w, pairs, preferred_element_type=jnp.float32)
    summed = summed + lax.dot_general(grad_up, up_w, pairs, preferred_element_type=jnp.float32)
    return summed.astype(jnp.bfloat16)


def move_out(slots):
    arrived = lax.all_to_all(slots, ("seq", "ep"), split_axis=0, concat_axis=0, tiled=True)
    return arrived


def move_back(slots):
    arrived = lax.all_to_all(slots, ("seq", "ep"), split_axis=0, concat_axis=0, tiled=True)
    return arrived


def run_live(compute, inputs):
    outputs = list(compute(inputs))
    return outputs


def shards(tokens, expert_ids, route_weights, norm_gain, gate_proj, up_proj, down_proj, out_grad):
    own_weights = (gate_proj[0], up_proj[0], down_proj[0])
    experts = lax.axis_size("seq") * lax.axis_size("ep")
    tok_count, fanout = expert_ids.shape
    model_width = tokens.shape[1]
    capacity = max(2, 3 * tok_count * fanout // (2 * experts))
    zero_value = jnp.zeros((), jnp.bfloat16)
    x_float = tokens.astype(jnp.float32)
    normed = scale_rows(x_float, norm_gain).astype(jnp.bfloat16)
    flat_ids = expert_ids.reshape(-1)
    one_hot = (flat_ids[:, None] == jnp.arange(experts, dtype=jnp.int32)[None, :]).astype(jnp.int32)
    slot_rank = jnp.sum((jnp.cumsum(one_hot, axis=0) - one_hot) * one_hot, axis=1)
    groups = [(0, capacity, own_weights)]
    position = flat_ids * capacity + slot_rank
    slot_route = (
        jnp.full((experts * capacity,), -1, jnp.int32)
        .at[position]
        .set(jnp.arange(flat_ids.shape[0], dtype=jnp.int32))
    )
    alive_slot = slot_route >= 0
    source = jnp.maximum(slot_route, 0) // fanout
    outgoing = jnp.where(alive_slot[:, None], normed[source], zero_value).reshape(
        experts, capacity, model_width
    )
    arrived = move_out(outgoing)
    first, width, weight_set = groups[0]
    inputs = arrived.reshape(-1, model_width)
    alive_rows = jnp.any(inputs != 0, axis=1)

    def forward_pass(parts, weight_set=weight_set):
        return expert_forward(parts[0], *weight_set)

    result, gate_act, upward = run_live(forward_pass, [inputs])
    saved = [(gate_act, upward, alive_rows)]
    result_parts = result.reshape(experts, width, model_width)
    route_out = move_back(result_parts).reshape(-1, model_width)[position]
    outgoing_grad = jnp.where(alive_slot[:, None], out_grad[source], zero_value).reshape(
        experts, capacity, model_width
    )
    grads_arrived = move_out(outgoing_grad)
    grad_parts = []
    for (first, width, weight_set), (gate_act, upward, alive_rows) in zip(groups, saved):
        grads = grads_arrived.reshape(-1, model_width)

        def backward_pass(parts, weight_set=weight_set):
            return (expert_backward(parts[0], parts[1], parts[2], *weight_set),)

        grad_rows = run_live(backward_pass, [grads, gate_act, upward])[0]
        grad_parts.append(grad_rows.reshape(experts, width, model_width))
    route_grad = move_back(grad_parts[0]).reshape(-1, model_width)[position]
    weight_cube = route_weights[:, :, None]
    moe_out = jnp.sum(
        weight_cube * route_out.reshape(tok_count, fanout, model_width).astype(jnp.float32), axis=1
    ).astype(jnp.bfloat16)
    grad_normed = jnp.sum(
        weight_cube * route_grad.reshape(tok_count, fanout, model_width).astype(jnp.float32), axis=1
    )

    def normalize(values):
        return scale_rows(values, norm_gain)

    _, pullback = jax.vjp(normalize, x_float)
    in_grad = pullback(grad_normed)[0].astype(jnp.bfloat16)
    return (moe_out, in_grad)


def solution(mesh):
    return jax.shard_map(
        shards,
        mesh=mesh,
        in_specs=(
            P(("seq", "ep"), None),
            P(("seq", "ep"), None),
            P(("seq", "ep"), None),
            P(),
            P(("seq", "ep"), None, None),
            P(("seq", "ep"), None, None),
            P(("seq", "ep"), None, None),
            P(("seq", "ep"), None),
        ),
        out_specs=(P(("seq", "ep"), None), P(("seq", "ep"), None)),
        check_vma=False,
    )
```

profile of v0, /device:TPU:0, one launch (start us, length us, event | category | flops | bytes accessed | tf_op | source)
XLA Modules:
  0.0 656.4 jit_solution(9774408032234985553)
XLA Ops:
  2.8 9.0 %reduce-window.6 = s32[32,8,128]{2,1,0:T(8,128)S(1)} reduce-window(s32[32,8,128]{2,1,0:T(8,128)S(1)} %fusion.24, s32[]{:T(128)} %constant.36.clone.1), window={size=1x1x128 pad=0_0x0_0x127_0}, to_apply=%region_0.0 | reduce-window | flops 4161536 | bytes 262148 | tf_op jit(solution)/shard_map/reduce-window
  12.3 4.3 scatter_custom_fusion
  16.7 1.2 fusion.15
  18.0 2.0 fusion.17
  20.1 13.8 %gather_fusion = bf16[1536,2048]{1,0:T(8,128)(2,1)} fusion(bf16[128,2048]{1,0:T(8,128)(2,1)} %fusion.17, s32[2048]{0:T(1024)S(1)} %pad_clamp_fusion), kind=kCustom, calls=%fused_computation | custom fusion | bytes 12589056 | tf_op jit(solution)/shard_map/gather | solution.py:71
  33.9 13.8 %gather_fusion.2 = bf16[1536,2048]{1,0:T(8,128)(2,1)} fusion(bf16[128,2048]{1,0:T(8,128)(2,1)} %param.15, s32[2048]{0:T(1024)S(1)} %pad_clamp_fusion), kind=kCustom, calls=%fused_computation.2 | custom fusion | bytes 12589056 | tf_op jit(solution)/shard_map/gather | solution.py:86
  47.7 8.2 %broadcast_select_fusion = (bf16[32,48,2048]{2,1,0:T(8,128)(2,1)}, bf16[32,48,2048]{2,1,0:T(8,128)(2,1)S(1)}) fusion(bf16[32,48,2048]{2,1,0:T(8,128)(2,1)} %bitcast.54, pred[32,48]{1,0:T(8,128)(4,1)S(1)} %broadcast_in_dim.40, bf16[32,48,2048]{2,1,0:T(8,128)(2,1)} %bitcast.53), kind=kLoop, calls=%fused_computation.11 | loop fusion | flops 6291456 | bytes 25167360 | tf_op jit(solution)/shard_map/jit(_where)/select_n | solution.py:86
  55.9 145.8 %all_to_all.20 = bf16[32,48,2048]{2,1,0:T(8,128)(2,1)} all-to-all(bf16[32,48,2048]{2,1,0:T(8,128)(2,1)S(1)} %get-tuple-element.5), channel_id=1, replica_groups=mesh['seq'=4,'ep'=8] {'seq','ep'}, dimensions={0} | all-to-all | bytes 12582912 | tf_op jit(solution)/shard_map/all_to_all | solution.py:36
  201.7 4.0 all-to-all-start.2
  205.8 8.2 %fusion.11 = f32[1536,768]{1,0:T(8,128)S(1)} fusion(bf16[1536,2048]{1,0:T(8,128)(2,1)} %bitcast.57, bf16[1,2048,768]{2,1,0:T(8,128)(2,1)} %param.12), kind=kOutput, calls=%fused_computation.26 | convolution fusion | flops 4831838208 | bytes 14155776 | tf_op jit(solution)/shard_map/dot_general | solution.py:15
  214.1 5.2 fusion.7
  219.2 2.1 copy-done.15
  221.4 7.0 %convolution_convert_fusion = bf16[1536,2048]{1,0:T(8,128)(2,1)} fusion(bf16[1,768,2048]{2,1,0:T(8,128)(2,1)S(1)} %copy-done, f32[1536,768]{1,0:T(8,128)S(1)} %fusion.7, f32[1536,768]{1,0:T(8,128)S(1)} %fusion.11), kind=kOutput, calls=%fused_computation.10 | convolution fusion | flops 4842061824 | bytes 18874368 | tf_op jit(solution)/shard_map/dot_general | solution.py:18
  228.4 117.3 %all-to-all-done.2 = bf16[32,48,2048]{2,1,0:T(8,128)(2,1)} async-done(((bf16[32,48,2048]{2,1,0:T(8,128)(2,1)}), bf16[32,48,2048]{2,1,0:T(8,128)(2,1)}, u32[]{:S(2)}, u32[]{:S(2)}) %all-to-all-start.2) | async-done | bytes 6291488 | tf_op jit(solution)/shard_map/all_to_all | solution.py:36
  345.7 3.8 all-to-all-start.1
  349.6 8.7 %fusion.3 = f32[1536,768]{1,0:T(8,128)} fusion(bf16[1536,2048]{1,0:T(8,128)(2,1)} %bitcast.13, bf16[1,768,2048]{2,1,0:T(8,128)(2,1)S(1)} %copy-done), kind=kOutput, calls=%fused_computation.18 | convolution fusion | flops 4831838208 | bytes 14155776 | tf_op jit(solution)/shard_map/dot_general | solution.py:24
  358.3 13.1 %fusion.9 = f32[1536,2048]{1,0:T(8,128)} fusion(bf16[1,2048,768]{2,1,0:T(8,128)(2,1)S(1)} %copy-done.10, f32[1536,768]{1,0:T(8,128)S(1)} %copy-done.14, f32[1536,768]{1,0:T(8,128)} %fusion.3, f32[1536,768]{1,0:T(8,128)S(1)} %copy-done.16), kind=kOutput, calls=%fused_computation.24 | convolution fusion | flops 4843634688 | bytes 29884416 | tf_op jit(solution)/shard_map/dot_general | solution.py:30
  371.4 11.5 %add_convert_fusion = bf16[1536,2048]{1,0:T(8,128)(2,1)} fusion(f32[1536,2048]{1,0:T(8,128)} %fusion.9, bf16[1,2048,768]{2,1,0:T(8,128)(2,1)S(1)} %copy-done.12, f32[1536,768]{1,0:T(8,128)} %fusion.3, f32[1536,768]{1,0:T(8,128)S(1)} %copy-done.14), kind=kOutput, calls=%fused_computation.5 | convolution fusion | flops 4845207552 | bytes 31457280 | tf_op jit(solution)/shard_map/dot_general | solution.py:31
  383.0 106.4 %all-to-all-done.1 = bf16[32,48,2048]{2,1,0:T(8,128)(2,1)} async-done(((bf16[32,48,2048]{2,1,0:T(8,128)(2,1)}), bf16[32,48,2048]{2,1,0:T(8,128)(2,1)}, u32[]{:S(2)}, u32[]{:S(2)}) %all-to-all-start.1) | async-done | bytes 6291488 | tf_op jit(solution)/shard_map/all_to_all | solution.py:41
  489.4 4.0 all-to-all-start.3
  493.5 12.4 %gather_fusion.1 = bf16[1024,2048]{1,0:T(8,128)(2,1)} fusion(bf16[1536,2048]{1,0:T(8,128)(2,1)} %bitcast.10, s32[1024]{0:T(1024)S(1)} %broadcast_clamp_fusion), kind=kCustom, calls=%fused_computation.1 | custom fusion | bytes 8392704 | tf_op jit(solution)/shard_map/gather | solution.py:85
  505.9 127.3 %all-to-all-done.3 = bf16[32,48,2048]{2,1,0:T(8,128)(2,1)} async-done(((bf16[32,48,2048]{2,1,0:T(8,128)(2,1)}), bf16[32,48,2048]{2,1,0:T(8,128)(2,1)}, u32[]{:S(2)}, u32[]{:S(2)}) %all-to-all-start.3) | async-done | bytes 6291488 | tf_op jit(solution)/shard_map/all_to_all | solution.py:41
  633.2 12.6 %gather_fusion.3 = bf16[1024,2048]{1,0:T(8,128)(2,1)} fusion(bf16[1536,2048]{1,0:T(8,128)(2,1)} %bitcast.15, s32[1024]{0:T(1024)S(1)} %broadcast_clamp_fusion), kind=kCustom, calls=%fused_computation.3 | custom fusion | bytes 8392704 | tf_op jit(solution)/shard_map/gather | solution.py:99
  645.8 9.3 %fusion = (f32[128,2048]{1,0:T(8,128)S(1)}, bf16[128,2048]{1,0:T(8,128)(2,1)}) fusion(bf16[1024,2048]{1,0:T(8,128)(2,1)} %gather_fusion.3, f32[128,8]{1,0:T(8,128)S(1)} %copy.11, bf16[1024,2048]{1,0:T(8,128)(2,1)} %gather_fusion.1), kind=kLoop, calls=%fused_computation.7 | loop fusion | flops 12058624 | bytes 9965568 | tf_op jit(solution)/shard_map/reduce_sum | solution.py:104
  (59 shorter events, 4.2 us)
Async XLA Ops:
  0.6 220.7 %copy-start = (bf16[1,768,2048]{2,1,0:T(8,128)(2,1)S(1)}, bf16[1,768,2048]{2,1,0:T(8,128)(2,1)}, u32[]{:S(2)}) copy-start(bf16[1,768,2048]{2,1,0:T(8,128)(2,1)} %param.14) | copy-start | bytes 9437188
  17.9 16.0 %copy-start.8 = (f32[128]{0:T(128)}, f32[128]{0:T(128)S(1)}, u32[]{:S(2)}) copy-start(f32[128]{0:T(128)S(1)} %fusion.15) | copy-start | bytes 1540
  17.9 16.0 %copy-start.6 = (f32[128]{0:T(128)}, f32[128]{0:T(128)S(1)}, u32[]{:S(2)}) copy-start(f32[128]{0:T(128)S(1)} %fusion.28) | copy-start | bytes 1540
  201.7 144.0 %all-to-all-start.2 = ((bf16[32,48,2048]{2,1,0:T(8,128)(2,1)}), bf16[32,48,2048]{2,1,0:T(8,128)(2,1)}, u32[]{:S(2)}, u32[]{:S(2)}) async-start(bf16[32,48,2048]{2,1,0:T(8,128)(2,1)} %get-tuple-element.4), calls=%async_computation.2 | async-start | bytes 12582912 | tf_op jit(solution)/shard_map/all_to_all | solution.py:36
  205.8 8.3 %copy-start.3 = (bf16[32,48,2048]{2,1,0:T(8,128)(2,1)S(1)}, bf16[32,48,2048]{2,1,0:T(8,128)(2,1)}, u32[]{:S(2)}) copy-start(bf16[32,48,2048]{2,1,0:T(8,128)(2,1)} %all_to_all.20) | copy-start | bytes 18874372
  205.8 8.3 %copy-start.11 = (bf16[1,2048,768]{2,1,0:T(8,128)(2,1)S(1)}, bf16[1,2048,768]{2,1,0:T(8,128)(2,1)}, u32[]{:S(2)}) copy-start(bf16[1,2048,768]{2,1,0:T(8,128)(2,1)} %param.13) | copy-start | bytes 9437188
  214.1 5.2 copy-start.13
  219.2 2.1 copy-start.15
  345.7 143.7 %all-to-all-start.1 = ((bf16[32,48,2048]{2,1,0:T(8,128)(2,1)}), bf16[32,48,2048]{2,1,0:T(8,128)(2,1)}, u32[]{:S(2)}, u32[]{:S(2)}) async-start(bf16[32,48,2048]{2,1,0:T(8,128)(2,1)} %bitcast.55), calls=%async_computation.1 | async-start | bytes 12582912 | tf_op jit(solution)/shard_map/all_to_all | solution.py:41
  349.5 8.8 %copy-start.10 = (bf16[1,2048,768]{2,1,0:T(8,128)(2,1)S(1)}, bf16[1,2048,768]{2,1,0:T(8,128)(2,1)}, u32[]{:S(2)}) copy-start(bf16[1,2048,768]{2,1,0:T(8,128)(2,1)} %param.12) | copy-start | bytes 9437188
  349.5 8.8 %copy-start.14 = (f32[1536,768]{1,0:T(8,128)S(1)}, f32[1536,768]{1,0:T(8,128)}, u32[]{:S(2)}) copy-start(f32[1536,768]{1,0:T(8,128)} %copy-done.13) | copy-start | bytes 14155780
  349.6 8.8 %copy-start.16 = (f32[1536,768]{1,0:T(8,128)S(1)}, f32[1536,768]{1,0:T(8,128)}, u32[]{:S(2)}) copy-start(f32[1536,768]{1,0:T(8,128)} %copy-done.15) | copy-start | bytes 14155780
  358.3 13.1 %copy-start.12 = (bf16[1,2048,768]{2,1,0:T(8,128)(2,1)S(1)}, bf16[1,2048,768]{2,1,0:T(8,128)(2,1)}, u32[]{:S(2)}) copy-start(bf16[1,2048,768]{2,1,0:T(8,128)(2,1)} %param.13) | copy-start | bytes 9437188
  489.4 4.0 copy-start.5
  489.4 143.8 %all-to-all-start.3 = ((bf16[32,48,2048]{2,1,0:T(8,128)(2,1)}), bf16[32,48,2048]{2,1,0:T(8,128)(2,1)}, u32[]{:S(2)}, u32[]{:S(2)}) async-start(bf16[32,48,2048]{2,1,0:T(8,128)(2,1)} %bitcast.56), calls=%async_computation.3 | async-start | bytes 12582912 | tf_op jit(solution)/shard_map/all_to_all | solution.py:41
  633.2 23.2 %copy-start.1 = (bf16[1,768,2048]{2,1,0:T(8,128)(2,1)S(1)}, bf16[1,768,2048]{2,1,0:T(8,128)(2,1)}, u32[]{:S(2)}) copy-start(bf16[1,768,2048]{2,1,0:T(8,128)(2,1)} %param.14) | copy-start | bytes 9437188
  645.8 9.3 %copy-start.2 = (bf16[128,2048]{1,0:T(8,128)(2,1)S(1)}, bf16[128,2048]{1,0:T(8,128)(2,1)}, u32[]{:S(2)}) copy-start(bf16[128,2048]{1,0:T(8,128)(2,1)} %param.8) | copy-start | bytes 1572868
  645.8 9.3 %copy-start.4 = (f32[2048]{0:T(1024)S(1)}, f32[2048]{0:T(1024)}, u32[]{:S(2)}) copy-start(f32[2048]{0:T(1024)} %param.11) | copy-start | bytes 24580
  645.8 9.5 %copy-start.9 = (f32[128]{0:T(128)S(1)}, f32[128]{0:T(128)}, u32[]{:S(2)}) copy-start(f32[128]{0:T(128)} %copy-done.8) | copy-start | bytes 1540
  645.8 9.5 %copy-start.7 = (f32[128]{0:T(128)S(1)}, f32[128]{0:T(128)}, u32[]{:S(2)}) copy-start(f32[128]{0:T(128)} %copy-done.6) | copy-start | bytes 1540
where the time goes:
time: 657 us; the launch traced here: 656 us
  waiting for transfers between devices  351 us (53%)
  blocking collectives  146 us (22%)
  local copies, waits for them, and re-layouts  60.9 us (9%)
  matrix products  53.7 us (8%)
  other arithmetic  32.1 us (5%)
  starting transfers between devices  11.9 us (2%)
    all_to_all x2, waiting for transfers between devices, move_back(): lax.all_to_all(slots, ('seq', 'ep'), split_axis=0, concat_axis=0, tiled=T...  234 us
    all_to_all x1, blocking collectives, move_out(): lax.all_to_all(slots, ('seq', 'ep'), split_axis=0, concat_axis=0, tiled=T...  146 us
    all_to_all x1, waiting for transfers between devices, move_out(): lax.all_to_all(slots, ('seq', 'ep'), split_axis=0, concat_axis=0, tiled=T...  117 us
    gather x1, local copies, waits for them, and re-layouts, shards(): normed[source]  13.8 us
    gather x1, local copies, waits for them, and re-layouts, shards(): out_grad[source]  13.8 us
  transfers between devices with their start and end apart: 3, of which 3 were waited for; matrix products, arithmetic and copies ran while one was open for 10% of the time, Pallas kernels for 0%

commit v1 on v0

--- a/solution.py
+++ b/solution.py
@@ -1,14 +1,321 @@
+import functools
+
 import jax
 import jax.numpy as jnp
 from jax import lax
+from jax.experimental import pallas as pl
+from jax.experimental.pallas import tpu as pltpu
 from jax.sharding import PartitionSpec as P
 
 EPS = 1e-06
+PAIRS = (((1,), (1,)), ((), ()))
+BF16, F32 = jnp.bfloat16, jnp.float32
 
 
 def scale_rows(values, norm_gain):
     mean_square = jnp.mean(values * values, axis=-1, keepdims=True)
     return values * lax.rsqrt(mean_square + EPS) * norm_gain
+
+
+def norm_grad(x_float, norm_gain, grad):
+    def normalize(values):
+        return scale_rows(values, norm_gain)
+
+    _, pullback = jax.vjp(normalize, x_float)
+    return pullback(grad)[0].astype(BF16)
+
+
+def slot_tables(index_ref, table_ref, onehot, factor, ranks, blocks, cap):
+    tok = table_ref.shape[2]
+    marks = jnp.concatenate(
+        [jnp.where(table_ref[index_ref[b]] > 0.0, 1.0, 0.0).astype(BF16) for b in range(blocks)], axis=0
+    )
+    before = lax.broadcasted_iota(jnp.int32, (tok, tok), 0) < lax.broadcasted_iota(jnp.int32, (tok, tok), 1)
+    ranks[...] = jnp.dot(marks, jnp.where(before, 1.0, 0.0).astype(BF16), preferred_element_type=F32)
+    slots = lax.broadcasted_iota(jnp.int32, (cap, tok), 0).astype(F32)
+    for b in range(blocks):
+        weights = table_ref[index_ref[b]]
+        for e in range(2):
+            weight = weights[e : e + 1, :]
+            rank = jnp.where(weight > 0.0, ranks[2 * b + e : 2 * b + e + 1, :], -1.0)
+            hit = slots == rank
+            onehot[b, e * cap : (e + 1) * cap, :] = jnp.where(hit, 1.0, 0.0).astype(BF16)
+            slot_weight = jnp.sum(jnp.where(hit, weight, 0.0), axis=1, keepdims=True)
+            factor[e, b * cap : (b + 1) * cap, :] = jnp.broadcast_to(slot_weight, (cap, tok))
+
+
+def pick_rows(sources, onehot, rows, cap):
+    for b, (ref, at) in enumerate(sources):
+        tok = onehot.shape[2]
+        picked = jnp.dot(onehot[b], ref[at * tok : (at + 1) * tok, :], preferred_element_type=F32).astype(BF16)
+        rows[0, b * cap : (b + 1) * cap, :] = picked[:cap]
+        rows[1, b * cap : (b + 1) * cap, :] = picked[cap:]
+
+
+def put_rows(targets, onehot, rows, cap):
+    tok = onehot.shape[2]
+    for b, (ref, at) in enumerate(targets):
+        both = jnp.concatenate([rows[0, b * cap : (b + 1) * cap, :], rows[1, b * cap : (b + 1) * cap, :]], axis=0)
+        summed = lax.dot_general(onehot[b], both, (((0,), (0,)), ((), ())), preferred_element_type=F32)
+        ref[at * tok : (at + 1) * tok, :] = summed.astype(BF16)
+
+
+def scaled(total, factor):
+    return (total * factor).astype(BF16)
+
+
+def forward_kernel(cap, in_map, out_map, n_in, n_out, index_ref, *refs):
+    table_ref = refs[0]
+    ins = refs[1 : 1 + n_in]
+    weights = refs[1 + n_in : 7 + n_in]
+    outs = refs[7 + n_in : 7 + n_in + n_out]
+    gate_ref, up_ref = refs[7 + n_in + n_out : 9 + n_in + n_out]
+    onehot, factor, ranks, rows, total = refs[9 + n_in + n_out :]
+    step = pl.program_id(0)
+    tiles = pl.num_programs(0) // 2
+
+    @pl.when(step == 0)
+    def _():
+        slot_tables(index_ref, table_ref, onehot, factor, ranks, len(in_map), cap)
+        pick_rows([(ins[i], at) for i, at in in_map], onehot, rows, cap)
+
+    def expert(e, gate_w, up_w, down_w):
+        inputs = rows[e]
+        gate_act = jnp.dot(inputs, gate_w[...], preferred_element_type=F32)
+        upward = jnp.dot(inputs, up_w[...], preferred_element_type=F32)
+        gate_ref[...] = gate_act
+        up_ref[...] = upward
+        hidden = (gate_act * jax.nn.sigmoid(gate_act) * upward).astype(BF16)
+        part = jnp.dot(hidden, down_w[...], preferred_element_type=F32)
+
+        @pl.when(step == e * tiles)
+        def _():
+            total[...] = part
+
+        @pl.when(step > e * tiles)
+        def _():
+            total[...] += part
+
+        @pl.when(step == (e + 1) * tiles - 1)
+        def _():
+            rows[e] = scaled(total[...], factor[e][:, :1])
+
+    @pl.when(step < tiles)
+    def _():
+        expert(0, *weights[:3])
+
+    @pl.when(step >= tiles)
+    def _():
+        expert(1, *weights[3:])
+
+    @pl.when(step == 2 * tiles - 1)
+    def _():
+        put_rows([(outs[i], at) for i, at in out_map], onehot, rows, cap)
+
+
+def backward_kernel(cap, in_map, out_map, n_in, n_out, index_ref, *refs):
+    table_ref = refs[0]
+    ins = refs[1 : 1 + n_in]
+    weights = refs[1 + n_in : 7 + n_in]
+    gate_ref, up_ref = refs[7 + n_in : 9 + n_in]
+    outs = refs[9 + n_in : 9 + n_in + n_out]
+    onehot, factor, ranks, rows, total = refs[9 + n_in + n_out :]
+    step = pl.program_id(0)
+    tiles = pl.num_programs(0) // 2
+
+    @pl.when(step == 0)
+    def _():
+        slot_tables(index_ref, table_ref, onehot, factor, ranks, len(in_map), cap)
+        pick_rows([(ins[i], at) for i, at in in_map], onehot, rows, cap)
+
+    def expert(e, gate_w, up_w, down_w):
+        grad_hidden = lax.dot_general(rows[e], down_w[...], PAIRS, preferred_element_type=F32)
+        gate_act = gate_ref[...]
+        sigmoid = jax.nn.sigmoid(gate_act)
+        grad_gate = (grad_hidden * up_ref[...] * sigmoid * (1.0 + gate_act * (1.0 - sigmoid))).astype(BF16)
+        grad_up = (grad_hidden * (gate_act * sigmoid)).astype(BF16)
+        part = lax.dot_general(grad_gate, gate_w[...], PAIRS, preferred_element_type=F32)
+        part = part + lax.dot_general(grad_up, up_w[...], PAIRS, preferred_element_type=F32)
+
+        @pl.when(step == e * tiles)
+        def _():
+            total[...] = part
+
+        @pl.when(step > e * tiles)
+        def _():
+            total[...] += part
+
+        @pl.when(step == (e + 1) * tiles - 1)
+        def _():
+            rows[e] = scaled(total[...], factor[e][:, :1])
+
+    @pl.when(step < tiles)
+    def _():
+        expert(0, *weights[:3])
+
+    @pl.when(step >= tiles)
+    def _():
+        expert(1, *weights[3:])
+
+    @pl.when(step == 2 * tiles - 1)
+    def _():
+        put_rows([(outs[i], at) for i, at in out_map], onehot, rows, cap)
+
+
+def run_experts(kernel, index, table, ins, in_map, weights, acts, out_rows, out_map, cap):
+    width = ins[0].shape[1]
+    ff = weights[0].shape[1]
+    tile = 256 if ff % 256 == 0 else ff
+    tiles = ff // tile
+    slots = len(in_map) * cap
+    tok = table.shape[2]
+    once = pl.Buffered(1)
+
+    def whole(shape):
+        return pl.BlockSpec(shape, lambda i, s: (0,) * len(shape), pipeline_mode=once)
+
+    def columns(e):
+        at = (lambda i: jnp.minimum(i, tiles - 1)) if e == 0 else (lambda i: jnp.maximum(i - tiles, 0))
+        side = pl.BlockSpec((width, tile), lambda i, s: (0, at(i)))
+        return [side, side, pl.BlockSpec((tile, width), lambda i, s: (at(i), 0))]
+
+    act_spec = pl.BlockSpec((None, slots, tile), lambda i, s: (i // tiles, 0, i % tiles))
+    in_specs = [whole(table.shape)] + [whole(a.shape) for a in ins] + columns(0) + columns(1)
+    out_specs = [whole((r, width)) for r in out_rows]
+    out_shape = [jax.ShapeDtypeStruct((r, width), BF16) for r in out_rows]
+    operands = [index, table, *ins, *weights]
+    if acts is None:
+        out_specs += [act_spec] * 2
+        out_shape += [jax.ShapeDtypeStruct((2, slots, ff), F32)] * 2
+    else:
+        in_specs += [act_spec] * 2
+        operands += list(acts)
+    return pl.pallas_call(
+        functools.partial(kernel, cap, in_map, out_map, len(ins), len(out_rows)),
+        out_shape=out_shape,
+        grid_spec=pltpu.PrefetchScalarGridSpec(
+            num_scalar_prefetch=1,
+            grid=(2 * tiles,),
+            in_specs=in_specs,
+            out_specs=out_specs,
+            scratch_shapes=[
+                pltpu.VMEM((len(in_map), 2 * cap, tok), BF16),
+                pltpu.VMEM((2, slots, tok), F32),
+                pltpu.VMEM((2 * len(in_map), tok), F32),
+                pltpu.VMEM((2, slots, width), BF16),
+                pltpu.VMEM((slots, width), F32),
+            ],
+        ),
+        compiler_params=pltpu.CompilerParams(
+            dimension_semantics=("arbitrary",), vmem_limit_bytes=56 << 20
+        ),
+        cost_estimate=pl.CostEstimate(
+            flops=2 * 2 * 3 * slots * width * ff,
+            bytes_accessed=2 * (6 * width * ff + 2 * len(in_map) * tok * width) + 16 * slots * ff,
+            transcendentals=2 * slots * ff,
+        ),
+    )(*operands)
+
+
+def ep_permute(value, partner):
+    return lax.ppermute(value, "ep", [(i, partner(i)) for i in range(8)])
+
+
+def first(value):
+    return ep_permute(value, lambda i: i ^ (4 if i & 1 else 2))
+
+
+def second(value):
+    return ep_permute(value, lambda i: i ^ (2 if i & 1 else 4))
+
+
+def along_z(value, k):
+    return lax.ppermute(value, "seq", [(i, i ^ k) for i in range(4)])
+
+
+def spread(own):
+    zs = [own] + [along_z(own, k) for k in (1, 2, 3)]
+    arrays, names = [], []
+    last0 = None
+    for k in range(4):
+        a = first(zs[k])
+        if k == 1:
+            b = along_z(last0, 1)
+        else:
+            b = second(jnp.concatenate([zs[k], a], axis=0))
+            last0 = b if k == 0 else last0
+        arrays += [zs[k], a, b]
+        names += [[(k, 0)], [(k, 1)], [(k, 2), (k, 3)]]
+    return arrays, names
+
+
+def add(*values):
+    total = values[0].astype(F32)
+    for value in values[1:]:
+        total = total + value.astype(F32)
+    return total
+
+
+def merge(near, far):
+    tok = near[0].shape[0] // 2
+    from_z = along_z(far[1], 1)
+    sums = {}
+    for k in (3, 2, 1, 0):
+        part = near[k]
+        if k != 1:
+            send = far[k] if k else add(far[0], from_z).astype(BF16)
+            got = second(send)
+            other = add(part[tok:], got[tok:]).astype(BF16)
+            mine = add(part[:tok], got[:tok])
+        else:
+            other = part[tok:]
+            mine = part[:tok].astype(F32)
+        mine = mine + first(other).astype(F32)
+        sums[k] = along_z(mine.astype(BF16), k).astype(F32) if k else mine
+    return sums[0] + sums[1] + sums[2] + sums[3]
+
+
+def gathered(tokens, expert_ids, route_weights, norm_gain, gate_proj, up_proj, down_proj, out_grad):
+    experts = lax.axis_size("seq") * lax.axis_size("ep")
+    tok, fanout = expert_ids.shape
+    cap = max(2, 3 * tok * fanout // (2 * experts))
+    mine = (gate_proj[0], up_proj[0], down_proj[0])
+    theirs = tuple(ep_permute(w, lambda i: i ^ 1) for w in mine)
+    core = lax.axis_index("ep") % 2
+
+    ids = jnp.arange(experts, dtype=jnp.int32)
+    routes = jnp.sum(
+        jnp.where(expert_ids[:, :, None] == ids[None, None, :], route_weights[:, :, None], 0.0), axis=1
+    )
+    pairs = routes.T.reshape(experts // 2, 2, tok)
+    for_device = jnp.stack([pairs, pairs[:, ::-1]], axis=1).reshape(experts, 2 * tok)
+    table = lax.all_to_all(for_device, ("seq", "ep"), split_axis=0, concat_axis=0, tiled=True)
+    table = table.reshape(experts, 2, tok)
+
+    x_float = tokens.astype(F32)
+    normed = scale_rows(x_float, norm_gain).astype(BF16)
+    x_arrays, x_names = spread(normed)
+    g_arrays, _ = spread(out_grad)
+
+    z, ep = lax.axis_index("seq"), lax.axis_index("ep")
+    step_first = jnp.where(core == 1, 4, 2)
+    step_second = jnp.where(core == 1, 2, 4)
+    masks = [0, step_first, step_second, step_first | step_second]
+    names = [n for group in x_names for n in group]
+    index = jnp.stack([(z ^ k) * 8 + (ep ^ masks[j]) for k, j in names]).astype(jnp.int32)
+    in_map = [(i, at) for i, group in enumerate(x_names) for at in range(len(group))]
+    out_map = [(k if j < 2 else 4 + k, j % 2) for k, j in names]
+    out_rows = [2 * tok] * 8
+
+    results = run_experts(
+        forward_kernel, index, table, x_arrays, in_map, mine + theirs, None, out_rows, out_map, cap
+    )
+    moe_out = merge(results[0:4], results[4:8]).astype(BF16)
+    grads = run_experts(
+        backward_kernel, index, table, g_arrays, in_map, mine + theirs, results[8:10], out_rows, out_map, cap
+    )
+    grad_normed = merge(grads[0:4], grads[4:8])
+    return (moe_out, norm_grad(x_float, norm_gain, grad_normed))
 
 
 def expert_forward(inputs, gate_w, up_w, down_w):
@@ -47,7 +354,7 @@
     return outputs
 
 
-def shards(tokens, expert_ids, route_weights, norm_gain, gate_proj, up_proj, down_proj, out_grad):
+def exchanged(tokens, expert_ids, route_weights, norm_gain, gate_proj, up_proj, down_proj, out_grad):
     own_weights = (gate_proj[0], up_proj[0], down_proj[0])
     experts = lax.axis_size("seq") * lax.axis_size("ep")
     tok_count, fanout = expert_ids.shape
@@ -114,19 +421,13 @@
 
 
 def solution(mesh):
+    rows = P(("seq", "ep"), None)
+    cubes = P(("seq", "ep"), None, None)
+    planes = mesh.shape["seq"] == 4 and mesh.shape["ep"] == 8
     return jax.shard_map(
-        shards,
+        gathered if planes else exchanged,
         mesh=mesh,
-        in_specs=(
-            P(("seq", "ep"), None),
-            P(("seq", "ep"), None),
-            P(("seq", "ep"), None),
-            P(),
-            P(("seq", "ep"), None, None),
-            P(("seq", "ep"), None, None),
-            P(("seq", "ep"), None, None),
-            P(("seq", "ep"), None),
-        ),
-        out_specs=(P(("seq", "ep"), None), P(("seq", "ep"), None)),
+        in_specs=(rows, rows, rows, P(), cubes, cubes, cubes, rows),
+        out_specs=(rows, rows),
         check_vma=False,
     )

time: 657 us -> 440 us (0.67)
  blocking collectives: 146 us -> 0 us
  waiting for transfers between devices: 351 us -> 239 us
  starting transfers between devices: 11.9 us -> 103 us
  Pallas kernels: 0 us -> 80.5 us
  local copies, waits for them, and re-layouts: 60.9 us -> 6.68 us
  matrix products: 53.7 us -> 0 us
  other arithmetic: 32.1 us -> 8.92 us
    all_to_all x3 -> x1, waiting for transfers between devices: 351 us -> 0.01 us  [gathered(): lax.all_to_all(for_device, ('seq', 'ep'), split_axis=0, concat_axis=0, ti...]
    ppermute x0 -> x47, waiting for transfers between devices: none -> 239 us  [the longest x31 122 us: ep_permute(): return lax.ppermute(value, 'ep', [(i, partner(i)) for i in range(8)])]
    all_to_all x1 -> x0, blocking collectives: 146 us -> none  [move_out(): lax.all_to_all(slots, ('seq', 'ep'), split_axis=0, concat_axis=0, tiled=T...]
    ppermute x0 -> x47, starting transfers between devices: none -> 99.5 us  [the longest x16 70.2 us: along_z(): return lax.ppermute(value, 'seq', [(i, i ^ k) for i in range(4)])]
    pallas_call x0 -> x2, Pallas kernels: none -> 80.5 us  [run_experts(): pl.pallas_call(functools.partial(kernel, cap, in_map, out_map, len(ins),...]
    dot_general x6 -> x0, matrix products: 53.7 us -> none  [the longest x1 13.1 us: expert_backward(): lax.dot_general(grad_gate, gate_w, pairs, preferred_element_type=jnp.floa...]
    gather x4 -> x0, local copies, waits for them, and re-layouts: 52.6 us -> none  [the longest x1 13.8 us: shards(): normed[source]]
    reduce_sum x2 -> x1, other arithmetic: 9.3 us -> 0.02 us  [gathered(): jnp.sum(jnp.where(expert_ids[:, :, None] == ids[None, None, :], route_wei...]
  transfers between devices with their start and end apart: 3 -> 48, of which waited for: 3 -> 20; matrix products, arithmetic and copies ran while one was open for 10% -> 2% of each run, Pallas kernels for 0% -> 18%
where the time goes in v1:
time: 440 us; the launch traced here: 439 us
  waiting for transfers between devices  239 us (54%)
  starting transfers between devices  103 us (23%)
  Pallas kernels  80.5 us (18%)
  other arithmetic  8.92 us (2%)
  local copies, waits for them, and re-layouts  6.68 us (2%)
    ppermute x31, waiting for transfers between devices, ep_permute(): return lax.ppermute(value, 'ep', [(i, partner(i)) for i in range(8)])  122 us
    ppermute x16, waiting for transfers between devices, along_z(): return lax.ppermute(value, 'seq', [(i, i ^ k) for i in range(4)])  117 us
    pallas_call x2, Pallas kernels, run_experts(): pl.pallas_call(functools.partial(kernel, cap, in_map, out_map, len(ins),...  80.5 us
    ppermute x16, starting transfers between devices, along_z(): return lax.ppermute(value, 'seq', [(i, i ^ k) for i in range(4)])  70.2 us
    ppermute x31, starting transfers between devices, ep_permute(): return lax.ppermute(value, 'ep', [(i, partner(i)) for i in range(8)])  29.3 us
  transfers between devices with their start and end apart: 48, of which 20 were waited for; matrix products, arithmetic and copies ran while one was open for 2% of the time, Pallas kernels for 18%

profile of v1, /device:TPU:0, one launch (start us, length us, event | category | flops | bytes accessed | tf_op | source)
XLA Modules:
  0.0 439.4 jit_solution(12582847569827955880)
XLA Ops:
  3.2 3.0 collective-permute-start
  7.8 2.6 collective-permute-start.5
  15.5 15.9 %collective-permute-done.2.refs_4_ = bf16[128,2048]{1,0:T(8,128)(2,1)S(1)} collective-permute-done((bf16[128,2048]{1,0:T(8,128)(2,1)S(1)}, bf16[128,2048]{1,0:T(8,128)(2,1)S(1)}, u32[]{:S(2)}, u32[]{:S(2)}) %collective-permute-start.2) | collective-permute-done | bytes 524320 | tf_op jit(solution)/shard_map/ppermute | solution.py:233
  33.1 13.0 %collective-permute-done.5.refs_7_ = bf16[128,2048]{1,0:T(8,128)(2,1)S(1)} collective-permute-done((bf16[128,2048]{1,0:T(8,128)(2,1)S(1)}, bf16[128,2048]{1,0:T(8,128)(2,1)S(1)}, u32[]{:S(2)}, u32[]{:S(2)}) %collective-permute-start.5) | collective-permute-done | bytes 524320 | tf_op jit(solution)/shard_map/ppermute | solution.py:233
  50.6 3.5 collective-permute-done.27.refs_4_
  55.0 36.0 %collective-permute-done.30.refs_7_ = bf16[128,2048]{1,0:T(8,128)(2,1)S(1)} collective-permute-done((bf16[128,2048]{1,0:T(8,128)(2,1)}, bf16[128,2048]{1,0:T(8,128)(2,1)S(1)}, u32[]{:S(2)}, u32[]{:S(2)}) %collective-permute-start.30) | collective-permute-done | bytes 524320 | tf_op jit(solution)/shard_map/ppermute | solution.py:233
  93.9 13.5 %collective-permute-done.31.refs_8_ = bf16[128,2048]{1,0:T(8,128)(2,1)S(1)} collective-permute-done((bf16[128,2048]{1,0:T(8,128)(2,1)S(1)}, bf16[128,2048]{1,0:T(8,128)(2,1)S(1)}, u32[]{:S(2)}, u32[]{:S(2)}) %collective-permute-start.31) | collective-permute-done | bytes 524320 | tf_op jit(solution)/shard_map/ppermute | solution.py:221
  108.3 8.4 %collective-permute-done.34.refs_11_ = bf16[128,2048]{1,0:T(8,128)(2,1)S(1)} collective-permute-done((bf16[128,2048]{1,0:T(8,128)(2,1)S(1)}, bf16[128,2048]{1,0:T(8,128)(2,1)S(1)}, u32[]{:S(2)}, u32[]{:S(2)}) %collective-permute-start.34) | collective-permute-done | bytes 524320 | tf_op jit(solution)/shard_map/ppermute | solution.py:221
  118.7 12.8 %collective-permute-done.26.refs_3_ = bf16[256,2048]{1,0:T(8,128)(2,1)} collective-permute-done((bf16[256,2048]{1,0:T(8,128)(2,1)S(1)}, bf16[256,2048]{1,0:T(8,128)(2,1)}, u32[]{:S(2)}, u32[]{:S(2)}) %collective-permute-start.26) | collective-permute-done | bytes 1048608 | tf_op jit(solution)/shard_map/ppermute | solution.py:221
  131.5 11.1 %collective-permute-done.7.refs_9_ = bf16[256,2048]{1,0:T(8,128)(2,1)S(1)} collective-permute-done((bf16[256,2048]{1,0:T(8,128)(2,1)S(1)}, bf16[256,2048]{1,0:T(8,128)(2,1)S(1)}, u32[]{:S(2)}, u32[]{:S(2)}) %collective-permute-start.7) | collective-permute-done | bytes 1048608 | tf_op jit(solution)/shard_map/ppermute | solution.py:221
  142.7 13.3 %collective-permute-start.4 = (bf16[256,2048]{1,0:T(8,128)(2,1)}, bf16[256,2048]{1,0:T(8,128)(2,1)}, u32[]{:S(2)}, u32[]{:S(2)}) collective-permute-start(bf16[256,2048]{1,0:T(8,128)(2,1)} %collective-permute-done.1.refs_3_), channel_id=1, source_target_pairs={{0,8},{8,0},{16,24},{24,16},{1,9},{9,1},{17,25},{25,17},{2,10},{10... | collective-permute-start | bytes 3145736 | tf_op jit(solution)/shard_map/ppermute | solution.py:233
  156.7 3.7 all-to-all-start
  164.0 12.3 %collective-permute-done.4.refs_6_ = bf16[256,2048]{1,0:T(8,128)(2,1)} collective-permute-done((bf16[256,2048]{1,0:T(8,128)(2,1)}, bf16[256,2048]{1,0:T(8,128)(2,1)}, u32[]{:S(2)}, u32[]{:S(2)}) %collective-permute-start.4) | collective-permute-done | bytes 1048608 | tf_op jit(solution)/shard_map/ppermute | solution.py:233
  181.0 35.2 %shard_map.95 = (bf16[256,2048]{1,0:T(8,128)(2,1)}, bf16[256,2048]{1,0:T(8,128)(2,1)}, bf16[256,2048]{1,0:T(8,128)(2,1)}, bf16[256,2048]{1,0:T(8,128)(2,1)}, bf1...) custom-call(s32[16]{0:T(128)} %stack.73.index_ref, ...), custom_call_target="tpu_custom_call" | custom-call | flops 14495514624 | bytes 45088768 | tf_op jit(solution)/shard_map/pallas_call | solution.py:193
  220.4 45.3 %shard_map.96 = (bf16[256,2048]{1,0:T(8,128)(2,1)}, bf16[256,2048]{1,0:T(8,128)(2,1)}, bf16[256,2048]{1,0:T(8,128)(2,1)}, bf16[256,2048]{1,0:T(8,128)(2,1)}, bf1...) custom-call(s32[16]{0:T(128)} %stack.73.index_ref, ...), custom_call_target="tpu_custom_call" | custom-call | flops 14495514624 | bytes 45088768 | tf_op jit(solution)/shard_map/pallas_call | solution.py:193
  271.3 10.6 %collective-permute-done.39 = bf16[128,2048]{1,0:T(8,128)(2,1)S(1)} collective-permute-done((bf16[128,2048]{1,0:T(8,128)(2,1)S(1)}, bf16[128,2048]{1,0:T(8,128)(2,1)S(1)}, u32[]{:S(2)}, u32[]{:S(2)}) %collective-permute-start.39) | collective-permute-done | bytes 524320 | tf_op jit(solution)/shard_map/ppermute | solution.py:221
  285.7 10.4 %collective-permute-done.44 = bf16[256,2048]{1,0:T(8,128)(2,1)S(1)} collective-permute-done((bf16[256,2048]{1,0:T(8,128)(2,1)}, bf16[256,2048]{1,0:T(8,128)(2,1)S(1)}, u32[]{:S(2)}, u32[]{:S(2)}) %collective-permute-start.44) | collective-permute-done | bytes 1048608 | tf_op jit(solution)/shard_map/ppermute | solution.py:221
  296.9 16.0 %collective-permute-done.41 = bf16[256,2048]{1,0:T(8,128)(2,1)S(1)} collective-permute-done((bf16[256,2048]{1,0:T(8,128)(2,1)S(1)}, bf16[256,2048]{1,0:T(8,128)(2,1)S(1)}, u32[]{:S(2)}, u32[]{:S(2)}) %collective-permute-start.41) | collective-permute-done | bytes 1048608 | tf_op jit(solution)/shard_map/ppermute | solution.py:221
  320.5 15.1 %collective-permute-done.45 = bf16[128,2048]{1,0:T(8,128)(2,1)S(1)} collective-permute-done((bf16[128,2048]{1,0:T(8,128)(2,1)S(1)}, bf16[128,2048]{1,0:T(8,128)(2,1)S(1)}, u32[]{:S(2)}, u32[]{:S(2)}) %collective-permute-start.45) | collective-permute-done | bytes 524320 | tf_op jit(solution)/shard_map/ppermute | solution.py:221
  337.6 9.2 %collective-permute-done.42 = bf16[128,2048]{1,0:T(8,128)(2,1)S(1)} collective-permute-done((bf16[128,2048]{1,0:T(8,128)(2,1)S(1)}, bf16[128,2048]{1,0:T(8,128)(2,1)S(1)}, u32[]{:S(2)}, u32[]{:S(2)}) %collective-permute-start.42) | collective-permute-done | bytes 524320 | tf_op jit(solution)/shard_map/ppermute | solution.py:221
  350.6 11.2 %collective-permute-done.15 = bf16[256,2048]{1,0:T(8,128)(2,1)S(1)} collective-permute-done((bf16[256,2048]{1,0:T(8,128)(2,1)S(1)}, bf16[256,2048]{1,0:T(8,128)(2,1)S(1)}, u32[]{:S(2)}, u32[]{:S(2)}) %collective-permute-start.15) | collective-permute-done | bytes 1048608 | tf_op jit(solution)/shard_map/ppermute | solution.py:221
  364.5 37.7 %collective-permute-start.21 = (bf16[128,2048]{1,0:T(8,128)(2,1)S(1)}, bf16[128,2048]{1,0:T(8,128)(2,1)S(1)}, u32[]{:S(2)}, u32[]{:S(2)}) collective-permute-start(bf16[128,2048]{1,0:T(8,128)(2,1)S(1)} %add_convert_fusion.11), channel_id=1, source_target_pairs={{0,16},{8,24},{16,0},{24,8},{1,17},{9,25},{17,1},{25,9},{2,18},{10... | collective-permute-start | bytes 1572872 | tf_op jit(solution)/shard_map/ppermute | solution.py:233
  402.2 15.5 %collective-permute-done.43 = bf16[128,2048]{1,0:T(8,128)(2,1)S(1)} collective-permute-done((bf16[128,2048]{1,0:T(8,128)(2,1)S(1)}, bf16[128,2048]{1,0:T(8,128)(2,1)S(1)}, u32[]{:S(2)}, u32[]{:S(2)}) %collective-permute-start.43) | collective-permute-done | bytes 524320 | tf_op jit(solution)/shard_map/ppermute | solution.py:233
  419.5 18.6 %collective-permute-done.21 = bf16[128,2048]{1,0:T(8,128)(2,1)S(1)} collective-permute-done((bf16[128,2048]{1,0:T(8,128)(2,1)S(1)}, bf16[128,2048]{1,0:T(8,128)(2,1)S(1)}, u32[]{:S(2)}, u32[]{:S(2)}) %collective-permute-start.21) | collective-permute-done | bytes 524320 | tf_op jit(solution)/shard_map/ppermute | solution.py:233
  (182 shorter events, 64.5 us)
Async XLA Ops:
  7.8 38.3 %collective-permute-start.5 = (bf16[128,2048]{1,0:T(8,128)(2,1)S(1)}, bf16[128,2048]{1,0:T(8,128)(2,1)S(1)}, u32[]{:S(2)}, u32[]{:S(2)}) collective-permute-start(bf16[128,2048]{1,0:T(8,128)(2,1)S(1)} %fusion.3.refs_1_), channel_id=1, source_target_pairs={{0,16},{8,24},{16,0},{24,8},{1,17},{9,25},{17,1},{25,9},{2,18},{10... | collective-permute-start | bytes 1572872 | tf_op jit(solution)/shard_map/ppermute | solution.py:233
  10.6 38.4 %collective-permute-start.25 = (bf16[128,2048]{1,0:T(8,128)(2,1)}, bf16[128,2048]{1,0:T(8,128)(2,1)S(1)}, u32[]{:S(2)}, u32[]{:S(2)}) collective-permute-start(bf16[128,2048]{1,0:T(8,128)(2,1)} %refs_1_.1), channel_id=1, source_target_pairs={{0,2},{1,5},{2,0},{3,7},{4,6},{5,1},{6,4},{7,3},{8,10},{9,13},{10,... | collective-permute-start | bytes 1572872 | tf_op jit(solution)/shard_map/ppermute | solution.py:221
  13.4 40.7 %collective-permute-start.27 = (bf16[128,2048]{1,0:T(8,128)(2,1)}, bf16[128,2048]{1,0:T(8,128)(2,1)}, u32[]{:S(2)}, u32[]{:S(2)}) collective-permute-start(bf16[128,2048]{1,0:T(8,128)(2,1)} %refs_1_.1), channel_id=1, source_target_pairs={{0,8},{8,0},{16,24},{24,16},{1,9},{9,1},{17,25},{25,17},{2,10},{10... | collective-permute-start | bytes 1572872 | tf_op jit(solution)/shard_map/ppermute | solution.py:233
  31.4 59.6 %collective-permute-start.30 = (bf16[128,2048]{1,0:T(8,128)(2,1)}, bf16[128,2048]{1,0:T(8,128)(2,1)S(1)}, u32[]{:S(2)}, u32[]{:S(2)}) collective-permute-start(bf16[128,2048]{1,0:T(8,128)(2,1)} %refs_1_.1), channel_id=1, source_target_pairs={{0,16},{8,24},{16,0},{24,8},{1,17},{9,25},{17,1},{25,9},{2,18},{10... | collective-permute-start | bytes 1572872 | tf_op jit(solution)/shard_map/ppermute | solution.py:233
  46.0 46.5 %collective-permute-start.33 = (bf16[128,2048]{1,0:T(8,128)(2,1)}, bf16[128,2048]{1,0:T(8,128)(2,1)S(1)}, u32[]{:S(2)}, u32[]{:S(2)}) collective-permute-start(bf16[128,2048]{1,0:T(8,128)(2,1)} %refs_1_.1), channel_id=1, source_target_pairs={{0,24},{8,16},{16,8},{24,0},{1,25},{9,17},{17,9},{25,1},{2,26},{10... | collective-permute-start | bytes 1572872 | tf_op jit(solution)/shard_map/ppermute | solution.py:233
  48.5 44.5 %collective-permute-start.3 = (bf16[128,2048]{1,0:T(8,128)(2,1)S(1)}, bf16[128,2048]{1,0:T(8,128)(2,1)S(1)}, u32[]{:S(2)}, u32[]{:S(2)}) collective-permute-start(bf16[128,2048]{1,0:T(8,128)(2,1)S(1)} %collective-permute-done.2.refs_4_), channel_id=1, source_target_pairs={{0,2},{1,5},{2,0},{3,7},{4,6},{5,1},{6,4},{7,3},{8,10},{9,13},{10,... | collective-permute-start | bytes 1572872 | tf_op jit(solution)/shard_map/ppermute | solution.py:221
  49.0 44.1 %collective-permute-start.6 = (bf16[128,2048]{1,0:T(8,128)(2,1)S(1)}, bf16[128,2048]{1,0:T(8,128)(2,1)S(1)}, u32[]{:S(2)}, u32[]{:S(2)}) collective-permute-start(bf16[128,2048]{1,0:T(8,128)(2,1)S(1)} %collective-permute-done.5.refs_7_), channel_id=1, source_target_pairs={{0,2},{1,5},{2,0},{3,7},{4,6},{5,1},{6,4},{7,3},{8,10},{9,13},{10,... | collective-permute-start | bytes 1572872 | tf_op jit(solution)/shard_map/ppermute | solution.py:221
  54.0 39.5 %collective-permute-start.9 = (bf16[128,2048]{1,0:T(8,128)(2,1)S(1)}, bf16[128,2048]{1,0:T(8,128)(2,1)S(1)}, u32[]{:S(2)}, u32[]{:S(2)}) collective-permute-start(bf16[128,2048]{1,0:T(8,128)(2,1)S(1)} %collective-permute-done.8.refs_10_), channel_id=1, source_target_pairs={{0,2},{1,5},{2,0},{3,7},{4,6},{5,1},{6,4},{7,3},{8,10},{9,13},{10,... | collective-permute-start | bytes 1572872 | tf_op jit(solution)/shard_map/ppermute | solution.py:221
  93.1 85.3 %collective-permute-start.11 = (bf16[2048,768]{1,0:T(8,128)(2,1)}, bf16[2048,768]{1,0:T(8,128)(2,1)}, u32[]{:S(2)}, u32[]{:S(2)}) collective-permute-start(bf16[2048,768]{1,0:T(8,128)(2,1)} %bitcast.22.refs_13_), channel_id=1, source_target_pairs={{0,1},{1,0},{2,3},{3,2},{4,5},{5,4},{6,7},{7,6},{8,9},{9,8},{10,11... | collective-permute-start | bytes 9437192 | tf_op jit(solution)/shard_map/ppermute | solution.py:221
  93.1 85.3 %collective-permute-start.12 = (bf16[2048,768]{1,0:T(8,128)(2,1)}, bf16[2048,768]{1,0:T(8,128)(2,1)}, u32[]{:S(2)}, u32[]{:S(2)}) collective-permute-start(bf16[2048,768]{1,0:T(8,128)(2,1)} %bitcast.23.refs_14_), channel_id=1, source_target_pairs={{0,1},{1,0},{2,3},{3,2},{4,5},{5,4},{6,7},{7,6},{8,9},{9,8},{10,11... | collective-permute-start | bytes 9437192 | tf_op jit(solution)/shard_map/ppermute | solution.py:221
  93.6 86.8 %collective-permute-start.13 = (bf16[768,2048]{1,0:T(8,128)(2,1)}, bf16[768,2048]{1,0:T(8,128)(2,1)}, u32[]{:S(2)}, u32[]{:S(2)}) collective-permute-start(bf16[768,2048]{1,0:T(8,128)(2,1)} %bitcast.24.refs_15_), channel_id=1, source_target_pairs={{0,1},{1,0},{2,3},{3,2},{4,5},{5,4},{6,7},{7,6},{8,9},{9,8},{10,11... | collective-permute-start | bytes 9437192 | tf_op jit(solution)/shard_map/ppermute | solution.py:221
  162.4 56.9 %collective-permute-start.28 = (bf16[128,2048]{1,0:T(8,128)(2,1)}, bf16[128,2048]{1,0:T(8,128)(2,1)}, u32[]{:S(2)}, u32[]{:S(2)}) collective-permute-start(bf16[128,2048]{1,0:T(8,128)(2,1)} %collective-permute-done.27.refs_4_), channel_id=1, source_target_pairs={{0,2},{1,5},{2,0},{3,7},{4,6},{5,1},{6,4},{7,3},{8,10},{9,13},{10,... | collective-permute-start | bytes 1572872 | tf_op jit(solution)/shard_map/ppermute | solution.py:221
  176.3 43.1 %collective-permute-start.32 = (bf16[256,2048]{1,0:T(8,128)(2,1)S(1)}, bf16[256,2048]{1,0:T(8,128)(2,1)S(1)}, u32[]{:S(2)}, u32[]{:S(2)}) collective-permute-start(bf16[256,2048]{1,0:T(8,128)(2,1)S(1)} %pad_maximum_fusion.4), channel_id=1, source_target_pairs={{0,4},{1,3},{2,6},{3,1},{4,0},{5,7},{6,2},{7,5},{8,12},{9,11},{10,... | collective-permute-start | bytes 3145736 | tf_op jit(solution)/shard_map/ppermute | solution.py:221
  178.3 41.1 %collective-permute-start.35 = (bf16[256,2048]{1,0:T(8,128)(2,1)S(1)}, bf16[256,2048]{1,0:T(8,128)(2,1)}, u32[]{:S(2)}, u32[]{:S(2)}) collective-permute-start(bf16[256,2048]{1,0:T(8,128)(2,1)S(1)} %pad_maximum_fusion.5), channel_id=1, source_target_pairs={{0,4},{1,3},{2,6},{3,1},{4,0},{5,7},{6,2},{7,5},{8,12},{9,11},{10,... | collective-permute-start | bytes 3145736 | tf_op jit(solution)/shard_map/ppermute | solution.py:221
  178.3 41.1 %collective-permute-start.29 = (bf16[256,2048]{1,0:T(8,128)(2,1)}, bf16[256,2048]{1,0:T(8,128)(2,1)}, u32[]{:S(2)}, u32[]{:S(2)}) collective-permute-start(bf16[256,2048]{1,0:T(8,128)(2,1)} %collective-permute-done.26.refs_3_), channel_id=1, source_target_pairs={{0,8},{8,0},{16,24},{24,16},{1,9},{9,1},{17,25},{25,17},{2,10},{10... | collective-permute-start | bytes 3145736 | tf_op jit(solution)/shard_map/ppermute | solution.py:233
  216.2 66.3 %collective-permute-start.22 = (bf16[256,2048]{1,0:T(8,128)(2,1)}, bf16[256,2048]{1,0:T(8,128)(2,1)S(1)}, u32[]{:S(2)}, u32[]{:S(2)}) collective-permute-start(bf16[256,2048]{1,0:T(8,128)(2,1)} %get-tuple-element.27), channel_id=1, source_target_pairs={{0,4},{1,3},{2,6},{3,1},{4,0},{5,7},{6,2},{7,5},{8,12},{9,11},{10,... | collective-permute-start | bytes 3145736 | tf_op jit(solution)/shard_map/ppermute | solution.py:221
  219.3 49.9 %collective-permute-start.17 = (bf16[128,2048]{1,0:T(8,128)(2,1)S(1)}, bf16[128,2048]{1,0:T(8,128)(2,1)S(1)}, u32[]{:S(2)}, u32[]{:S(2)}) collective-permute-start(bf16[128,2048]{1,0:T(8,128)(2,1)S(1)} %slice.89), channel_id=1, source_target_pairs={{0,2},{1,5},{2,0},{3,7},{4,6},{5,1},{6,4},{7,3},{8,10},{9,13},{10,... | collective-permute-start | bytes 1572872 | tf_op jit(solution)/shard_map/ppermute | solution.py:221
  269.2 44.6 %collective-permute-start.14 = (bf16[256,2048]{1,0:T(8,128)(2,1)S(1)}, bf16[256,2048]{1,0:T(8,128)(2,1)S(1)}, u32[]{:S(2)}, u32[]{:S(2)}) collective-permute-start(bf16[256,2048]{1,0:T(8,128)(2,1)S(1)} %copy-done.30), channel_id=1, source_target_pairs={{0,8},{8,0},{16,24},{24,16},{1,9},{9,1},{17,25},{25,17},{2,10},{10... | collective-permute-start | bytes 3145736 | tf_op jit(solution)/shard_map/ppermute | solution.py:233
  284.8 77.1 %collective-permute-start.40 = (bf16[128,2048]{1,0:T(8,128)(2,1)S(1)}, bf16[128,2048]{1,0:T(8,128)(2,1)S(1)}, u32[]{:S(2)}, u32[]{:S(2)}) collective-permute-start(bf16[128,2048]{1,0:T(8,128)(2,1)S(1)} %add_convert_fusion.6), channel_id=1, source_target_pairs={{0,8},{8,0},{16,24},{24,16},{1,9},{9,1},{17,25},{25,17},{2,10},{10... | collective-permute-start | bytes 1572872 | tf_op jit(solution)/shard_map/ppermute | solution.py:233
  349.4 68.3 %collective-permute-start.43 = (bf16[128,2048]{1,0:T(8,128)(2,1)S(1)}, bf16[128,2048]{1,0:T(8,128)(2,1)S(1)}, u32[]{:S(2)}, u32[]{:S(2)}) collective-permute-start(bf16[128,2048]{1,0:T(8,128)(2,1)S(1)} %add_convert_fusion.4), channel_id=1, source_target_pairs={{0,16},{8,24},{16,0},{24,8},{1,17},{9,25},{17,1},{25,9},{2,18},{10... | collective-permute-start | bytes 1572872 | tf_op jit(solution)/shard_map/ppermute | solution.py:233
  349.6 68.1 %collective-permute-start.38 = (bf16[128,2048]{1,0:T(8,128)(2,1)S(1)}, bf16[128,2048]{1,0:T(8,128)(2,1)S(1)}, u32[]{:S(2)}, u32[]{:S(2)}) collective-permute-start(bf16[128,2048]{1,0:T(8,128)(2,1)S(1)} %add_convert_fusion.7), channel_id=1, source_target_pairs={{0,2},{1,5},{2,0},{3,7},{4,6},{5,1},{6,4},{7,3},{8,10},{9,13},{10,... | collective-permute-start | bytes 1572872 | tf_op jit(solution)/shard_map/ppermute | solution.py:221
  361.8 57.7 %collective-permute-start.18 = (bf16[128,2048]{1,0:T(8,128)(2,1)S(1)}, bf16[128,2048]{1,0:T(8,128)(2,1)S(1)}, u32[]{:S(2)}, u32[]{:S(2)}) collective-permute-start(bf16[128,2048]{1,0:T(8,128)(2,1)S(1)} %add_convert_fusion.13), channel_id=1, source_target_pairs={{0,8},{8,0},{16,24},{24,16},{1,9},{9,1},{17,25},{25,17},{2,10},{10... | collective-permute-start | bytes 1572872 | tf_op jit(solution)/shard_map/ppermute | solution.py:233
  362.0 57.5 %collective-permute-start.24 = (bf16[128,2048]{1,0:T(8,128)(2,1)S(1)}, bf16[128,2048]{1,0:T(8,128)(2,1)S(1)}, u32[]{:S(2)}, u32[]{:S(2)}) collective-permute-start(bf16[128,2048]{1,0:T(8,128)(2,1)S(1)} %add_convert_fusion.9), channel_id=1, source_target_pairs={{0,24},{8,16},{16,8},{24,0},{1,25},{9,17},{17,9},{25,1},{2,26},{10... | collective-permute-start | bytes 1572872 | tf_op jit(solution)/shard_map/ppermute | solution.py:233
  364.5 73.5 %collective-permute-start.21 = (bf16[128,2048]{1,0:T(8,128)(2,1)S(1)}, bf16[128,2048]{1,0:T(8,128)(2,1)S(1)}, u32[]{:S(2)}, u32[]{:S(2)}) collective-permute-start(bf16[128,2048]{1,0:T(8,128)(2,1)S(1)} %add_convert_fusion.11), channel_id=1, source_target_pairs={{0,16},{8,24},{16,0},{24,8},{1,17},{9,25},{17,1},{25,9},{2,18},{10... | collective-permute-start | bytes 1572872 | tf_op jit(solution)/shard_map/ppermute | solution.py:233
  (61 other events, 2000.0 us)

commit v2 on v1

--- a/solution.py
+++ b/solution.py
@@ -233,20 +233,49 @@
     return lax.ppermute(value, "seq", [(i, i ^ k) for i in range(4)])
 
 
-def spread(own):
-    zs = [own] + [along_z(own, k) for k in (1, 2, 3)]
-    arrays, names = [], []
-    last0 = None
+def after(value, *others):
+    return lax.optimization_barrier((value, *others))[0]
+
+
+def both(near, far):
+    return jnp.concatenate([near, far], axis=0)
+
+
+def named(name, move, value, *args):
+    with jax.named_scope(name):
+        return move(value, *args)
+
+
+def spread(x, g, weights, table):
+    xs, gs = {}, {}
+    xz, gz = {0: x}, {0: g}
+    xs[0, 1] = named("x0a", first, x)
+    xz[1] = named("x1z", along_z, x, 1)
+    xz[2] = named("x2z", along_z, x, 2)
+    gs[0, 1] = named("g0a", first, g)
+    xs[0, 2] = named("x0b", second, both(x, xs[0, 1]))
+    xz[3] = named("x3z", along_z, after(x, xz[1]), 3)
+    xs[1, 1] = named("x1a", first, after(xz[1], gs[0, 1]))
+    gs[0, 2] = named("g0b", second, both(g, after(gs[0, 1], xs[0, 2])))
+    xs[1, 2] = named("x1b", along_z, after(xs[0, 2], xz[2]), 1)
+    xs[2, 1] = named("x2a", first, after(xz[2], xs[1, 1], *weights, table))
+    xs[2, 2] = named("x2b", second, both(xz[2], after(xs[2, 1], gs[0, 2])))
+    gz[1] = named("g1z", along_z, after(g, xz[3]), 1)
+    gz[2] = named("g2z", along_z, after(g, xz[3]), 2)
+    xs[3, 1] = named("x3a", first, after(xz[3], xs[2, 1]))
+    xs[3, 2] = named("x3b", second, both(xz[3], after(xs[3, 1], xs[2, 2])))
+    gz[3] = named("g3z", along_z, after(g, gz[1], xs[1, 2]), 3)
+    gs[1, 1] = named("g1a", first, after(gz[1], xs[3, 1]))
+    gs[2, 1] = named("g2a", first, after(gz[2], gs[1, 1]))
+    gs[1, 2] = named("g1b", along_z, after(gs[0, 2], gz[2]), 1)
+    gs[2, 2] = named("g2b", second, both(gz[2], after(gs[2, 1], xs[3, 2])))
+    gs[3, 1] = named("g3a", first, after(gz[3], gs[2, 1]))
+    gs[3, 2] = named("g3b", second, both(gz[3], gs[3, 1]))
     for k in range(4):
-        a = first(zs[k])
-        if k == 1:
-            b = along_z(last0, 1)
-        else:
-            b = second(jnp.concatenate([zs[k], a], axis=0))
-            last0 = b if k == 0 else last0
-        arrays += [zs[k], a, b]
-        names += [[(k, 0)], [(k, 1)], [(k, 2), (k, 3)]]
-    return arrays, names
+        xs[k, 0], gs[k, 0] = xz[k], gz[k]
+    keys = [(k, s) for k in range(4) for s in range(3)]
+    names = [[(k, s)] if s < 2 else [(k, 2), (k, 3)] for k, s in keys]
+    return [xs[i] for i in keys], [gs[i] for i in keys], names
 
 
 def add(*values):
@@ -256,23 +285,26 @@
     return total
 
 
-def merge(near, far):
+def merge(near, far, tag, later=None):
     tok = near[0].shape[0] // 2
-    from_z = along_z(far[1], 1)
-    sums = {}
-    for k in (3, 2, 1, 0):
-        part = near[k]
-        if k != 1:
-            send = far[k] if k else add(far[0], from_z).astype(BF16)
-            got = second(send)
-            other = add(part[tok:], got[tok:]).astype(BF16)
-            mine = add(part[:tok], got[:tok])
-        else:
-            other = part[tok:]
-            mine = part[:tok].astype(F32)
-        mine = mine + first(other).astype(F32)
-        sums[k] = along_z(mine.astype(BF16), k).astype(F32) if k else mine
-    return sums[0] + sums[1] + sums[2] + sums[3]
+    got3 = named(tag + "3b", second, far[3])
+    got2 = named(tag + "2b", second, far[2])
+    from_z = named(tag + "1b", along_z, far[1], 1)
+    got1 = named(tag + "1a", first, near[1][tok:])
+    hold = (lambda v, *o: after(v, later, *o)) if later is not None else after
+    send3 = add(hold(near[3][tok:]), got3[tok:]).astype(BF16)
+    got3a = named(tag + "3a", first, send3)
+    send2 = add(hold(near[2][tok:]), got2[tok:]).astype(BF16)
+    got2a = named(tag + "2a", first, send2)
+    sum3 = add(near[3][:tok], got3[:tok], got3a).astype(BF16)
+    z3 = named(tag + "3z", along_z, sum3, 3)
+    got0 = named(tag + "0b", second, add(far[0], hold(from_z)).astype(BF16))
+    sum2 = add(near[2][:tok], got2[:tok], got2a).astype(BF16)
+    z2 = named(tag + "2z", along_z, sum2, 2)
+    sum1 = add(near[1][:tok], hold(got1)).astype(BF16)
+    z1 = named(tag + "1z", along_z, sum1, 1)
+    got0a = named(tag + "0a", first, add(near[0][tok:], got0[tok:]).astype(BF16))
+    return add(near[0][:tok], got0[:tok], got0a, z1, z2, z3)
 
 
 def gathered(tokens, expert_ids, route_weights, norm_gain, gate_proj, up_proj, down_proj, out_grad):
@@ -280,7 +312,7 @@
     tok, fanout = expert_ids.shape
     cap = max(2, 3 * tok * fanout // (2 * experts))
     mine = (gate_proj[0], up_proj[0], down_proj[0])
-    theirs = tuple(ep_permute(w, lambda i: i ^ 1) for w in mine)
+    theirs = tuple(named("swap", ep_permute, w, lambda i: i ^ 1) for w in mine)
     core = lax.axis_index("ep") % 2
 
     ids = jnp.arange(experts, dtype=jnp.int32)
@@ -294,8 +326,7 @@
 
     x_float = tokens.astype(F32)
     normed = scale_rows(x_float, norm_gain).astype(BF16)
-    x_arrays, x_names = spread(normed)
-    g_arrays, _ = spread(out_grad)
+    x_arrays, g_arrays, x_names = spread(normed, out_grad, theirs, table)
 
     z, ep = lax.axis_index("seq"), lax.axis_index("ep")
     step_first = jnp.where(core == 1, 4, 2)
@@ -310,11 +341,11 @@
     results = run_experts(
         forward_kernel, index, table, x_arrays, in_map, mine + theirs, None, out_rows, out_map, cap
     )
-    moe_out = merge(results[0:4], results[4:8]).astype(BF16)
     grads = run_experts(
         backward_kernel, index, table, g_arrays, in_map, mine + theirs, results[8:10], out_rows, out_map, cap
     )
-    grad_normed = merge(grads[0:4], grads[4:8])
+    moe_out = merge(results[0:4], results[4:8], "o", grads[0]).astype(BF16)
+    grad_normed = merge(grads[0:4], grads[4:8], "d")
     return (moe_out, norm_grad(x_float, norm_gain, grad_normed))
 
 

time: 440 us -> 406 us (0.923); the launches traced: 439 us -> 399 us
  waiting for transfers between devices: 239 us -> 204 us
  starting transfers between devices: 103 us -> 95.2 us
    ppermute x31, waiting for transfers between devices: 122 us -> 72.5 us  [ep_permute(): return lax.ppermute(value, 'ep', [(i, partner(i)) for i in range(8)])]
    ppermute x16, starting transfers between devices: 70.2 us -> 49.4 us  [along_z(): return lax.ppermute(value, 'seq', [(i, i ^ k) for i in range(4)])]
    ppermute x16, waiting for transfers between devices: 117 us -> 127 us  [along_z(): return lax.ppermute(value, 'seq', [(i, i ^ k) for i in range(4)])]
    ppermute x31, starting transfers between devices: 29.3 us -> 39.5 us  [ep_permute(): return lax.ppermute(value, 'ep', [(i, partner(i)) for i in range(8)])]
  transfers between devices with their start and end apart: 48 -> 48, of which waited for: 20 -> 21; matrix products, arithmetic and copies ran while one was open for 2% -> 4% of each run, Pallas kernels for 18% -> 20%
where the time goes in v2:
time: 406 us; the launch traced here: 399 us
  waiting for transfers between devices  204 us (50%)
  starting transfers between devices  95.2 us (23%)
  Pallas kernels  80.7 us (20%)
  other arithmetic  11.2 us (3%)
  local copies, waits for them, and re-layouts  6.81 us (2%)
    ppermute x16, waiting for transfers between devices, along_z(): return lax.ppermute(value, 'seq', [(i, i ^ k) for i in range(4)])  127 us
    pallas_call x2, Pallas kernels, run_experts(): pl.pallas_call(functools.partial(kernel, cap, in_map, out_map, len(ins),...  80.7 us
    ppermute x31, waiting for transfers between devices, ep_permute(): return lax.ppermute(value, 'ep', [(i, partner(i)) for i in range(8)])  72.5 us
    ppermute x16, starting transfers between devices, along_z(): return lax.ppermute(value, 'seq', [(i, i ^ k) for i in range(4)])  49.4 us
    ppermute x31, starting transfers between devices, ep_permute(): return lax.ppermute(value, 'ep', [(i, partner(i)) for i in range(8)])  39.5 us
  transfers between devices with their start and end apart: 48, of which 21 were waited for; matrix products, arithmetic and copies ran while one was open for 4% of the time, Pallas kernels for 20%

profile of v2, /device:TPU:0, one launch (start us, length us, event | category | flops | bytes accessed | tf_op | source)
XLA Modules:
  0.0 399.1 jit_solution(16740757516652984866)
XLA Ops:
  8.4 5.6 %collective-permute-done.refs_2_ = bf16[128,2048]{1,0:T(8,128)(2,1)S(1)} collective-permute-done((bf16[128,2048]{1,0:T(8,128)(2,1)S(1)}, bf16[128,2048]{1,0:T(8,128)(2,1)S(1)}, u32[]{:S(2)}, u32[]{:S(2)}) %collective-permute-start) | collective-permute-done | bytes 524320 | tf_op jit(solution)/shard_map/x0a/ppermute | solution.py:221
  16.2 4.7 %collective-permute-done.2.refs_4_ = bf16[128,2048]{1,0:T(8,128)(2,1)} collective-permute-done((bf16[128,2048]{1,0:T(8,128)(2,1)S(1)}, bf16[128,2048]{1,0:T(8,128)(2,1)}, u32[]{:S(2)}, u32[]{:S(2)}) %collective-permute-start.2) | collective-permute-done | bytes 524320 | tf_op jit(solution)/shard_map/x1z/ppermute | solution.py:233
  21.3 12.3 %collective-permute-done.3.refs_2_ = bf16[128,2048]{1,0:T(8,128)(2,1)S(1)} collective-permute-done((bf16[128,2048]{1,0:T(8,128)(2,1)S(1)}, bf16[128,2048]{1,0:T(8,128)(2,1)S(1)}, u32[]{:S(2)}, u32[]{:S(2)}) %collective-permute-start.3) | collective-permute-done | bytes 524320 | tf_op jit(solution)/shard_map/g0a/ppermute | solution.py:221
  38.0 22.4 %collective-permute-done.5.refs_7_ = bf16[128,2048]{1,0:T(8,128)(2,1)S(1)} collective-permute-done((bf16[128,2048]{1,0:T(8,128)(2,1)S(1)}, bf16[128,2048]{1,0:T(8,128)(2,1)S(1)}, u32[]{:S(2)}, u32[]{:S(2)}) %collective-permute-start.5) | collective-permute-done | bytes 524320 | tf_op jit(solution)/shard_map/x2z/ppermute | solution.py:233
  61.4 6.3 %all-to-all-start = ((f32[32,1,256]{2,1,0:T(1,128)}), f32[32,1,256]{2,1,0:T(1,128)S(1)}, u32[]{:S(2)}, u32[]{:S(2)}) async-start(f32[32,1,256]{2,1,0:T(1,128)} %bitcast.20), calls=%async_computation | async-start | bytes 65536 | tf_op jit(solution)/shard_map/all_to_all | solution.py:324
  67.7 3.7 collective-permute-start.13
  71.4 4.2 %all-to-all-done = f32[32,1,256]{2,1,0:T(1,128)S(1)} async-done(((f32[32,1,256]{2,1,0:T(1,128)}), f32[32,1,256]{2,1,0:T(1,128)S(1)}, u32[]{:S(2)}, u32[]{:S(2)}) %all-to-all-start) | async-done | bytes 32800 | tf_op jit(solution)/shard_map/all_to_all | solution.py:324
  77.4 6.9 %collective-permute-done.13.refs_10_ = bf16[128,2048]{1,0:T(8,128)(2,1)} collective-permute-done((bf16[128,2048]{1,0:T(8,128)(2,1)S(1)}, bf16[128,2048]{1,0:T(8,128)(2,1)}, u32[]{:S(2)}, u32[]{:S(2)}) %collective-permute-start.13) | collective-permute-done | bytes 524320 | tf_op jit(solution)/shard_map/x3z/ppermute | solution.py:233
  84.3 11.1 %collective-permute-start.17 = (bf16[128,2048]{1,0:T(8,128)(2,1)S(1)}, bf16[128,2048]{1,0:T(8,128)(2,1)S(1)}, u32[]{:S(2)}, u32[]{:S(2)}) collective-permute-start(bf16[128,2048]{1,0:T(8,128)(2,1)S(1)} %copy-done.12), channel_id=1, source_target_pairs={{0,8},{8,0},{16,24},{24,16},{1,9},{9,1},{17,25},{25,17},{2,10},{10... | collective-permute-start | bytes 1572872 | tf_op jit(solution)/shard_map/g1z/ppermute | solution.py:233
  101.0 18.4 %collective-permute-done.17.refs_4_ = bf16[128,2048]{1,0:T(8,128)(2,1)S(1)} collective-permute-done((bf16[128,2048]{1,0:T(8,128)(2,1)S(1)}, bf16[128,2048]{1,0:T(8,128)(2,1)S(1)}, u32[]{:S(2)}, u32[]{:S(2)}) %collective-permute-start.17) | collective-permute-done | bytes 524320 | tf_op jit(solution)/shard_map/g1z/ppermute | solution.py:233
  120.9 19.8 %collective-permute-done.6.refs_6_ = bf16[256,2048]{1,0:T(8,128)(2,1)S(1)} collective-permute-done((bf16[256,2048]{1,0:T(8,128)(2,1)}, bf16[256,2048]{1,0:T(8,128)(2,1)S(1)}, u32[]{:S(2)}, u32[]{:S(2)}) %collective-permute-start.6) | collective-permute-done | bytes 1048608 | tf_op jit(solution)/shard_map/x1b/ppermute | solution.py:233
  146.6 8.9 %collective-permute-done.23.refs_10_ = bf16[128,2048]{1,0:T(8,128)(2,1)} collective-permute-done((bf16[128,2048]{1,0:T(8,128)(2,1)S(1)}, bf16[128,2048]{1,0:T(8,128)(2,1)}, u32[]{:S(2)}, u32[]{:S(2)}) %collective-permute-start.23) | collective-permute-done | bytes 524320 | tf_op jit(solution)/shard_map/g3z/ppermute | solution.py:233
  160.1 8.0 %collective-permute-start.20 = (bf16[256,2048]{1,0:T(8,128)(2,1)}, bf16[256,2048]{1,0:T(8,128)(2,1)}, u32[]{:S(2)}, u32[]{:S(2)}) collective-permute-start(bf16[256,2048]{1,0:T(8,128)(2,1)} %collective-permute-done.11.refs_3_), channel_id=1, source_target_pairs={{0,8},{8,0},{16,24},{24,16},{1,9},{9,1},{17,25},{25,17},{2,10},{10... | collective-permute-start | bytes 3145736 | tf_op jit(solution)/shard_map/g1b/ppermute | solution.py:233
  171.9 35.3 %shard_map.95 = (bf16[256,2048]{1,0:T(8,128)(2,1)}, bf16[256,2048]{1,0:T(8,128)(2,1)}, bf16[256,2048]{1,0:T(8,128)(2,1)}, bf16[256,2048]{1,0:T(8,128)(2,1)}, bf1...) custom-call(s32[16]{0:T(128)} %stack.73.index_ref, ...), custom_call_target="tpu_custom_call" | custom-call | flops 14495514624 | bytes 45088768 | tf_op jit(solution)/shard_map/pallas_call | solution.py:193
  211.1 7.1 %collective-permute-start.16 = (bf16[256,2048]{1,0:T(8,128)(2,1)}, bf16[256,2048]{1,0:T(8,128)(2,1)S(1)}, u32[]{:S(2)}, u32[]{:S(2)}) collective-permute-start(bf16[256,2048]{1,0:T(8,128)(2,1)} %get-tuple-element.49), channel_id=1, source_target_pairs={{0,8},{8,0},{16,24},{24,16},{1,9},{9,1},{17,25},{25,17},{2,10},{10... | collective-permute-start | bytes 3145736 | tf_op jit(solution)/shard_map/o1b/ppermute | solution.py:233
  220.2 45.4 %shard_map.96 = (bf16[256,2048]{1,0:T(8,128)(2,1)}, bf16[256,2048]{1,0:T(8,128)(2,1)}, bf16[256,2048]{1,0:T(8,128)(2,1)}, bf16[256,2048]{1,0:T(8,128)(2,1)}, bf1...) custom-call(s32[16]{0:T(128)} %stack.73.index_ref, ...), custom_call_target="tpu_custom_call" | custom-call | flops 14495514624 | bytes 45088768 | tf_op jit(solution)/shard_map/pallas_call | solution.py:193
  273.2 19.1 %collective-permute-done.31 = bf16[128,2048]{1,0:T(8,128)(2,1)S(1)} collective-permute-done((bf16[128,2048]{1,0:T(8,128)(2,1)S(1)}, bf16[128,2048]{1,0:T(8,128)(2,1)S(1)}, u32[]{:S(2)}, u32[]{:S(2)}) %collective-permute-start.31) | collective-permute-done | bytes 524320 | tf_op jit(solution)/shard_map/o2a/ppermute | solution.py:221
  294.2 6.1 %collective-permute-done.34 = bf16[128,2048]{1,0:T(8,128)(2,1)S(1)} collective-permute-done((bf16[128,2048]{1,0:T(8,128)(2,1)S(1)}, bf16[128,2048]{1,0:T(8,128)(2,1)S(1)}, u32[]{:S(2)}, u32[]{:S(2)}) %collective-permute-start.34) | collective-permute-done | bytes 524320 | tf_op jit(solution)/shard_map/o3a/ppermute | solution.py:221
  304.1 8.6 %collective-permute-done.36 = bf16[256,2048]{1,0:T(8,128)(2,1)S(1)} collective-permute-done((bf16[256,2048]{1,0:T(8,128)(2,1)S(1)}, bf16[256,2048]{1,0:T(8,128)(2,1)S(1)}, u32[]{:S(2)}, u32[]{:S(2)}) %collective-permute-start.36) | collective-permute-done | bytes 1048608 | tf_op jit(solution)/shard_map/d1b/ppermute | solution.py:233
  318.6 13.7 %collective-permute-done.44 = bf16[256,2048]{1,0:T(8,128)(2,1)S(1)} collective-permute-done((bf16[256,2048]{1,0:T(8,128)(2,1)S(1)}, bf16[256,2048]{1,0:T(8,128)(2,1)S(1)}, u32[]{:S(2)}, u32[]{:S(2)}) %collective-permute-start.44) | collective-permute-done | bytes 1048608 | tf_op jit(solution)/shard_map/d3b/ppermute | solution.py:221
  334.6 6.8 %collective-permute-done.42 = bf16[128,2048]{1,0:T(8,128)(2,1)S(1)} collective-permute-done((bf16[128,2048]{1,0:T(8,128)(2,1)S(1)}, bf16[128,2048]{1,0:T(8,128)(2,1)S(1)}, u32[]{:S(2)}, u32[]{:S(2)}) %collective-permute-start.42) | collective-permute-done | bytes 524320 | tf_op jit(solution)/shard_map/d2a/ppermute | solution.py:221
  343.4 3.6 collective-permute-done.45
  359.7 6.8 %collective-permute-done.40 = bf16[128,2048]{1,0:T(8,128)(2,1)S(1)} collective-permute-done((bf16[128,2048]{1,0:T(8,128)(2,1)S(1)}, bf16[128,2048]{1,0:T(8,128)(2,1)S(1)}, u32[]{:S(2)}, u32[]{:S(2)}) %collective-permute-start.40) | collective-permute-done | bytes 524320 | tf_op jit(solution)/shard_map/d1z/ppermute | solution.py:233
  366.5 30.7 %collective-permute-done.43 = bf16[128,2048]{1,0:T(8,128)(2,1)S(1)} collective-permute-done((bf16[128,2048]{1,0:T(8,128)(2,1)S(1)}, bf16[128,2048]{1,0:T(8,128)(2,1)S(1)}, u32[]{:S(2)}, u32[]{:S(2)}) %collective-permute-start.43) | collective-permute-done | bytes 524320 | tf_op jit(solution)/shard_map/d2z/ppermute | solution.py:233
  (176 shorter events, 82.5 us)
Async XLA Ops:
  0.6 75.0 %collective-permute-start.7 = (bf16[2048,768]{1,0:T(8,128)(2,1)}, bf16[2048,768]{1,0:T(8,128)(2,1)}, u32[]{:S(2)}, u32[]{:S(2)}) collective-permute-start(bf16[2048,768]{1,0:T(8,128)(2,1)} %bitcast.32), channel_id=1, source_target_pairs={{0,1},{1,0},{2,3},{3,2},{4,5},{5,4},{6,7},{7,6},{8,9},{9,8},{10,11... | collective-permute-start | bytes 9437192 | tf_op jit(solution)/shard_map/swap/ppermute | solution.py:221
  1.2 74.5 %collective-permute-start.8 = (bf16[2048,768]{1,0:T(8,128)(2,1)}, bf16[2048,768]{1,0:T(8,128)(2,1)}, u32[]{:S(2)}, u32[]{:S(2)}) collective-permute-start(bf16[2048,768]{1,0:T(8,128)(2,1)} %bitcast.35), channel_id=1, source_target_pairs={{0,1},{1,0},{2,3},{3,2},{4,5},{5,4},{6,7},{7,6},{8,9},{9,8},{10,11... | collective-permute-start | bytes 9437192 | tf_op jit(solution)/shard_map/swap/ppermute | solution.py:221
  1.2 74.4 %collective-permute-start.9 = (bf16[768,2048]{1,0:T(8,128)(2,1)}, bf16[768,2048]{1,0:T(8,128)(2,1)}, u32[]{:S(2)}, u32[]{:S(2)}) collective-permute-start(bf16[768,2048]{1,0:T(8,128)(2,1)} %bitcast.38), channel_id=1, source_target_pairs={{0,1},{1,0},{2,3},{3,2},{4,5},{5,4},{6,7},{7,6},{8,9},{9,8},{10,11... | collective-permute-start | bytes 9437192 | tf_op jit(solution)/shard_map/swap/ppermute | solution.py:221
  36.4 31.3 %collective-permute-start.4 = (bf16[128,2048]{1,0:T(8,128)(2,1)}, bf16[128,2048]{1,0:T(8,128)(2,1)}, u32[]{:S(2)}, u32[]{:S(2)}) collective-permute-start(bf16[128,2048]{1,0:T(8,128)(2,1)} %collective-permute-done.2.refs_4_), channel_id=1, source_target_pairs={{0,2},{1,5},{2,0},{3,7},{4,6},{5,1},{6,4},{7,3},{8,10},{9,13},{10,... | collective-permute-start | bytes 1572872 | tf_op jit(solution)/shard_map/x1a/ppermute | solution.py:221
  60.4 35.1 %collective-permute-start.11 = (bf16[256,2048]{1,0:T(8,128)(2,1)S(1)}, bf16[256,2048]{1,0:T(8,128)(2,1)}, u32[]{:S(2)}, u32[]{:S(2)}) collective-permute-start(bf16[256,2048]{1,0:T(8,128)(2,1)S(1)} %pad_maximum_fusion.1), channel_id=1, source_target_pairs={{0,4},{1,3},{2,6},{3,1},{4,0},{5,7},{6,2},{7,5},{8,12},{9,11},{10,... | collective-permute-start | bytes 3145736 | tf_op jit(solution)/shard_map/g0b/ppermute | solution.py:221
  84.3 35.1 %collective-permute-start.17 = (bf16[128,2048]{1,0:T(8,128)(2,1)S(1)}, bf16[128,2048]{1,0:T(8,128)(2,1)S(1)}, u32[]{:S(2)}, u32[]{:S(2)}) collective-permute-start(bf16[128,2048]{1,0:T(8,128)(2,1)S(1)} %copy-done.12), channel_id=1, source_target_pairs={{0,8},{8,0},{16,24},{24,16},{1,9},{9,1},{17,25},{25,17},{2,10},{10... | collective-permute-start | bytes 1572872 | tf_op jit(solution)/shard_map/g1z/ppermute | solution.py:233
  95.4 45.3 %collective-permute-start.6 = (bf16[256,2048]{1,0:T(8,128)(2,1)}, bf16[256,2048]{1,0:T(8,128)(2,1)S(1)}, u32[]{:S(2)}, u32[]{:S(2)}) collective-permute-start(bf16[256,2048]{1,0:T(8,128)(2,1)} %collective-permute-done.1.refs_3_), channel_id=1, source_target_pairs={{0,8},{8,0},{16,24},{24,16},{1,9},{9,1},{17,25},{25,17},{2,10},{10... | collective-permute-start | bytes 3145736 | tf_op jit(solution)/shard_map/x1b/ppermute | solution.py:233
  97.1 46.8 %collective-permute-start.12 = (bf16[256,2048]{1,0:T(8,128)(2,1)S(1)}, bf16[256,2048]{1,0:T(8,128)(2,1)}, u32[]{:S(2)}, u32[]{:S(2)}) collective-permute-start(bf16[256,2048]{1,0:T(8,128)(2,1)S(1)} %pad_maximum_fusion.2), channel_id=1, source_target_pairs={{0,4},{1,3},{2,6},{3,1},{4,0},{5,7},{6,2},{7,5},{8,12},{9,11},{10,... | collective-permute-start | bytes 3145736 | tf_op jit(solution)/shard_map/x2b/ppermute | solution.py:221
  98.6 43.7 %collective-permute-start.19 = (bf16[128,2048]{1,0:T(8,128)(2,1)S(1)}, bf16[128,2048]{1,0:T(8,128)(2,1)S(1)}, u32[]{:S(2)}, u32[]{:S(2)}) collective-permute-start(bf16[128,2048]{1,0:T(8,128)(2,1)S(1)} %copy-done.12), channel_id=1, source_target_pairs={{0,16},{8,24},{16,0},{24,8},{1,17},{9,25},{17,1},{25,9},{2,18},{10... | collective-permute-start | bytes 1572872 | tf_op jit(solution)/shard_map/g2z/ppermute | solution.py:233
  160.1 58.1 %collective-permute-start.20 = (bf16[256,2048]{1,0:T(8,128)(2,1)}, bf16[256,2048]{1,0:T(8,128)(2,1)}, u32[]{:S(2)}, u32[]{:S(2)}) collective-permute-start(bf16[256,2048]{1,0:T(8,128)(2,1)} %collective-permute-done.11.refs_3_), channel_id=1, source_target_pairs={{0,8},{8,0},{16,24},{24,16},{1,9},{9,1},{17,25},{25,17},{2,10},{10... | collective-permute-start | bytes 3145736 | tf_op jit(solution)/shard_map/g1b/ppermute | solution.py:233
  169.6 50.0 %collective-permute-start.25 = (bf16[256,2048]{1,0:T(8,128)(2,1)S(1)}, bf16[256,2048]{1,0:T(8,128)(2,1)}, u32[]{:S(2)}, u32[]{:S(2)}) collective-permute-start(bf16[256,2048]{1,0:T(8,128)(2,1)S(1)} %pad_maximum_fusion.5), channel_id=1, source_target_pairs={{0,4},{1,3},{2,6},{3,1},{4,0},{5,7},{6,2},{7,5},{8,12},{9,11},{10,... | collective-permute-start | bytes 3145736 | tf_op jit(solution)/shard_map/g3b/ppermute | solution.py:221
  171.1 49.1 %collective-permute-start.22 = (bf16[256,2048]{1,0:T(8,128)(2,1)S(1)}, bf16[256,2048]{1,0:T(8,128)(2,1)}, u32[]{:S(2)}, u32[]{:S(2)}) collective-permute-start(bf16[256,2048]{1,0:T(8,128)(2,1)S(1)} %pad_maximum_fusion.4), channel_id=1, source_target_pairs={{0,4},{1,3},{2,6},{3,1},{4,0},{5,7},{6,2},{7,5},{8,12},{9,11},{10,... | collective-permute-start | bytes 3145736 | tf_op jit(solution)/shard_map/g2b/ppermute | solution.py:221
  209.6 58.4 %collective-permute-start.28 = (bf16[128,2048]{1,0:T(8,128)(2,1)S(1)}, bf16[128,2048]{1,0:T(8,128)(2,1)S(1)}, u32[]{:S(2)}, u32[]{:S(2)}) collective-permute-start(bf16[128,2048]{1,0:T(8,128)(2,1)S(1)} %slice.89), channel_id=1, source_target_pairs={{0,2},{1,5},{2,0},{3,7},{4,6},{5,1},{6,4},{7,3},{8,10},{9,13},{10,... | collective-permute-start | bytes 1572872 | tf_op jit(solution)/shard_map/o1a/ppermute | solution.py:221
  211.1 57.7 %collective-permute-start.16 = (bf16[256,2048]{1,0:T(8,128)(2,1)}, bf16[256,2048]{1,0:T(8,128)(2,1)S(1)}, u32[]{:S(2)}, u32[]{:S(2)}) collective-permute-start(bf16[256,2048]{1,0:T(8,128)(2,1)} %get-tuple-element.49), channel_id=1, source_target_pairs={{0,8},{8,0},{16,24},{24,16},{1,9},{9,1},{17,25},{25,17},{2,10},{10... | collective-permute-start | bytes 3145736 | tf_op jit(solution)/shard_map/o1b/ppermute | solution.py:233
  218.2 50.7 %collective-permute-start.30 = (bf16[256,2048]{1,0:T(8,128)(2,1)}, bf16[256,2048]{1,0:T(8,128)(2,1)S(1)}, u32[]{:S(2)}, u32[]{:S(2)}) collective-permute-start(bf16[256,2048]{1,0:T(8,128)(2,1)} %get-tuple-element.64), channel_id=1, source_target_pairs={{0,4},{1,3},{2,6},{3,1},{4,0},{5,7},{6,2},{7,5},{8,12},{9,11},{10,... | collective-permute-start | bytes 3145736 | tf_op jit(solution)/shard_map/o2b/ppermute | solution.py:221
  219.7 50.9 %collective-permute-start.33 = (bf16[256,2048]{1,0:T(8,128)(2,1)}, bf16[256,2048]{1,0:T(8,128)(2,1)S(1)}, u32[]{:S(2)}, u32[]{:S(2)}) collective-permute-start(bf16[256,2048]{1,0:T(8,128)(2,1)} %get-tuple-element.67), channel_id=1, source_target_pairs={{0,4},{1,3},{2,6},{3,1},{4,0},{5,7},{6,2},{7,5},{8,12},{9,11},{10,... | collective-permute-start | bytes 3145736 | tf_op jit(solution)/shard_map/o3b/ppermute | solution.py:221
  268.1 86.2 %collective-permute-start.29 = (bf16[128,2048]{1,0:T(8,128)(2,1)S(1)}, bf16[128,2048]{1,0:T(8,128)(2,1)S(1)}, u32[]{:S(2)}, u32[]{:S(2)}) collective-permute-start(bf16[128,2048]{1,0:T(8,128)(2,1)S(1)} %add_convert_fusion.13), channel_id=1, source_target_pairs={{0,8},{8,0},{16,24},{24,16},{1,9},{9,1},{17,25},{25,17},{2,10},{10... | collective-permute-start | bytes 1572872 | tf_op jit(solution)/shard_map/o1z/ppermute | solution.py:233
  268.2 35.7 %collective-permute-start.39 = (bf16[128,2048]{1,0:T(8,128)(2,1)S(1)}, bf16[128,2048]{1,0:T(8,128)(2,1)S(1)}, u32[]{:S(2)}, u32[]{:S(2)}) collective-permute-start(bf16[128,2048]{1,0:T(8,128)(2,1)S(1)} %slice.103), channel_id=1, source_target_pairs={{0,2},{1,5},{2,0},{3,7},{4,6},{5,1},{6,4},{7,3},{8,10},{9,13},{10,... | collective-permute-start | bytes 1572872 | tf_op jit(solution)/shard_map/d1a/ppermute | solution.py:221
  271.7 62.3 %collective-permute-start.26 = (bf16[256,2048]{1,0:T(8,128)(2,1)S(1)}, bf16[256,2048]{1,0:T(8,128)(2,1)S(1)}, u32[]{:S(2)}, u32[]{:S(2)}) collective-permute-start(bf16[256,2048]{1,0:T(8,128)(2,1)S(1)} %add_convert_fusion.1), channel_id=1, source_target_pairs={{0,4},{1,3},{2,6},{3,1},{4,0},{5,7},{6,2},{7,5},{8,12},{9,11},{10,... | collective-permute-start | bytes 3145736 | tf_op jit(solution)/shard_map/o0b/ppermute | solution.py:221
  312.7 42.0 %collective-permute-start.32 = (bf16[128,2048]{1,0:T(8,128)(2,1)S(1)}, bf16[128,2048]{1,0:T(8,128)(2,1)S(1)}, u32[]{:S(2)}, u32[]{:S(2)}) collective-permute-start(bf16[128,2048]{1,0:T(8,128)(2,1)S(1)} %add_convert_fusion.11), channel_id=1, source_target_pairs={{0,16},{8,24},{16,0},{24,8},{1,17},{9,25},{17,1},{25,9},{2,18},{10... | collective-permute-start | bytes 1572872 | tf_op jit(solution)/shard_map/o2z/ppermute | solution.py:233
  316.4 35.5 %collective-permute-start.37 = (bf16[256,2048]{1,0:T(8,128)(2,1)S(1)}, bf16[256,2048]{1,0:T(8,128)(2,1)S(1)}, u32[]{:S(2)}, u32[]{:S(2)}) collective-permute-start(bf16[256,2048]{1,0:T(8,128)(2,1)S(1)} %add_convert_fusion), channel_id=1, source_target_pairs={{0,4},{1,3},{2,6},{3,1},{4,0},{5,7},{6,2},{7,5},{8,12},{9,11},{10,... | collective-permute-start | bytes 3145736 | tf_op jit(solution)/shard_map/d0b/ppermute | solution.py:221
  354.3 42.9 %collective-permute-start.43 = (bf16[128,2048]{1,0:T(8,128)(2,1)S(1)}, bf16[128,2048]{1,0:T(8,128)(2,1)S(1)}, u32[]{:S(2)}, u32[]{:S(2)}) collective-permute-start(bf16[128,2048]{1,0:T(8,128)(2,1)S(1)} %add_convert_fusion.4), channel_id=1, source_target_pairs={{0,16},{8,24},{16,0},{24,8},{1,17},{9,25},{17,1},{25,9},{2,18},{10... | collective-permute-start | bytes 1572872 | tf_op jit(solution)/shard_map/d2z/ppermute | solution.py:233
  354.7 42.6 %collective-permute-start.46 = (bf16[128,2048]{1,0:T(8,128)(2,1)S(1)}, bf16[128,2048]{1,0:T(8,128)(2,1)S(1)}, u32[]{:S(2)}, u32[]{:S(2)}) collective-permute-start(bf16[128,2048]{1,0:T(8,128)(2,1)S(1)} %add_convert_fusion.2), channel_id=1, source_target_pairs={{0,24},{8,16},{16,8},{24,0},{1,25},{9,17},{17,9},{25,1},{2,26},{10... | collective-permute-start | bytes 1572872 | tf_op jit(solution)/shard_map/d3z/ppermute | solution.py:233
  356.8 40.5 %collective-permute-start.38 = (bf16[128,2048]{1,0:T(8,128)(2,1)S(1)}, bf16[128,2048]{1,0:T(8,128)(2,1)S(1)}, u32[]{:S(2)}, u32[]{:S(2)}) collective-permute-start(bf16[128,2048]{1,0:T(8,128)(2,1)S(1)} %add_convert_fusion.7), channel_id=1, source_target_pairs={{0,2},{1,5},{2,0},{3,7},{4,6},{5,1},{6,4},{7,3},{8,10},{9,13},{10,... | collective-permute-start | bytes 1572872 | tf_op jit(solution)/shard_map/d0a/ppermute | solution.py:221
  (56 other events, 1353.3 us)

commit v3 on v0

--- a/solution.py
+++ b/solution.py
@@ -1,14 +1,331 @@
+import functools
+
 import jax
 import jax.numpy as jnp
 from jax import lax
+from jax.experimental import pallas as pl
+from jax.experimental.pallas import tpu as pltpu
 from jax.sharding import PartitionSpec as P
 
 EPS = 1e-06
+PAIRS = (((1,), (1,)), ((), ()))
+BF16, F32 = jnp.bfloat16, jnp.float32
 
 
 def scale_rows(values, norm_gain):
     mean_square = jnp.mean(values * values, axis=-1, keepdims=True)
     return values * lax.rsqrt(mean_square + EPS) * norm_gain
+
+
+def norm_grad(x_float, norm_gain, grad):
+    def normalize(values):
+        return scale_rows(values, norm_gain)
+
+    _, pullback = jax.vjp(normalize, x_float)
+    return pullback(grad)[0].astype(BF16)
+
+
+def slot_tables(index_ref, table_ref, onehot, factor, ranks, blocks, cap):
+    tok = table_ref.shape[2]
+    marks = jnp.concatenate(
+        [jnp.where(table_ref[index_ref[b]] > 0.0, 1.0, 0.0).astype(BF16) for b in range(blocks)], axis=0
+    )
+    before = lax.broadcasted_iota(jnp.int32, (tok, tok), 0) < lax.broadcasted_iota(jnp.int32, (tok, tok), 1)
+    ranks[...] = jnp.dot(marks, jnp.where(before, 1.0, 0.0).astype(BF16), preferred_element_type=F32)
+    slots = lax.broadcasted_iota(jnp.int32, (cap, tok), 0).astype(F32)
+    for b in range(blocks):
+        weights = table_ref[index_ref[b]]
+        for e in range(2):
+            weight = weights[e : e + 1, :]
+            rank = jnp.where(weight > 0.0, ranks[2 * b + e : 2 * b + e + 1, :], -1.0)
+            hit = slots == rank
+            onehot[b, e * cap : (e + 1) * cap, :] = jnp.where(hit, 1.0, 0.0).astype(BF16)
+            slot_weight = jnp.sum(jnp.where(hit, weight, 0.0), axis=1, keepdims=True)
+            factor[e, b * cap : (b + 1) * cap, :] = jnp.broadcast_to(slot_weight, (cap, tok))
+
+
+def pick_rows(buffer, onehot, rows, blocks, cap):
+    tok = onehot.shape[2]
+    for b in blocks:
+        picked = jnp.dot(onehot[b], buffer[b * tok : (b + 1) * tok, :], preferred_element_type=F32).astype(BF16)
+        rows[0, b * cap : (b + 1) * cap, :] = picked[:cap]
+        rows[1, b * cap : (b + 1) * cap, :] = picked[cap:]
+
+
+def put_rows(buffer, onehot, rows, blocks, cap):
+    tok = onehot.shape[2]
+    for b in blocks:
+        pair = jnp.concatenate([rows[0, b * cap : (b + 1) * cap, :], rows[1, b * cap : (b + 1) * cap, :]], axis=0)
+        summed = lax.dot_general(onehot[b], pair, (((0,), (0,)), ((), ())), preferred_element_type=F32)
+        buffer[b * tok : (b + 1) * tok, :] = summed.astype(BF16)
+
+
+def tiles(size, most):
+    step = most if size % most == 0 else size
+    return [slice(at, at + step) for at in range(0, size, step)]
+
+
+def forward_expert(e, rows, factor, gate_w, up_w, down_w, arrived, acts, keep, hidden):
+    arrived("gate", e), arrived("up", e)
+    for n in tiles(gate_w.shape[1], 256):
+        gate_act = jnp.dot(rows[e], gate_w[:, n], preferred_element_type=F32)
+        upward = jnp.dot(rows[e], up_w[:, n], preferred_element_type=F32)
+        acts[0, :, n] = gate_act
+        acts[1, :, n] = upward
+        hidden[0, :, n] = (gate_act * jax.nn.sigmoid(gate_act) * upward).astype(BF16)
+    keep(e)
+    arrived("down", e)
+    for n in tiles(down_w.shape[1], 512):
+        total = jnp.dot(hidden[0], down_w[:, n], preferred_element_type=F32)
+        rows[e, :, n] = (total * factor[e][:, :1]).astype(BF16)
+
+
+def backward_expert(e, rows, factor, gate_w, up_w, down_w, arrived, acts, keep, hidden):
+    arrived("down", e), keep(e)
+    for n in tiles(gate_w.shape[1], 256):
+        grad_hidden = lax.dot_general(rows[e], down_w[n, :], PAIRS, preferred_element_type=F32)
+        gate_act = acts[0, :, n]
+        sigmoid = jax.nn.sigmoid(gate_act)
+        slope = sigmoid * (1.0 + gate_act * (1.0 - sigmoid))
+        hidden[0, :, n] = (grad_hidden * acts[1, :, n] * slope).astype(BF16)
+        hidden[1, :, n] = (grad_hidden * (gate_act * sigmoid)).astype(BF16)
+    arrived("gate", e), arrived("up", e)
+    for n in tiles(down_w.shape[1], 512):
+        total = lax.dot_general(hidden[0], gate_w[n, :], PAIRS, preferred_element_type=F32)
+        total = total + lax.dot_general(hidden[1], up_w[n, :], PAIRS, preferred_element_type=F32)
+        rows[e, :, n] = (total * factor[e][:, :1]).astype(BF16)
+
+
+def experts_kernel(forward, cap, groups, index_ref, *refs):
+    count = len(groups)
+    table_ref, ins, weights = refs[0], refs[1 : 1 + count], refs[1 + count : 7 + count]
+    rest = refs[7 + count :]
+    if forward:
+        outs, kept, scratch = rest[:count], rest[count], rest[count + 1 :]
+    else:
+        kept, outs, scratch = rest[0], rest[1 : 1 + count], rest[1 + count :]
+    buffer, rows, onehot, factor, ranks, sides, downs, acts, hidden, in_sem, weight_sem, act_sem = scratch
+    tok = onehot.shape[2]
+    blocks = sum(len(g) for g in groups)
+
+    def window(i):
+        return buffer.at[groups[i][0] * tok : (groups[i][-1] + 1) * tok]
+
+    copies_in = [pltpu.make_async_copy(ins[i], window(i), in_sem.at[i]) for i in range(count)]
+    held = {}
+    for e in range(2):
+        held["gate", e] = pltpu.make_async_copy(weights[3 * e], sides.at[2 * e], weight_sem.at[3 * e])
+        held["up", e] = pltpu.make_async_copy(weights[3 * e + 1], sides.at[2 * e + 1], weight_sem.at[3 * e + 1])
+        held["down", e] = pltpu.make_async_copy(weights[3 * e + 2], downs.at[e], weight_sem.at[3 * e + 2])
+    if forward:
+        copies_act = [pltpu.make_async_copy(acts.at[e], kept.at[e], act_sem.at[e]) for e in range(2)]
+    else:
+        copies_act = [pltpu.make_async_copy(kept.at[e], acts.at[e], act_sem.at[e]) for e in range(2)]
+    for copy in copies_in:
+        copy.start()
+    for e in range(2):
+        for name in ("gate", "up", "down") if forward else ("down", "gate", "up"):
+            held[name, e].start()
+        if not forward:
+            copies_act[e].start()
+    slot_tables(index_ref, table_ref, onehot, factor, ranks, blocks, cap)
+    for copy, group in zip(copies_in, groups):
+        copy.wait()
+        pick_rows(buffer, onehot, rows, group, cap)
+    for e in range(2):
+        (forward_expert if forward else backward_expert)(
+            e, rows, factor, sides.at[2 * e], sides.at[2 * e + 1], downs.at[e],
+            lambda name, e: held[name, e].wait(), acts.at[e],
+            lambda e: copies_act[e].start() if forward else copies_act[e].wait(), hidden,
+        )
+    copies_out = [pltpu.make_async_copy(window(i), outs[i], in_sem.at[i]) for i in range(count)]
+    for copy, group in zip(copies_out, groups):
+        put_rows(buffer, onehot, rows, group, cap)
+        copy.start()
+    for copy in copies_out:
+        copy.wait()
+    if forward:
+        for copy in copies_act:
+            copy.wait()
+
+
+def run_experts(forward, index, table, ins, weights, acts, cap):
+    width, ff, tok = ins[0].shape[1], weights[0].shape[1], table.shape[2]
+    groups, blocks = [], 0
+    for value in ins:
+        groups.append(list(range(blocks, blocks + value.shape[0] // tok)))
+        blocks += value.shape[0] // tok
+    slots = blocks * cap
+    kept = jax.ShapeDtypeStruct((2, 2, slots, ff), F32)
+    out_shape = [jax.ShapeDtypeStruct(value.shape, BF16) for value in ins] + ([kept] if forward else [])
+    in_place = pl.BlockSpec(memory_space=pl.ANY)
+    operands = [index, table, *ins, *weights] + ([] if forward else [acts])
+    return pl.pallas_call(
+        functools.partial(experts_kernel, forward, cap, groups),
+        out_shape=out_shape,
+        in_specs=[pl.BlockSpec(memory_space=pltpu.SMEM), pl.BlockSpec(memory_space=pltpu.VMEM)]
+        + [in_place] * (len(operands) - 2),
+        out_specs=[in_place] * len(out_shape),
+        scratch_shapes=[
+            pltpu.VMEM((blocks * tok, width), BF16),
+            pltpu.VMEM((2, slots, width), BF16),
+            pltpu.VMEM((blocks, 2 * cap, tok), BF16),
+            pltpu.VMEM((2, slots, tok), F32),
+            pltpu.VMEM((2 * blocks, tok), F32),
+            pltpu.VMEM((4, width, ff), BF16),
+            pltpu.VMEM((2, ff, width), BF16),
+            pltpu.VMEM((2, 2, slots, ff), F32),
+            pltpu.VMEM((1 if forward else 2, slots, ff), BF16),
+            pltpu.SemaphoreType.DMA((len(ins),)),
+            pltpu.SemaphoreType.DMA((6,)),
+            pltpu.SemaphoreType.DMA((2,)),
+        ],
+        compiler_params=pltpu.CompilerParams(vmem_limit_bytes=58 << 20),
+        cost_estimate=pl.CostEstimate(
+            flops=2 * 2 * 3 * slots * width * ff,
+            bytes_accessed=2 * (6 * width * ff + 2 * blocks * tok * width) + 16 * slots * ff,
+            transcendentals=2 * slots * ff,
+        ),
+    )(*operands)
+
+
+def ep_permute(value, partner):
+    return lax.ppermute(value, "ep", [(i, partner(i)) for i in range(8)])
+
+
+def first(value):
+    return ep_permute(value, lambda i: i ^ (4 if i & 1 else 2))
+
+
+def second(value):
+    return ep_permute(value, lambda i: i ^ (2 if i & 1 else 4))
+
+
+def along_z(value, k):
+    return lax.ppermute(value, "seq", [(i, i ^ k) for i in range(4)])
+
+
+def add(*values):
+    total = values[0].astype(F32)
+    for value in values[1:]:
+        total = total + value.astype(F32)
+    return total
+
+
+ORDER = (
+    ("g0a", ()), ("x0a", ()), ("x2z", ()), ("x1z", ()), ("w0", ()), ("x0b", ("g0a",)), ("g0b", ("w0", "x0a",)),
+    ("w2", ("w0", "x0a", "g0a",)), ("w1", ("w2",)), ("x3z", ("w2",)), ("x1a", ("x2z", "w2",)),
+    ("x2a", ("w1", "x1z",)), ("x1b", ("w1", "x1z", "x2z",)), ("g2z", ("x3z", "x0b", "w1", "x1z",)),
+    ("tab", ("g0b", "x3z", "x0b", "w1", "x1z",)), ("x3a", ("x1a", "g0b", "x0b", "w1",)),
+    ("x2b", ("x1a", "g0b", "x3z", "x0b",)), ("x3b", ("x2a",)), ("g2a", ("x3a", "x2a",)),
+    ("g3z", ("x3a", "x2a",)), ("g1z", ("x1b", "x2b", "g2z", "x3a",)), ("g2b", ("x1b", "x2b",)),
+    ("F", ("g2a",)), ("o1a", ("g1z", "g2b", "g3z",)), ("g3a", ("F", "g1z", "g2b",)),
+    ("o3b", ("g1z", "g2b", "g3z",)), ("g1b", ("F", "g1z", "g2b", "g3z",)), ("o1z", ()), ("g3b", ("o1a",)),
+    ("o3a", ("g3a", "o1a",)), ("g1a", ("o3b", "g3a", "o1a",)), ("o2b", ("o1z", "o3b", "g3a",)),
+    ("o1b", ("g1b", "o1z", "o3b", "g3a",)), ("o3z", ("g3b", "g1b", "o1z",)), ("B", ("o3a", "o1z",)),
+    ("o2a", ("B", "o1b", "o3z",)), ("d3b", ("o1b", "o3z", "o2b",)), ("d2b", ("o1b", "o3z", "o2b",)),
+    ("d1b", ("o1b", "o3z", "o2b",)), ("o2z", ()), ("d3a", ("o2a",)), ("d1a", ("d2b", "d3b", "o2a",)),
+    ("d2a", ("d3a", "o2z",)), ("d3z", ("o2z", "d2b",)), ("d0b", ("d1a", "d3a", "o2z",)),
+    ("o0b", ("d1b", "d1a", "d3a", "o2z",)), ("d2z", ("d1b", "d1a",)), ("d1z", ("d3z", "d2a", "d1b",)),
+    ("d0a", ("d3z", "d2a",)), ("o0a", ("d0b", "d3z", "d2a",)),
+)
+
+
+def gathered(tokens, expert_ids, route_weights, norm_gain, gate_proj, up_proj, down_proj, out_grad):
+    experts = lax.axis_size("seq") * lax.axis_size("ep")
+    tok, fanout = expert_ids.shape
+    cap = max(2, 3 * tok * fanout // (2 * experts))
+    mine = (gate_proj[0], up_proj[0], down_proj[0])
+    ids = jnp.arange(experts, dtype=jnp.int32)
+    routes = jnp.sum(
+        jnp.where(expert_ids[:, :, None] == ids[None, None, :], route_weights[:, :, None], 0.0), axis=1
+    )
+    pairs = routes.T.reshape(experts // 2, 2, tok)
+    for_device = jnp.stack([pairs, pairs[:, ::-1]], axis=1).reshape(experts, 2 * tok)
+    x_float = tokens.astype(F32)
+    normed = scale_rows(x_float, norm_gain).astype(BF16)
+    z, ep = lax.axis_index("seq"), lax.axis_index("ep")
+    core = ep % 2
+    step_first = jnp.where(core == 1, 4, 2)
+    step_second = jnp.where(core == 1, 2, 4)
+    masks = [0, step_first, step_second, step_first | step_second]
+    done = {"x0": normed, "g0": out_grad}
+
+    def experts_pass(forward, offsets, source, target, acts, wait):
+        keys = [(k, s) for k in offsets for s in "0ab"]
+        blocks = [(k, j) for k, s in keys for j in ((2, 3) if s == "b" else ("0a".index(s),))]
+        index = jnp.stack([(z ^ k) * 8 + (ep ^ masks[j]) for k, j in blocks]).astype(jnp.int32)
+        arrays = [done[source + ("0" if (k, s) == (0, "0") else f"{k}z" if s == "0" else f"{k}{s}")] for k, s in keys]
+        theirs = tuple(done[f"w{i}"] for i in range(3))
+        table = done["tab"].reshape(experts, 2, tok)
+        out = run_experts(forward, wait(index), table, arrays, mine + theirs, acts, cap)
+        for (k, s), value in zip(keys, out):
+            done[f"{target}part{k}{s}"] = value
+        return out
+
+    def spread_step(name, wait):
+        t, k, move = name[0], int(name[1]), name[2]
+        own = done[f"{t}0"]
+        if move == "z":
+            return along_z(wait(done[f"{t}2z"]), 1) if k == 3 else along_z(wait(own), k)
+        if name[1:] == "1b":
+            return along_z(wait(done[f"{t}0b"]), 1)
+        shard = own if k == 0 else done[f"{t}{k}z"]
+        if move == "a":
+            return first(wait(shard))
+        return second(jnp.concatenate([shard, wait(done[f"{t}{k}a"])], axis=0))
+
+    def merge_step(name, wait):
+        t, k, move = name[0], int(name[1]), name[2]
+
+        def part(s):
+            return done[f"{t}part{k}{s}"]
+
+        if name[1:] == "1b":
+            return along_z(wait(part("b")), 1)
+        if move == "b":
+            value = add(part("b"), done[f"{t}1b"]).astype(BF16) if k == 0 else part("b")
+            return second(wait(value))
+        if move == "a":
+            value = part("a") if k == 1 else add(part("a"), done[f"{t}{k}b"][tok:]).astype(BF16)
+            return first(wait(value))
+        value = total(t, k)
+        return along_z(wait(value.astype(BF16)), 2 if k == 2 else 1)
+
+    def total(t, k):
+        values = [done[f"{t}part{k}0"], done[f"{t}{k}a"]]
+        if k != 1:
+            values.append(done[f"{t}{k}b"][:tok])
+        if k == 2:
+            values.append(done[f"{t}3z"])
+        if k == 0:
+            values += [done[f"{t}1z"], done[f"{t}2z"]]
+        return add(*values)
+
+    acts = {}
+    for name, others in ORDER:
+
+        def wait(value, others=others):
+            if not others:
+                return value
+            return lax.optimization_barrier((value, *[done[n] for n in others]))[0]
+
+        with jax.named_scope(name):
+            if name[0] in "FB":
+                offsets = {"0": (0, 2), "1": (1, 3)}.get(name[1:], (0, 1, 2, 3))
+                if name[0] == "F":
+                    out = experts_pass(True, offsets, "x", "o", None, wait)
+                    acts[offsets] = out[-1]
+                else:
+                    out = experts_pass(False, offsets, "g", "d", acts[offsets], wait)
+                done[name] = out[0]
+            elif name == "tab":
+                done[name] = lax.all_to_all(wait(for_device), ("seq", "ep"), split_axis=0, concat_axis=0, tiled=True)
+            elif name[0] == "w":
+                done[name] = ep_permute(wait(mine[int(name[1])]), lambda i: i ^ 1)
+            else:
+                done[name] = (spread_step if name[0] in "xg" else merge_step)(name, wait)
+    return (total("o", 0).astype(BF16), norm_grad(x_float, norm_gain, total("d", 0)))
 
 
 def expert_forward(inputs, gate_w, up_w, down_w):
@@ -47,7 +364,7 @@
     return outputs
 
 
-def shards(tokens, expert_ids, route_weights, norm_gain, gate_proj, up_proj, down_proj, out_grad):
+def exchanged(tokens, expert_ids, route_weights, norm_gain, gate_proj, up_proj, down_proj, out_grad):
     own_weights = (gate_proj[0], up_proj[0], down_proj[0])
     experts = lax.axis_size("seq") * lax.axis_size("ep")
     tok_count, fanout = expert_ids.shape
@@ -114,19 +431,13 @@
 
 
 def solution(mesh):
+    rows = P(("seq", "ep"), None)
+    cubes = P(("seq", "ep"), None, None)
+    planes = mesh.shape["seq"] == 4 and mesh.shape["ep"] == 8
     return jax.shard_map(
-        shards,
+        gathered if planes else exchanged,
         mesh=mesh,
-        in_specs=(
-            P(("seq", "ep"), None),
-            P(("seq", "ep"), None),
-            P(("seq", "ep"), None),
-            P(),
-            P(("seq", "ep"), None, None),
-            P(("seq", "ep"), None, None),
-            P(("seq", "ep"), None, None),
-            P(("seq", "ep"), None),
-        ),
-        out_specs=(P(("seq", "ep"), None), P(("seq", "ep"), None)),
+        in_specs=(rows, rows, rows, P(), cubes, cubes, cubes, rows),
+        out_specs=(rows, rows),
         check_vma=False,
     )

time: 657 us -> 335 us (0.51)
  waiting for transfers between devices: 351 us -> 183 us
  blocking collectives: 146 us -> 0 us
  starting transfers between devices: 11.9 us -> 72.8 us
  Pallas kernels: 0 us -> 60.7 us
  local copies, waits for them, and re-layouts: 60.9 us -> 2.87 us
  matrix products: 53.7 us -> 0 us
  other arithmetic: 32.1 us -> 12.4 us
    all_to_all x3 -> x1, waiting for transfers between devices: 351 us -> 0.01 us  [gathered(): lax.all_to_all(wait(for_device), ('seq', 'ep'), split_axis=0, concat_axis...]
    ppermute x0 -> x47, waiting for transfers between devices: none -> 183 us  [the longest x31 130 us: ep_permute(): return lax.ppermute(value, 'ep', [(i, partner(i)) for i in range(8)])]
    all_to_all x1 -> x0, blocking collectives: 146 us -> none  [move_out(): lax.all_to_all(slots, ('seq', 'ep'), split_axis=0, concat_axis=0, tiled=T...]
    ppermute x0 -> x47, starting transfers between devices: none -> 68.6 us  [the longest x31 41.2 us: ep_permute(): return lax.ppermute(value, 'ep', [(i, partner(i)) for i in range(8)])]
    pallas_call x0 -> x2, Pallas kernels: none -> 60.7 us  [run_experts(): pl.pallas_call(functools.partial(experts_kernel, forward, cap, groups), o...]
    dot_general x6 -> x0, matrix products: 53.7 us -> none  [the longest x1 13.1 us: expert_backward(): lax.dot_general(grad_gate, gate_w, pairs, preferred_element_type=jnp.floa...]
    gather x4 -> x0, local copies, waits for them, and re-layouts: 52.6 us -> none  [the longest x1 13.8 us: shards(): normed[source]]
    reduce_sum x2 -> x1, other arithmetic: 9.3 us -> 0.02 us  [gathered(): jnp.sum(jnp.where(expert_ids[:, :, None] == ids[None, None, :], route_wei...]
  transfers between devices with their start and end apart: 3 -> 48, of which waited for: 3 -> 25; matrix products, arithmetic and copies ran while one was open for 10% -> 3% of each run, Pallas kernels for 0% -> 18%
where the time goes in v3:
time: 335 us; the launch traced here: 334 us
  waiting for transfers between devices  183 us (55%)
  starting transfers between devices  72.8 us (22%)
  Pallas kernels  60.7 us (18%)
  other arithmetic  12.4 us (4%)
    ppermute x31, waiting for transfers between devices, ep_permute(): return lax.ppermute(value, 'ep', [(i, partner(i)) for i in range(8)])  130 us
    pallas_call x2, Pallas kernels, run_experts(): pl.pallas_call(functools.partial(experts_kernel, forward, cap, groups), o...  60.7 us
    ppermute x16, waiting for transfers between devices, along_z(): return lax.ppermute(value, 'seq', [(i, i ^ k) for i in range(4)])  52.8 us
    ppermute x31, starting transfers between devices, ep_permute(): return lax.ppermute(value, 'ep', [(i, partner(i)) for i in range(8)])  41.2 us
    ppermute x16, starting transfers between devices, along_z(): return lax.ppermute(value, 'seq', [(i, i ^ k) for i in range(4)])  27.4 us
  transfers between devices with their start and end apart: 48, of which 25 were waited for; matrix products, arithmetic and copies ran while one was open for 3% of the time, Pallas kernels for 18%

profile of v3, /device:TPU:0, one launch (start us, length us, event | category | flops | bytes accessed | tf_op | source)
XLA Modules:
  0.0 333.6 jit_solution(12009235157632431634)
XLA Ops:
  6.3 7.1 %collective-permute-done.2.refs_2_ = bf16[128,2048]{1,0:T(8,128)(2,1)S(1)} collective-permute-done((bf16[128,2048]{1,0:T(8,128)(2,1)S(1)}, bf16[128,2048]{1,0:T(8,128)(2,1)S(1)}, u32[]{:S(2)}, u32[]{:S(2)}) %collective-permute-start.2) | collective-permute-done | bytes 524320 | tf_op jit(solution)/shard_map/x0a/ppermute | solution.py:193
  13.4 5.6 %collective-permute-done.3.refs_2_ = bf16[128,2048]{1,0:T(8,128)(2,1)S(1)} collective-permute-done((bf16[128,2048]{1,0:T(8,128)(2,1)}, bf16[128,2048]{1,0:T(8,128)(2,1)S(1)}, u32[]{:S(2)}, u32[]{:S(2)}) %collective-permute-start.3) | collective-permute-done | bytes 524320 | tf_op jit(solution)/shard_map/g0a/ppermute | solution.py:193
  19.1 5.9 %collective-permute-done.4.refs_18_ = bf16[768,2048]{1,0:T(8,128)(2,1)S(1)} collective-permute-done((bf16[768,2048]{1,0:T(8,128)(2,1)}, bf16[768,2048]{1,0:T(8,128)(2,1)S(1)}, u32[]{:S(2)}, u32[]{:S(2)}) %collective-permute-start.4) | collective-permute-done | bytes 3145760 | tf_op jit(solution)/shard_map/w2/ppermute | solution.py:193
  32.2 18.6 %collective-permute-done.8.refs_4_ = bf16[128,2048]{1,0:T(8,128)(2,1)S(1)} collective-permute-done((bf16[128,2048]{1,0:T(8,128)(2,1)S(1)}, bf16[128,2048]{1,0:T(8,128)(2,1)S(1)}, u32[]{:S(2)}, u32[]{:S(2)}) %collective-permute-start.8) | collective-permute-done | bytes 524320 | tf_op jit(solution)/shard_map/x1z/ppermute | solution.py:205
  56.2 9.2 %collective-permute-done.5.refs_10_ = bf16[128,2048]{1,0:T(8,128)(2,1)S(1)} collective-permute-done((bf16[128,2048]{1,0:T(8,128)(2,1)S(1)}, bf16[128,2048]{1,0:T(8,128)(2,1)S(1)}, u32[]{:S(2)}, u32[]{:S(2)}) %collective-permute-start.5) | collective-permute-done | bytes 524320 | tf_op jit(solution)/shard_map/x3z/ppermute | solution.py:205
  79.6 12.7 %collective-permute-done.9.refs_7_ = bf16[128,2048]{1,0:T(8,128)(2,1)S(1)} collective-permute-done((bf16[128,2048]{1,0:T(8,128)(2,1)S(1)}, bf16[128,2048]{1,0:T(8,128)(2,1)S(1)}, u32[]{:S(2)}, u32[]{:S(2)}) %collective-permute-start.9) | collective-permute-done | bytes 524320 | tf_op jit(solution)/shard_map/g2z/ppermute | solution.py:205
  95.3 4.2 %all-to-all-start = ((f32[32,1,256]{2,1,0:T(1,128)}), f32[32,1,256]{2,1,0:T(1,128)S(1)}, u32[]{:S(2)}, u32[]{:S(2)}) async-start(f32[32,1,256]{2,1,0:T(1,128)} %all_to_all.6), calls=%async_computation | async-start | bytes 65536 | tf_op jit(solution)/shard_map/tab/all_to_all | solution.py:323
  108.8 28.6 %F.1 = (bf16[128,2048]{1,0:T(8,128)(2,1)}, bf16[128,2048]{1,0:T(8,128)(2,1)}, bf16[256,2048]{1,0:T(8,128)(2,1)}, bf16[128,2048]{1,0:T(8,128)(2,1)}, bf16[128,204...) custom-call(s32[16]{0:T(128)} %stack.90.index_ref, ...), custom_call_target="tpu_custom_call" | custom-call | flops 14495514624 | bytes 45088768 | tf_op jit(solution)/shard_map/F/pallas_call | solution.py:163
  143.2 9.3 %collective-permute-done.25.refs_11_ = bf16[128,2048]{1,0:T(8,128)(2,1)S(1)} collective-permute-done((bf16[128,2048]{1,0:T(8,128)(2,1)}, bf16[128,2048]{1,0:T(8,128)(2,1)S(1)}, u32[]{:S(2)}, u32[]{:S(2)}) %collective-permute-start.25) | collective-permute-done | bytes 524320 | tf_op jit(solution)/shard_map/g3a/ppermute | solution.py:193
  152.5 11.0 %collective-permute-done.22 = bf16[128,2048]{1,0:T(8,128)(2,1)S(1)} collective-permute-done((bf16[128,2048]{1,0:T(8,128)(2,1)}, bf16[128,2048]{1,0:T(8,128)(2,1)S(1)}, u32[]{:S(2)}, u32[]{:S(2)}) %collective-permute-start.22) | collective-permute-done | bytes 524320 | tf_op jit(solution)/shard_map/o1a/ppermute | solution.py:193
  170.6 5.7 %collective-permute-done.23 = bf16[128,2048]{1,0:T(8,128)(2,1)S(1)} collective-permute-done((bf16[128,2048]{1,0:T(8,128)(2,1)S(1)}, bf16[128,2048]{1,0:T(8,128)(2,1)S(1)}, u32[]{:S(2)}, u32[]{:S(2)}) %collective-permute-start.23) | collective-permute-done | bytes 524320 | tf_op jit(solution)/shard_map/o1z/ppermute | solution.py:205
  178.6 4.7 %collective-permute-done.27 = bf16[128,2048]{1,0:T(8,128)(2,1)S(1)} collective-permute-done((bf16[128,2048]{1,0:T(8,128)(2,1)S(1)}, bf16[128,2048]{1,0:T(8,128)(2,1)S(1)}, u32[]{:S(2)}, u32[]{:S(2)}) %collective-permute-start.27) | collective-permute-done | bytes 524320 | tf_op jit(solution)/shard_map/o3a/ppermute | solution.py:193
  183.6 4.8 %collective-permute-done.29.refs_12_ = bf16[256,2048]{1,0:T(8,128)(2,1)} collective-permute-done((bf16[256,2048]{1,0:T(8,128)(2,1)S(1)}, bf16[256,2048]{1,0:T(8,128)(2,1)}, u32[]{:S(2)}, u32[]{:S(2)}) %collective-permute-start.29) | collective-permute-done | bytes 1048608 | tf_op jit(solution)/shard_map/g3b/ppermute | solution.py:193
  188.4 6.1 %collective-permute-done.28.refs_5_ = bf16[128,2048]{1,0:T(8,128)(2,1)S(1)} collective-permute-done((bf16[128,2048]{1,0:T(8,128)(2,1)}, bf16[128,2048]{1,0:T(8,128)(2,1)S(1)}, u32[]{:S(2)}, u32[]{:S(2)}) %collective-permute-start.28) | collective-permute-done | bytes 524320 | tf_op jit(solution)/shard_map/g1a/ppermute | solution.py:193
  195.4 32.1 %B.1 = (bf16[128,2048]{1,0:T(8,128)(2,1)}, bf16[128,2048]{1,0:T(8,128)(2,1)}, bf16[256,2048]{1,0:T(8,128)(2,1)}, bf16[128,2048]{1,0:T(8,128)(2,1)}, bf16[128,204...) custom-call(s32[16]{0:T(128)} %stack.90.index_ref, ...), custom_call_target="tpu_custom_call" | custom-call | flops 14495514624 | bytes 45088768 | tf_op jit(solution)/shard_map/B/pallas_call | solution.py:163
  232.3 10.6 %collective-permute-done.35 = bf16[128,2048]{1,0:T(8,128)(2,1)S(1)} collective-permute-done((bf16[128,2048]{1,0:T(8,128)(2,1)S(1)}, bf16[128,2048]{1,0:T(8,128)(2,1)S(1)}, u32[]{:S(2)}, u32[]{:S(2)}) %collective-permute-start.35) | collective-permute-done | bytes 524320 | tf_op jit(solution)/shard_map/o2a/ppermute | solution.py:193
  245.6 10.9 %collective-permute-done.33 = bf16[256,2048]{1,0:T(8,128)(2,1)S(1)} collective-permute-done((bf16[256,2048]{1,0:T(8,128)(2,1)}, bf16[256,2048]{1,0:T(8,128)(2,1)S(1)}, u32[]{:S(2)}, u32[]{:S(2)}) %collective-permute-start.33) | collective-permute-done | bytes 1048608 | tf_op jit(solution)/shard_map/d2b/ppermute | solution.py:193
  256.6 3.9 %collective-permute-start.36 = (bf16[128,2048]{1,0:T(8,128)(2,1)S(1)}, bf16[128,2048]{1,0:T(8,128)(2,1)S(1)}, u32[]{:S(2)}, u32[]{:S(2)}) collective-permute-start(bf16[128,2048]{1,0:T(8,128)(2,1)S(1)} %copy-done.38), channel_id=1, source_target_pairs={{0,2},{1,5},{2,0},{3,7},{4,6},{5,1},{6,4},{7,3},{8,10},{9,13},{10,... | collective-permute-start | bytes 1572872 | tf_op jit(solution)/shard_map/d1a/ppermute | solution.py:193
  261.1 16.5 %collective-permute-done.37 = bf16[128,2048]{1,0:T(8,128)(2,1)S(1)} collective-permute-done((bf16[128,2048]{1,0:T(8,128)(2,1)S(1)}, bf16[128,2048]{1,0:T(8,128)(2,1)S(1)}, u32[]{:S(2)}, u32[]{:S(2)}) %collective-permute-start.37) | collective-permute-done | bytes 524320 | tf_op jit(solution)/shard_map/d3a/ppermute | solution.py:193
  286.7 6.5 %collective-permute-done.42 = bf16[128,2048]{1,0:T(8,128)(2,1)S(1)} collective-permute-done((bf16[128,2048]{1,0:T(8,128)(2,1)S(1)}, bf16[128,2048]{1,0:T(8,128)(2,1)S(1)}, u32[]{:S(2)}, u32[]{:S(2)}) %collective-permute-start.42) | collective-permute-done | bytes 524320 | tf_op jit(solution)/shard_map/d2a/ppermute | solution.py:193
  294.2 5.2 %collective-permute-start.45 = (bf16[128,2048]{1,0:T(8,128)(2,1)S(1)}, bf16[128,2048]{1,0:T(8,128)(2,1)S(1)}, u32[]{:S(2)}, u32[]{:S(2)}) collective-permute-start(bf16[128,2048]{1,0:T(8,128)(2,1)S(1)} %add_convert_fusion.3), channel_id=1, source_target_pairs={{0,8},{8,0},{16,24},{24,16},{1,9},{9,1},{17,25},{25,17},{2,10},{10... | collective-permute-start | bytes 1572872 | tf_op jit(solution)/shard_map/d1z/ppermute | solution.py:205
  299.3 5.4 %collective-permute-done.40 = bf16[256,2048]{1,0:T(8,128)(2,1)S(1)} collective-permute-done((bf16[256,2048]{1,0:T(8,128)(2,1)S(1)}, bf16[256,2048]{1,0:T(8,128)(2,1)S(1)}, u32[]{:S(2)}, u32[]{:S(2)}) %collective-permute-start.40) | collective-permute-done | bytes 1048608 | tf_op jit(solution)/shard_map/d0b/ppermute | solution.py:193
  306.8 14.6 %collective-permute-done.39 = bf16[256,2048]{1,0:T(8,128)(2,1)S(1)} collective-permute-done((bf16[256,2048]{1,0:T(8,128)(2,1)S(1)}, bf16[256,2048]{1,0:T(8,128)(2,1)S(1)}, u32[]{:S(2)}, u32[]{:S(2)}) %collective-permute-start.39) | collective-permute-done | bytes 1048608 | tf_op jit(solution)/shard_map/o0b/ppermute | solution.py:193
  324.2 6.6 %collective-permute-done.43 = bf16[128,2048]{1,0:T(8,128)(2,1)S(1)} collective-permute-done((bf16[128,2048]{1,0:T(8,128)(2,1)S(1)}, bf16[128,2048]{1,0:T(8,128)(2,1)S(1)}, u32[]{:S(2)}, u32[]{:S(2)}) %collective-permute-start.43) | collective-permute-done | bytes 524320 | tf_op jit(solution)/shard_map/o0a/ppermute | solution.py:193
  (188 shorter events, 86.3 us)
Async XLA Ops:
  25.0 30.6 %collective-permute-start.7 = (bf16[2048,768]{1,0:T(8,128)(2,1)}, bf16[2048,768]{1,0:T(8,128)(2,1)}, u32[]{:S(2)}, u32[]{:S(2)}) collective-permute-start(bf16[2048,768]{1,0:T(8,128)(2,1)} %bitcast.41), channel_id=1, source_target_pairs={{0,1},{1,0},{2,3},{3,2},{4,5},{5,4},{6,7},{7,6},{8,9},{9,8},{10,11... | collective-permute-start | bytes 9437192 | tf_op jit(solution)/shard_map/w1/ppermute | solution.py:193
  25.1 25.7 %collective-permute-start.8 = (bf16[128,2048]{1,0:T(8,128)(2,1)S(1)}, bf16[128,2048]{1,0:T(8,128)(2,1)S(1)}, u32[]{:S(2)}, u32[]{:S(2)}) collective-permute-start(bf16[128,2048]{1,0:T(8,128)(2,1)S(1)} %fusion.3.refs_1_), channel_id=1, source_target_pairs={{0,8},{8,0},{16,24},{24,16},{1,9},{9,1},{17,25},{25,17},{2,10},{10... | collective-permute-start | bytes 1572872 | tf_op jit(solution)/shard_map/x1z/ppermute | solution.py:205
  27.2 26.1 %collective-permute-start = (bf16[128,2048]{1,0:T(8,128)(2,1)S(1)}, bf16[128,2048]{1,0:T(8,128)(2,1)S(1)}, u32[]{:S(2)}, u32[]{:S(2)}) collective-permute-start(bf16[128,2048]{1,0:T(8,128)(2,1)S(1)} %fusion.3.refs_1_), channel_id=1, source_target_pairs={{0,16},{8,24},{16,0},{24,8},{1,17},{9,25},{17,1},{25,9},{2,18},{10... | collective-permute-start | bytes 1572872 | tf_op jit(solution)/shard_map/x2z/ppermute | solution.py:205
  29.9 26.2 %collective-permute-start.6 = (bf16[256,2048]{1,0:T(8,128)(2,1)S(1)}, bf16[256,2048]{1,0:T(8,128)(2,1)}, u32[]{:S(2)}, u32[]{:S(2)}) collective-permute-start(bf16[256,2048]{1,0:T(8,128)(2,1)S(1)} %pad_maximum_fusion), channel_id=1, source_target_pairs={{0,4},{1,3},{2,6},{3,1},{4,0},{5,7},{6,2},{7,5},{8,12},{9,11},{10,... | collective-permute-start | bytes 3145736 | tf_op jit(solution)/shard_map/x0b/ppermute | solution.py:193
  31.6 24.6 %collective-permute-start.11 = (bf16[256,2048]{1,0:T(8,128)(2,1)S(1)}, bf16[256,2048]{1,0:T(8,128)(2,1)S(1)}, u32[]{:S(2)}, u32[]{:S(2)}) collective-permute-start(bf16[256,2048]{1,0:T(8,128)(2,1)S(1)} %pad_maximum_fusion.1), channel_id=1, source_target_pairs={{0,4},{1,3},{2,6},{3,1},{4,0},{5,7},{6,2},{7,5},{8,12},{9,11},{10,... | collective-permute-start | bytes 3145736 | tf_op jit(solution)/shard_map/g0b/ppermute | solution.py:193
  67.0 25.2 %collective-permute-start.9 = (bf16[128,2048]{1,0:T(8,128)(2,1)S(1)}, bf16[128,2048]{1,0:T(8,128)(2,1)S(1)}, u32[]{:S(2)}, u32[]{:S(2)}) collective-permute-start(bf16[128,2048]{1,0:T(8,128)(2,1)S(1)} %copy-done.14), channel_id=1, source_target_pairs={{0,16},{8,24},{16,0},{24,8},{1,17},{9,25},{17,1},{25,9},{2,18},{10... | collective-permute-start | bytes 1572872 | tf_op jit(solution)/shard_map/g2z/ppermute | solution.py:205
  70.4 36.0 %collective-permute-start.15 = (bf16[256,2048]{1,0:T(8,128)(2,1)}, bf16[256,2048]{1,0:T(8,128)(2,1)}, u32[]{:S(2)}, u32[]{:S(2)}) collective-permute-start(bf16[256,2048]{1,0:T(8,128)(2,1)} %collective-permute-done.6.refs_3_), channel_id=1, source_target_pairs={{0,8},{8,0},{16,24},{24,16},{1,9},{9,1},{17,25},{25,17},{2,10},{10... | collective-permute-start | bytes 3145736 | tf_op jit(solution)/shard_map/x1b/ppermute | solution.py:205
  72.3 34.2 %collective-permute-start.16 = (bf16[256,2048]{1,0:T(8,128)(2,1)S(1)}, bf16[256,2048]{1,0:T(8,128)(2,1)}, u32[]{:S(2)}, u32[]{:S(2)}) collective-permute-start(bf16[256,2048]{1,0:T(8,128)(2,1)S(1)} %pad_maximum_fusion.2), channel_id=1, source_target_pairs={{0,4},{1,3},{2,6},{3,1},{4,0},{5,7},{6,2},{7,5},{8,12},{9,11},{10,... | collective-permute-start | bytes 3145736 | tf_op jit(solution)/shard_map/x2b/ppermute | solution.py:193
  77.0 31.2 %collective-permute-start.17 = (bf16[256,2048]{1,0:T(8,128)(2,1)S(1)}, bf16[256,2048]{1,0:T(8,128)(2,1)}, u32[]{:S(2)}, u32[]{:S(2)}) collective-permute-start(bf16[256,2048]{1,0:T(8,128)(2,1)S(1)} %pad_maximum_fusion.3), channel_id=1, source_target_pairs={{0,4},{1,3},{2,6},{3,1},{4,0},{5,7},{6,2},{7,5},{8,12},{9,11},{10,... | collective-permute-start | bytes 3145736 | tf_op jit(solution)/shard_map/x3b/ppermute | solution.py:193
  99.5 38.0 %collective-permute-start.20 = (bf16[128,2048]{1,0:T(8,128)(2,1)S(1)}, bf16[128,2048]{1,0:T(8,128)(2,1)}, u32[]{:S(2)}, u32[]{:S(2)}) collective-permute-start(bf16[128,2048]{1,0:T(8,128)(2,1)S(1)} %collective-permute-done.9.refs_7_), channel_id=1, source_target_pairs={{0,8},{8,0},{16,24},{24,16},{1,9},{9,1},{17,25},{25,17},{2,10},{10... | collective-permute-start | bytes 1572872 | tf_op jit(solution)/shard_map/g3z/ppermute | solution.py:205
  106.4 31.1 %collective-permute-start.18 = (bf16[128,2048]{1,0:T(8,128)(2,1)S(1)}, bf16[128,2048]{1,0:T(8,128)(2,1)}, u32[]{:S(2)}, u32[]{:S(2)}) collective-permute-start(bf16[128,2048]{1,0:T(8,128)(2,1)S(1)} %copy-done.14), channel_id=1, source_target_pairs={{0,8},{8,0},{16,24},{24,16},{1,9},{9,1},{17,25},{25,17},{2,10},{10... | collective-permute-start | bytes 1572872 | tf_op jit(solution)/shard_map/g1z/ppermute | solution.py:205
  108.1 29.4 %collective-permute-start.19 = (bf16[256,2048]{1,0:T(8,128)(2,1)S(1)}, bf16[256,2048]{1,0:T(8,128)(2,1)}, u32[]{:S(2)}, u32[]{:S(2)}) collective-permute-start(bf16[256,2048]{1,0:T(8,128)(2,1)S(1)} %pad_maximum_fusion.4), channel_id=1, source_target_pairs={{0,4},{1,3},{2,6},{3,1},{4,0},{5,7},{6,2},{7,5},{8,12},{9,11},{10,... | collective-permute-start | bytes 3145736 | tf_op jit(solution)/shard_map/g2b/ppermute | solution.py:193
  139.1 24.4 %collective-permute-start.22 = (bf16[128,2048]{1,0:T(8,128)(2,1)}, bf16[128,2048]{1,0:T(8,128)(2,1)S(1)}, u32[]{:S(2)}, u32[]{:S(2)}) collective-permute-start(bf16[128,2048]{1,0:T(8,128)(2,1)} %get-tuple-element.93), channel_id=1, source_target_pairs={{0,2},{1,5},{2,0},{3,7},{4,6},{5,1},{6,4},{7,3},{8,10},{9,13},{10,... | collective-permute-start | bytes 1572872 | tf_op jit(solution)/shard_map/o1a/ppermute | solution.py:193
  139.6 28.5 %collective-permute-start.24 = (bf16[256,2048]{1,0:T(8,128)(2,1)}, bf16[256,2048]{1,0:T(8,128)(2,1)S(1)}, u32[]{:S(2)}, u32[]{:S(2)}) collective-permute-start(bf16[256,2048]{1,0:T(8,128)(2,1)} %get-tuple-element.95), channel_id=1, source_target_pairs={{0,4},{1,3},{2,6},{3,1},{4,0},{5,7},{6,2},{7,5},{8,12},{9,11},{10,... | collective-permute-start | bytes 3145736 | tf_op jit(solution)/shard_map/o3b/ppermute | solution.py:193
  141.6 34.7 %collective-permute-start.21 = (bf16[256,2048]{1,0:T(8,128)(2,1)S(1)}, bf16[256,2048]{1,0:T(8,128)(2,1)S(1)}, u32[]{:S(2)}, u32[]{:S(2)}) collective-permute-start(bf16[256,2048]{1,0:T(8,128)(2,1)S(1)} %copy-done.33), channel_id=1, source_target_pairs={{0,8},{8,0},{16,24},{24,16},{1,9},{9,1},{17,25},{25,17},{2,10},{10... | collective-permute-start | bytes 3145736 | tf_op jit(solution)/shard_map/g1b/ppermute | solution.py:205
  176.3 51.2 %collective-permute-start.26 = (bf16[256,2048]{1,0:T(8,128)(2,1)}, bf16[256,2048]{1,0:T(8,128)(2,1)S(1)}, u32[]{:S(2)}, u32[]{:S(2)}) collective-permute-start(bf16[256,2048]{1,0:T(8,128)(2,1)} %get-tuple-element.97), channel_id=1, source_target_pairs={{0,8},{8,0},{16,24},{24,16},{1,9},{9,1},{17,25},{25,17},{2,10},{10... | collective-permute-start | bytes 3145736 | tf_op jit(solution)/shard_map/o1b/ppermute | solution.py:205
  177.1 50.4 %collective-permute-start.31 = (bf16[256,2048]{1,0:T(8,128)(2,1)S(1)}, bf16[256,2048]{1,0:T(8,128)(2,1)S(1)}, u32[]{:S(2)}, u32[]{:S(2)}) collective-permute-start(bf16[256,2048]{1,0:T(8,128)(2,1)S(1)} %copy-done.34), channel_id=1, source_target_pairs={{0,4},{1,3},{2,6},{3,1},{4,0},{5,7},{6,2},{7,5},{8,12},{9,11},{10,... | collective-permute-start | bytes 3145736 | tf_op jit(solution)/shard_map/o2b/ppermute | solution.py:193
  188.4 39.0 %collective-permute-start.30 = (bf16[128,2048]{1,0:T(8,128)(2,1)S(1)}, bf16[128,2048]{1,0:T(8,128)(2,1)S(1)}, u32[]{:S(2)}, u32[]{:S(2)}) collective-permute-start(bf16[128,2048]{1,0:T(8,128)(2,1)S(1)} %add_convert_fusion.12), channel_id=1, source_target_pairs={{0,8},{8,0},{16,24},{24,16},{1,9},{9,1},{17,25},{25,17},{2,10},{10... | collective-permute-start | bytes 1572872 | tf_op jit(solution)/shard_map/o3z/ppermute | solution.py:205
  229.8 26.7 %collective-permute-start.33 = (bf16[256,2048]{1,0:T(8,128)(2,1)}, bf16[256,2048]{1,0:T(8,128)(2,1)S(1)}, u32[]{:S(2)}, u32[]{:S(2)}) collective-permute-start(bf16[256,2048]{1,0:T(8,128)(2,1)} %get-tuple-element.112), channel_id=1, source_target_pairs={{0,4},{1,3},{2,6},{3,1},{4,0},{5,7},{6,2},{7,5},{8,12},{9,11},{10,... | collective-permute-start | bytes 3145736 | tf_op jit(solution)/shard_map/d2b/ppermute | solution.py:193
  231.8 28.7 %collective-permute-start.32 = (bf16[256,2048]{1,0:T(8,128)(2,1)}, bf16[256,2048]{1,0:T(8,128)(2,1)S(1)}, u32[]{:S(2)}, u32[]{:S(2)}) collective-permute-start(bf16[256,2048]{1,0:T(8,128)(2,1)} %get-tuple-element.109), channel_id=1, source_target_pairs={{0,8},{8,0},{16,24},{24,16},{1,9},{9,1},{17,25},{25,17},{2,10},{10... | collective-permute-start | bytes 3145736 | tf_op jit(solution)/shard_map/d1b/ppermute | solution.py:205
  243.3 34.6 %collective-permute-start.38 = (bf16[128,2048]{1,0:T(8,128)(2,1)S(1)}, bf16[128,2048]{1,0:T(8,128)(2,1)S(1)}, u32[]{:S(2)}, u32[]{:S(2)}) collective-permute-start(bf16[128,2048]{1,0:T(8,128)(2,1)S(1)} %add_convert_fusion.9), channel_id=1, source_target_pairs={{0,16},{8,24},{16,0},{24,8},{1,17},{9,25},{17,1},{25,9},{2,18},{10... | collective-permute-start | bytes 1572872 | tf_op jit(solution)/shard_map/o2z/ppermute | solution.py:205
  284.5 36.9 %collective-permute-start.39 = (bf16[256,2048]{1,0:T(8,128)(2,1)S(1)}, bf16[256,2048]{1,0:T(8,128)(2,1)S(1)}, u32[]{:S(2)}, u32[]{:S(2)}) collective-permute-start(bf16[256,2048]{1,0:T(8,128)(2,1)S(1)} %add_convert_fusion.1), channel_id=1, source_target_pairs={{0,4},{1,3},{2,6},{3,1},{4,0},{5,7},{6,2},{7,5},{8,12},{9,11},{10,... | collective-permute-start | bytes 3145736 | tf_op jit(solution)/shard_map/o0b/ppermute | solution.py:193
  294.2 29.3 %collective-permute-start.45 = (bf16[128,2048]{1,0:T(8,128)(2,1)S(1)}, bf16[128,2048]{1,0:T(8,128)(2,1)S(1)}, u32[]{:S(2)}, u32[]{:S(2)}) collective-permute-start(bf16[128,2048]{1,0:T(8,128)(2,1)S(1)} %add_convert_fusion.3), channel_id=1, source_target_pairs={{0,8},{8,0},{16,24},{24,16},{1,9},{9,1},{17,25},{25,17},{2,10},{10... | collective-permute-start | bytes 1572872 | tf_op jit(solution)/shard_map/d1z/ppermute | solution.py:205
  299.3 24.2 %collective-permute-start.46 = (bf16[128,2048]{1,0:T(8,128)(2,1)S(1)}, bf16[128,2048]{1,0:T(8,128)(2,1)S(1)}, u32[]{:S(2)}, u32[]{:S(2)}) collective-permute-start(bf16[128,2048]{1,0:T(8,128)(2,1)S(1)} %add_convert_fusion.2), channel_id=1, source_target_pairs={{0,16},{8,24},{16,0},{24,8},{1,17},{9,25},{17,1},{25,9},{2,18},{10... | collective-permute-start | bytes 1572872 | tf_op jit(solution)/shard_map/d2z/ppermute | solution.py:205
  (64 other events, 1275.7 us)

commit v4 on v3

--- a/solution.py
+++ b/solution.py
@@ -33,15 +33,17 @@
     before = lax.broadcasted_iota(jnp.int32, (tok, tok), 0) < lax.broadcasted_iota(jnp.int32, (tok, tok), 1)
     ranks[...] = jnp.dot(marks, jnp.where(before, 1.0, 0.0).astype(BF16), preferred_element_type=F32)
     slots = lax.broadcasted_iota(jnp.int32, (cap, tok), 0).astype(F32)
-    for b in range(blocks):
+
+    @pl.loop(0, blocks)
+    def _(b):
         weights = table_ref[index_ref[b]]
         for e in range(2):
             weight = weights[e : e + 1, :]
-            rank = jnp.where(weight > 0.0, ranks[2 * b + e : 2 * b + e + 1, :], -1.0)
+            rank = jnp.where(weight > 0.0, ranks[pl.ds(2 * b + e, 1), :], -1.0)
             hit = slots == rank
             onehot[b, e * cap : (e + 1) * cap, :] = jnp.where(hit, 1.0, 0.0).astype(BF16)
             slot_weight = jnp.sum(jnp.where(hit, weight, 0.0), axis=1, keepdims=True)
-            factor[e, b * cap : (b + 1) * cap, :] = jnp.broadcast_to(slot_weight, (cap, tok))
+            factor[e, pl.ds(pl.multiple_of(b * cap, 16), cap), :] = jnp.broadcast_to(slot_weight, (cap, tok))
 
 
 def pick_rows(buffer, onehot, rows, blocks, cap):
@@ -66,34 +68,33 @@
 
 
 def forward_expert(e, rows, factor, gate_w, up_w, down_w, arrived, acts, keep, hidden):
-    arrived("gate", e), arrived("up", e)
+    arrived(0), arrived(1)
     for n in tiles(gate_w.shape[1], 256):
         gate_act = jnp.dot(rows[e], gate_w[:, n], preferred_element_type=F32)
         upward = jnp.dot(rows[e], up_w[:, n], preferred_element_type=F32)
-        acts[0, :, n] = gate_act
-        acts[1, :, n] = upward
-        hidden[0, :, n] = (gate_act * jax.nn.sigmoid(gate_act) * upward).astype(BF16)
-    keep(e)
-    arrived("down", e)
+        sigmoid = jax.nn.sigmoid(gate_act)
+        silu = gate_act * sigmoid
+        acts[0, :, n] = (upward * sigmoid * (1.0 + gate_act * (1.0 - sigmoid))).astype(BF16)
+        acts[1, :, n] = silu.astype(BF16)
+        hidden[0, :, n] = (silu * upward).astype(BF16)
+    keep.start()
+    arrived(2)
     for n in tiles(down_w.shape[1], 512):
         total = jnp.dot(hidden[0], down_w[:, n], preferred_element_type=F32)
-        rows[e, :, n] = (total * factor[e][:, :1]).astype(BF16)
+        rows[e, :, n] = (total * factor[e, :, :1]).astype(BF16)
 
 
 def backward_expert(e, rows, factor, gate_w, up_w, down_w, arrived, acts, keep, hidden):
-    arrived("down", e), keep(e)
+    arrived(2), keep.wait()
     for n in tiles(gate_w.shape[1], 256):
         grad_hidden = lax.dot_general(rows[e], down_w[n, :], PAIRS, preferred_element_type=F32)
-        gate_act = acts[0, :, n]
-        sigmoid = jax.nn.sigmoid(gate_act)
-        slope = sigmoid * (1.0 + gate_act * (1.0 - sigmoid))
-        hidden[0, :, n] = (grad_hidden * acts[1, :, n] * slope).astype(BF16)
-        hidden[1, :, n] = (grad_hidden * (gate_act * sigmoid)).astype(BF16)
-    arrived("gate", e), arrived("up", e)
+        hidden[0, :, n] = (grad_hidden * acts[0, :, n].astype(F32)).astype(BF16)
+        hidden[1, :, n] = (grad_hidden * acts[1, :, n].astype(F32)).astype(BF16)
+    arrived(0), arrived(1)
     for n in tiles(down_w.shape[1], 512):
         total = lax.dot_general(hidden[0], gate_w[n, :], PAIRS, preferred_element_type=F32)
         total = total + lax.dot_general(hidden[1], up_w[n, :], PAIRS, preferred_element_type=F32)
-        rows[e, :, n] = (total * factor[e][:, :1]).astype(BF16)
+        rows[e, :, n] = (total * factor[e, :, :1]).astype(BF16)
 
 
 def experts_kernel(forward, cap, groups, index_ref, *refs):
@@ -104,40 +105,42 @@
         outs, kept, scratch = rest[:count], rest[count], rest[count + 1 :]
     else:
         kept, outs, scratch = rest[0], rest[1 : 1 + count], rest[1 + count :]
-    buffer, rows, onehot, factor, ranks, sides, downs, acts, hidden, in_sem, weight_sem, act_sem = scratch
+    buffer, rows, onehot, factor, ranks, gates, ups, downs, acts, hidden, in_sem, weight_sem, act_sem = scratch
     tok = onehot.shape[2]
     blocks = sum(len(g) for g in groups)
+    held = (gates, ups, downs)
 
     def window(i):
         return buffer.at[groups[i][0] * tok : (groups[i][-1] + 1) * tok]
 
+    def weight_copy(e, i, source=None):
+        slot = held[i].at[e]
+        return pltpu.make_async_copy(slot if source is None else source, slot, weight_sem.at[3 * e + i])
+
+    def act_copy(e):
+        ends = (acts.at[e], kept.at[e]) if forward else (kept.at[e], acts.at[e])
+        return pltpu.make_async_copy(*ends, act_sem.at[e])
+
     copies_in = [pltpu.make_async_copy(ins[i], window(i), in_sem.at[i]) for i in range(count)]
-    held = {}
-    for e in range(2):
-        held["gate", e] = pltpu.make_async_copy(weights[3 * e], sides.at[2 * e], weight_sem.at[3 * e])
-        held["up", e] = pltpu.make_async_copy(weights[3 * e + 1], sides.at[2 * e + 1], weight_sem.at[3 * e + 1])
-        held["down", e] = pltpu.make_async_copy(weights[3 * e + 2], downs.at[e], weight_sem.at[3 * e + 2])
-    if forward:
-        copies_act = [pltpu.make_async_copy(acts.at[e], kept.at[e], act_sem.at[e]) for e in range(2)]
-    else:
-        copies_act = [pltpu.make_async_copy(kept.at[e], acts.at[e], act_sem.at[e]) for e in range(2)]
     for copy in copies_in:
         copy.start()
     for e in range(2):
-        for name in ("gate", "up", "down") if forward else ("down", "gate", "up"):
-            held[name, e].start()
+        for i in (0, 1, 2) if forward else (2, 0, 1):
+            weight_copy(e, i, weights[3 * e + i]).start()
         if not forward:
-            copies_act[e].start()
+            act_copy(e).start()
     slot_tables(index_ref, table_ref, onehot, factor, ranks, blocks, cap)
     for copy, group in zip(copies_in, groups):
         copy.wait()
         pick_rows(buffer, onehot, rows, group, cap)
-    for e in range(2):
+
+    @pl.loop(0, 2)
+    def _(e):
         (forward_expert if forward else backward_expert)(
-            e, rows, factor, sides.at[2 * e], sides.at[2 * e + 1], downs.at[e],
-            lambda name, e: held[name, e].wait(), acts.at[e],
-            lambda e: copies_act[e].start() if forward else copies_act[e].wait(), hidden,
+            e, rows, factor, gates.at[e], ups.at[e], downs.at[e],
+            lambda i: weight_copy(e, i).wait(), acts.at[e], act_copy(e), hidden,
         )
+
     copies_out = [pltpu.make_async_copy(window(i), outs[i], in_sem.at[i]) for i in range(count)]
     for copy, group in zip(copies_out, groups):
         put_rows(buffer, onehot, rows, group, cap)
@@ -145,8 +148,8 @@
     for copy in copies_out:
         copy.wait()
     if forward:
-        for copy in copies_act:
-            copy.wait()
+        for e in range(2):
+            act_copy(e).wait()
 
 
 def run_experts(forward, index, table, ins, weights, acts, cap):
@@ -156,7 +159,7 @@
         groups.append(list(range(blocks, blocks + value.shape[0] // tok)))
         blocks += value.shape[0] // tok
     slots = blocks * cap
-    kept = jax.ShapeDtypeStruct((2, 2, slots, ff), F32)
+    kept = jax.ShapeDtypeStruct((2, 2, slots, ff), BF16)
     out_shape = [jax.ShapeDtypeStruct(value.shape, BF16) for value in ins] + ([kept] if forward else [])
     in_place = pl.BlockSpec(memory_space=pl.ANY)
     operands = [index, table, *ins, *weights] + ([] if forward else [acts])
@@ -172,9 +175,10 @@
             pltpu.VMEM((blocks, 2 * cap, tok), BF16),
             pltpu.VMEM((2, slots, tok), F32),
             pltpu.VMEM((2 * blocks, tok), F32),
-            pltpu.VMEM((4, width, ff), BF16),
+            pltpu.VMEM((2, width, ff), BF16),
+            pltpu.VMEM((2, width, ff), BF16),
             pltpu.VMEM((2, ff, width), BF16),
-            pltpu.VMEM((2, 2, slots, ff), F32),
+            pltpu.VMEM((2, 2, slots, ff), BF16),
             pltpu.VMEM((1 if forward else 2, slots, ff), BF16),
             pltpu.SemaphoreType.DMA((len(ins),)),
             pltpu.SemaphoreType.DMA((6,)),
@@ -183,7 +187,7 @@
         compiler_params=pltpu.CompilerParams(vmem_limit_bytes=58 << 20),
         cost_estimate=pl.CostEstimate(
             flops=2 * 2 * 3 * slots * width * ff,
-            bytes_accessed=2 * (6 * width * ff + 2 * blocks * tok * width) + 16 * slots * ff,
+            bytes_accessed=2 * (6 * width * ff + 2 * blocks * tok * width) + 8 * slots * ff,
             transcendentals=2 * slots * ff,
         ),
     )(*operands)

time: 335 us -> 333 us (level)
  transfers between devices with their start and end apart: 48 -> 48, of which waited for: 25 -> 24; matrix products, arithmetic and copies ran while one was open for 3% -> 3% of each run, Pallas kernels for 18% -> 18%
where the time goes in v4:
time: 333 us; the launch traced here: 332 us
  waiting for transfers between devices  182 us (55%)
  starting transfers between devices  74.7 us (22%)
  Pallas kernels  58.7 us (18%)
  other arithmetic  12.4 us (4%)
    ppermute x31, waiting for transfers between devices, ep_permute(): return lax.ppermute(value, 'ep', [(i, partner(i)) for i in range(8)])  128 us
    pallas_call x2, Pallas kernels, run_experts(): pl.pallas_call(functools.partial(experts_kernel, forward, cap, groups), o...  58.7 us
    ppermute x16, waiting for transfers between devices, along_z(): return lax.ppermute(value, 'seq', [(i, i ^ k) for i in range(4)])  54.5 us
    ppermute x31, starting transfers between devices, ep_permute(): return lax.ppermute(value, 'ep', [(i, partner(i)) for i in range(8)])  40.9 us
    ppermute x16, starting transfers between devices, along_z(): return lax.ppermute(value, 'seq', [(i, i ^ k) for i in range(4)])  29.8 us
  transfers between devices with their start and end apart: 48, of which 24 were waited for; matrix products, arithmetic and copies ran while one was open for 3% of the time, Pallas kernels for 18%

profile of v4, /device:TPU:0, one launch (start us, length us, event | category | flops | bytes accessed | tf_op | source)
XLA Modules:
  0.0 332.2 jit_solution(8055800104401624986)
XLA Ops:
  6.3 7.1 %collective-permute-done.2.refs_2_ = bf16[128,2048]{1,0:T(8,128)(2,1)S(1)} collective-permute-done((bf16[128,2048]{1,0:T(8,128)(2,1)S(1)}, bf16[128,2048]{1,0:T(8,128)(2,1)S(1)}, u32[]{:S(2)}, u32[]{:S(2)}) %collective-permute-start.2) | collective-permute-done | bytes 524320 | tf_op jit(solution)/shard_map/x0a/ppermute | solution.py:197
  13.4 5.6 %collective-permute-done.3.refs_2_ = bf16[128,2048]{1,0:T(8,128)(2,1)S(1)} collective-permute-done((bf16[128,2048]{1,0:T(8,128)(2,1)}, bf16[128,2048]{1,0:T(8,128)(2,1)S(1)}, u32[]{:S(2)}, u32[]{:S(2)}) %collective-permute-start.3) | collective-permute-done | bytes 524320 | tf_op jit(solution)/shard_map/g0a/ppermute | solution.py:197
  19.1 5.9 %collective-permute-done.4.refs_18_ = bf16[768,2048]{1,0:T(8,128)(2,1)S(1)} collective-permute-done((bf16[768,2048]{1,0:T(8,128)(2,1)}, bf16[768,2048]{1,0:T(8,128)(2,1)S(1)}, u32[]{:S(2)}, u32[]{:S(2)}) %collective-permute-start.4) | collective-permute-done | bytes 3145760 | tf_op jit(solution)/shard_map/w2/ppermute | solution.py:197
  32.2 18.6 %collective-permute-done.8.refs_4_ = bf16[128,2048]{1,0:T(8,128)(2,1)S(1)} collective-permute-done((bf16[128,2048]{1,0:T(8,128)(2,1)S(1)}, bf16[128,2048]{1,0:T(8,128)(2,1)S(1)}, u32[]{:S(2)}, u32[]{:S(2)}) %collective-permute-start.8) | collective-permute-done | bytes 524320 | tf_op jit(solution)/shard_map/x1z/ppermute | solution.py:209
  56.2 9.3 %collective-permute-done.5.refs_10_ = bf16[128,2048]{1,0:T(8,128)(2,1)S(1)} collective-permute-done((bf16[128,2048]{1,0:T(8,128)(2,1)S(1)}, bf16[128,2048]{1,0:T(8,128)(2,1)S(1)}, u32[]{:S(2)}, u32[]{:S(2)}) %collective-permute-start.5) | collective-permute-done | bytes 524320 | tf_op jit(solution)/shard_map/x3z/ppermute | solution.py:209
  79.6 12.7 %collective-permute-done.9.refs_7_ = bf16[128,2048]{1,0:T(8,128)(2,1)S(1)} collective-permute-done((bf16[128,2048]{1,0:T(8,128)(2,1)S(1)}, bf16[128,2048]{1,0:T(8,128)(2,1)S(1)}, u32[]{:S(2)}, u32[]{:S(2)}) %collective-permute-start.9) | collective-permute-done | bytes 524320 | tf_op jit(solution)/shard_map/g2z/ppermute | solution.py:209
  95.3 4.1 %all-to-all-start = ((f32[32,1,256]{2,1,0:T(1,128)}), f32[32,1,256]{2,1,0:T(1,128)S(1)}, u32[]{:S(2)}, u32[]{:S(2)}) async-start(f32[32,1,256]{2,1,0:T(1,128)} %all_to_all.6), calls=%async_computation | async-start | bytes 65536 | tf_op jit(solution)/shard_map/tab/all_to_all | solution.py:327
  109.0 29.0 %F.1 = (bf16[128,2048]{1,0:T(8,128)(2,1)}, bf16[128,2048]{1,0:T(8,128)(2,1)}, bf16[256,2048]{1,0:T(8,128)(2,1)}, bf16[128,2048]{1,0:T(8,128)(2,1)}, bf16[128,204...) custom-call(s32[16]{0:T(128)} %stack.90.index_ref, ...), custom_call_target="tpu_custom_call" | custom-call | flops 14495514624 | bytes 40370176 | tf_op jit(solution)/shard_map/F/pallas_call | solution.py:166
  143.5 9.5 %collective-permute-done.25.refs_11_ = bf16[128,2048]{1,0:T(8,128)(2,1)S(1)} collective-permute-done((bf16[128,2048]{1,0:T(8,128)(2,1)}, bf16[128,2048]{1,0:T(8,128)(2,1)S(1)}, u32[]{:S(2)}, u32[]{:S(2)}) %collective-permute-start.25) | collective-permute-done | bytes 524320 | tf_op jit(solution)/shard_map/g3a/ppermute | solution.py:197
  153.0 11.0 %collective-permute-done.22 = bf16[128,2048]{1,0:T(8,128)(2,1)S(1)} collective-permute-done((bf16[128,2048]{1,0:T(8,128)(2,1)}, bf16[128,2048]{1,0:T(8,128)(2,1)S(1)}, u32[]{:S(2)}, u32[]{:S(2)}) %collective-permute-start.22) | collective-permute-done | bytes 524320 | tf_op jit(solution)/shard_map/o1a/ppermute | solution.py:197
  170.9 6.2 %collective-permute-done.23 = bf16[128,2048]{1,0:T(8,128)(2,1)S(1)} collective-permute-done((bf16[128,2048]{1,0:T(8,128)(2,1)S(1)}, bf16[128,2048]{1,0:T(8,128)(2,1)S(1)}, u32[]{:S(2)}, u32[]{:S(2)}) %collective-permute-start.23) | collective-permute-done | bytes 524320 | tf_op jit(solution)/shard_map/o1z/ppermute | solution.py:209
  179.1 4.5 %collective-permute-done.27 = bf16[128,2048]{1,0:T(8,128)(2,1)S(1)} collective-permute-done((bf16[128,2048]{1,0:T(8,128)(2,1)S(1)}, bf16[128,2048]{1,0:T(8,128)(2,1)S(1)}, u32[]{:S(2)}, u32[]{:S(2)}) %collective-permute-start.27) | collective-permute-done | bytes 524320 | tf_op jit(solution)/shard_map/o3a/ppermute | solution.py:197
  183.9 5.0 %collective-permute-done.29.refs_12_ = bf16[256,2048]{1,0:T(8,128)(2,1)} collective-permute-done((bf16[256,2048]{1,0:T(8,128)(2,1)S(1)}, bf16[256,2048]{1,0:T(8,128)(2,1)}, u32[]{:S(2)}, u32[]{:S(2)}) %collective-permute-start.29) | collective-permute-done | bytes 1048608 | tf_op jit(solution)/shard_map/g3b/ppermute | solution.py:197
  189.0 5.9 %collective-permute-done.28.refs_5_ = bf16[128,2048]{1,0:T(8,128)(2,1)S(1)} collective-permute-done((bf16[128,2048]{1,0:T(8,128)(2,1)}, bf16[128,2048]{1,0:T(8,128)(2,1)S(1)}, u32[]{:S(2)}, u32[]{:S(2)}) %collective-permute-start.28) | collective-permute-done | bytes 524320 | tf_op jit(solution)/shard_map/g1a/ppermute | solution.py:197
  195.7 29.8 %B.1 = (bf16[128,2048]{1,0:T(8,128)(2,1)}, bf16[128,2048]{1,0:T(8,128)(2,1)}, bf16[256,2048]{1,0:T(8,128)(2,1)}, bf16[128,2048]{1,0:T(8,128)(2,1)}, bf16[128,204...) custom-call(s32[16]{0:T(128)} %stack.90.index_ref, ...), custom_call_target="tpu_custom_call" | custom-call | flops 14495514624 | bytes 40370176 | tf_op jit(solution)/shard_map/B/pallas_call | solution.py:166
  230.5 10.4 %collective-permute-done.35 = bf16[128,2048]{1,0:T(8,128)(2,1)S(1)} collective-permute-done((bf16[128,2048]{1,0:T(8,128)(2,1)S(1)}, bf16[128,2048]{1,0:T(8,128)(2,1)S(1)}, u32[]{:S(2)}, u32[]{:S(2)}) %collective-permute-start.35) | collective-permute-done | bytes 524320 | tf_op jit(solution)/shard_map/o2a/ppermute | solution.py:197
  243.7 10.7 %collective-permute-done.33 = bf16[256,2048]{1,0:T(8,128)(2,1)S(1)} collective-permute-done((bf16[256,2048]{1,0:T(8,128)(2,1)}, bf16[256,2048]{1,0:T(8,128)(2,1)S(1)}, u32[]{:S(2)}, u32[]{:S(2)}) %collective-permute-start.33) | collective-permute-done | bytes 1048608 | tf_op jit(solution)/shard_map/d2b/ppermute | solution.py:197
  258.7 15.9 %collective-permute-done.37 = bf16[128,2048]{1,0:T(8,128)(2,1)S(1)} collective-permute-done((bf16[128,2048]{1,0:T(8,128)(2,1)S(1)}, bf16[128,2048]{1,0:T(8,128)(2,1)S(1)}, u32[]{:S(2)}, u32[]{:S(2)}) %collective-permute-start.37) | collective-permute-done | bytes 524320 | tf_op jit(solution)/shard_map/d3a/ppermute | solution.py:197
  277.4 5.6 %collective-permute-start.41 = (bf16[128,2048]{1,0:T(8,128)(2,1)S(1)}, bf16[128,2048]{1,0:T(8,128)(2,1)S(1)}, u32[]{:S(2)}, u32[]{:S(2)}) collective-permute-start(bf16[128,2048]{1,0:T(8,128)(2,1)S(1)} %add_convert_fusion.7), channel_id=1, source_target_pairs={{0,8},{8,0},{16,24},{24,16},{1,9},{9,1},{17,25},{25,17},{2,10},{10... | collective-permute-start | bytes 1572872 | tf_op jit(solution)/shard_map/d3z/ppermute | solution.py:209
  285.5 4.7 %collective-permute-done.42 = bf16[128,2048]{1,0:T(8,128)(2,1)S(1)} collective-permute-done((bf16[128,2048]{1,0:T(8,128)(2,1)S(1)}, bf16[128,2048]{1,0:T(8,128)(2,1)S(1)}, u32[]{:S(2)}, u32[]{:S(2)}) %collective-permute-start.42) | collective-permute-done | bytes 524320 | tf_op jit(solution)/shard_map/d2a/ppermute | solution.py:197
  292.3 5.8 %collective-permute-start.45 = (bf16[128,2048]{1,0:T(8,128)(2,1)S(1)}, bf16[128,2048]{1,0:T(8,128)(2,1)S(1)}, u32[]{:S(2)}, u32[]{:S(2)}) collective-permute-start(bf16[128,2048]{1,0:T(8,128)(2,1)S(1)} %add_convert_fusion.3), channel_id=1, source_target_pairs={{0,8},{8,0},{16,24},{24,16},{1,9},{9,1},{17,25},{25,17},{2,10},{10... | collective-permute-start | bytes 1572872 | tf_op jit(solution)/shard_map/d1z/ppermute | solution.py:209
  298.2 6.6 %collective-permute-done.40 = bf16[256,2048]{1,0:T(8,128)(2,1)S(1)} collective-permute-done((bf16[256,2048]{1,0:T(8,128)(2,1)S(1)}, bf16[256,2048]{1,0:T(8,128)(2,1)S(1)}, u32[]{:S(2)}, u32[]{:S(2)}) %collective-permute-start.40) | collective-permute-done | bytes 1048608 | tf_op jit(solution)/shard_map/d0b/ppermute | solution.py:197
  306.8 13.3 %collective-permute-done.39 = bf16[256,2048]{1,0:T(8,128)(2,1)S(1)} collective-permute-done((bf16[256,2048]{1,0:T(8,128)(2,1)S(1)}, bf16[256,2048]{1,0:T(8,128)(2,1)S(1)}, u32[]{:S(2)}, u32[]{:S(2)}) %collective-permute-start.39) | collective-permute-done | bytes 1048608 | tf_op jit(solution)/shard_map/o0b/ppermute | solution.py:197
  323.0 6.6 %collective-permute-done.43 = bf16[128,2048]{1,0:T(8,128)(2,1)S(1)} collective-permute-done((bf16[128,2048]{1,0:T(8,128)(2,1)S(1)}, bf16[128,2048]{1,0:T(8,128)(2,1)S(1)}, u32[]{:S(2)}, u32[]{:S(2)}) %collective-permute-start.43) | collective-permute-done | bytes 524320 | tf_op jit(solution)/shard_map/o0a/ppermute | solution.py:197
  (188 shorter events, 87.3 us)
Async XLA Ops:
  25.0 30.6 %collective-permute-start.7 = (bf16[2048,768]{1,0:T(8,128)(2,1)}, bf16[2048,768]{1,0:T(8,128)(2,1)}, u32[]{:S(2)}, u32[]{:S(2)}) collective-permute-start(bf16[2048,768]{1,0:T(8,128)(2,1)} %bitcast.41), channel_id=1, source_target_pairs={{0,1},{1,0},{2,3},{3,2},{4,5},{5,4},{6,7},{7,6},{8,9},{9,8},{10,11... | collective-permute-start | bytes 9437192 | tf_op jit(solution)/shard_map/w1/ppermute | solution.py:197
  25.1 25.7 %collective-permute-start.8 = (bf16[128,2048]{1,0:T(8,128)(2,1)S(1)}, bf16[128,2048]{1,0:T(8,128)(2,1)S(1)}, u32[]{:S(2)}, u32[]{:S(2)}) collective-permute-start(bf16[128,2048]{1,0:T(8,128)(2,1)S(1)} %fusion.3.refs_1_), channel_id=1, source_target_pairs={{0,8},{8,0},{16,24},{24,16},{1,9},{9,1},{17,25},{25,17},{2,10},{10... | collective-permute-start | bytes 1572872 | tf_op jit(solution)/shard_map/x1z/ppermute | solution.py:209
  27.2 26.1 %collective-permute-start = (bf16[128,2048]{1,0:T(8,128)(2,1)S(1)}, bf16[128,2048]{1,0:T(8,128)(2,1)S(1)}, u32[]{:S(2)}, u32[]{:S(2)}) collective-permute-start(bf16[128,2048]{1,0:T(8,128)(2,1)S(1)} %fusion.3.refs_1_), channel_id=1, source_target_pairs={{0,16},{8,24},{16,0},{24,8},{1,17},{9,25},{17,1},{25,9},{2,18},{10... | collective-permute-start | bytes 1572872 | tf_op jit(solution)/shard_map/x2z/ppermute | solution.py:209
  29.9 26.2 %collective-permute-start.6 = (bf16[256,2048]{1,0:T(8,128)(2,1)S(1)}, bf16[256,2048]{1,0:T(8,128)(2,1)}, u32[]{:S(2)}, u32[]{:S(2)}) collective-permute-start(bf16[256,2048]{1,0:T(8,128)(2,1)S(1)} %pad_maximum_fusion), channel_id=1, source_target_pairs={{0,4},{1,3},{2,6},{3,1},{4,0},{5,7},{6,2},{7,5},{8,12},{9,11},{10,... | collective-permute-start | bytes 3145736 | tf_op jit(solution)/shard_map/x0b/ppermute | solution.py:197
  31.6 24.6 %collective-permute-start.11 = (bf16[256,2048]{1,0:T(8,128)(2,1)S(1)}, bf16[256,2048]{1,0:T(8,128)(2,1)S(1)}, u32[]{:S(2)}, u32[]{:S(2)}) collective-permute-start(bf16[256,2048]{1,0:T(8,128)(2,1)S(1)} %pad_maximum_fusion.1), channel_id=1, source_target_pairs={{0,4},{1,3},{2,6},{3,1},{4,0},{5,7},{6,2},{7,5},{8,12},{9,11},{10,... | collective-permute-start | bytes 3145736 | tf_op jit(solution)/shard_map/g0b/ppermute | solution.py:197
  67.1 25.2 %collective-permute-start.9 = (bf16[128,2048]{1,0:T(8,128)(2,1)S(1)}, bf16[128,2048]{1,0:T(8,128)(2,1)S(1)}, u32[]{:S(2)}, u32[]{:S(2)}) collective-permute-start(bf16[128,2048]{1,0:T(8,128)(2,1)S(1)} %copy-done.14), channel_id=1, source_target_pairs={{0,16},{8,24},{16,0},{24,8},{1,17},{9,25},{17,1},{25,9},{2,18},{10... | collective-permute-start | bytes 1572872 | tf_op jit(solution)/shard_map/g2z/ppermute | solution.py:209
  70.5 36.0 %collective-permute-start.15 = (bf16[256,2048]{1,0:T(8,128)(2,1)}, bf16[256,2048]{1,0:T(8,128)(2,1)}, u32[]{:S(2)}, u32[]{:S(2)}) collective-permute-start(bf16[256,2048]{1,0:T(8,128)(2,1)} %collective-permute-done.6.refs_3_), channel_id=1, source_target_pairs={{0,8},{8,0},{16,24},{24,16},{1,9},{9,1},{17,25},{25,17},{2,10},{10... | collective-permute-start | bytes 3145736 | tf_op jit(solution)/shard_map/x1b/ppermute | solution.py:209
  72.3 34.1 %collective-permute-start.16 = (bf16[256,2048]{1,0:T(8,128)(2,1)S(1)}, bf16[256,2048]{1,0:T(8,128)(2,1)}, u32[]{:S(2)}, u32[]{:S(2)}) collective-permute-start(bf16[256,2048]{1,0:T(8,128)(2,1)S(1)} %pad_maximum_fusion.2), channel_id=1, source_target_pairs={{0,4},{1,3},{2,6},{3,1},{4,0},{5,7},{6,2},{7,5},{8,12},{9,11},{10,... | collective-permute-start | bytes 3145736 | tf_op jit(solution)/shard_map/x2b/ppermute | solution.py:197
  77.0 31.4 %collective-permute-start.17 = (bf16[256,2048]{1,0:T(8,128)(2,1)S(1)}, bf16[256,2048]{1,0:T(8,128)(2,1)}, u32[]{:S(2)}, u32[]{:S(2)}) collective-permute-start(bf16[256,2048]{1,0:T(8,128)(2,1)S(1)} %pad_maximum_fusion.3), channel_id=1, source_target_pairs={{0,4},{1,3},{2,6},{3,1},{4,0},{5,7},{6,2},{7,5},{8,12},{9,11},{10,... | collective-permute-start | bytes 3145736 | tf_op jit(solution)/shard_map/x3b/ppermute | solution.py:197
  99.4 38.6 %collective-permute-start.20 = (bf16[128,2048]{1,0:T(8,128)(2,1)S(1)}, bf16[128,2048]{1,0:T(8,128)(2,1)}, u32[]{:S(2)}, u32[]{:S(2)}) collective-permute-start(bf16[128,2048]{1,0:T(8,128)(2,1)S(1)} %collective-permute-done.9.refs_7_), channel_id=1, source_target_pairs={{0,8},{8,0},{16,24},{24,16},{1,9},{9,1},{17,25},{25,17},{2,10},{10... | collective-permute-start | bytes 1572872 | tf_op jit(solution)/shard_map/g3z/ppermute | solution.py:209
  106.4 31.6 %collective-permute-start.18 = (bf16[128,2048]{1,0:T(8,128)(2,1)S(1)}, bf16[128,2048]{1,0:T(8,128)(2,1)}, u32[]{:S(2)}, u32[]{:S(2)}) collective-permute-start(bf16[128,2048]{1,0:T(8,128)(2,1)S(1)} %copy-done.14), channel_id=1, source_target_pairs={{0,8},{8,0},{16,24},{24,16},{1,9},{9,1},{17,25},{25,17},{2,10},{10... | collective-permute-start | bytes 1572872 | tf_op jit(solution)/shard_map/g1z/ppermute | solution.py:209
  108.3 29.7 %collective-permute-start.19 = (bf16[256,2048]{1,0:T(8,128)(2,1)S(1)}, bf16[256,2048]{1,0:T(8,128)(2,1)}, u32[]{:S(2)}, u32[]{:S(2)}) collective-permute-start(bf16[256,2048]{1,0:T(8,128)(2,1)S(1)} %pad_maximum_fusion.4), channel_id=1, source_target_pairs={{0,4},{1,3},{2,6},{3,1},{4,0},{5,7},{6,2},{7,5},{8,12},{9,11},{10,... | collective-permute-start | bytes 3145736 | tf_op jit(solution)/shard_map/g2b/ppermute | solution.py:197
  139.4 24.5 %collective-permute-start.22 = (bf16[128,2048]{1,0:T(8,128)(2,1)}, bf16[128,2048]{1,0:T(8,128)(2,1)S(1)}, u32[]{:S(2)}, u32[]{:S(2)}) collective-permute-start(bf16[128,2048]{1,0:T(8,128)(2,1)} %get-tuple-element.93), channel_id=1, source_target_pairs={{0,2},{1,5},{2,0},{3,7},{4,6},{5,1},{6,4},{7,3},{8,10},{9,13},{10,... | collective-permute-start | bytes 1572872 | tf_op jit(solution)/shard_map/o1a/ppermute | solution.py:197
  140.1 28.5 %collective-permute-start.24 = (bf16[256,2048]{1,0:T(8,128)(2,1)}, bf16[256,2048]{1,0:T(8,128)(2,1)S(1)}, u32[]{:S(2)}, u32[]{:S(2)}) collective-permute-start(bf16[256,2048]{1,0:T(8,128)(2,1)} %get-tuple-element.95), channel_id=1, source_target_pairs={{0,4},{1,3},{2,6},{3,1},{4,0},{5,7},{6,2},{7,5},{8,12},{9,11},{10,... | collective-permute-start | bytes 3145736 | tf_op jit(solution)/shard_map/o3b/ppermute | solution.py:197
  142.1 34.9 %collective-permute-start.21 = (bf16[256,2048]{1,0:T(8,128)(2,1)S(1)}, bf16[256,2048]{1,0:T(8,128)(2,1)S(1)}, u32[]{:S(2)}, u32[]{:S(2)}) collective-permute-start(bf16[256,2048]{1,0:T(8,128)(2,1)S(1)} %copy-done.33), channel_id=1, source_target_pairs={{0,8},{8,0},{16,24},{24,16},{1,9},{9,1},{17,25},{25,17},{2,10},{10... | collective-permute-start | bytes 3145736 | tf_op jit(solution)/shard_map/g1b/ppermute | solution.py:209
  177.0 48.4 %collective-permute-start.26 = (bf16[256,2048]{1,0:T(8,128)(2,1)}, bf16[256,2048]{1,0:T(8,128)(2,1)S(1)}, u32[]{:S(2)}, u32[]{:S(2)}) collective-permute-start(bf16[256,2048]{1,0:T(8,128)(2,1)} %get-tuple-element.97), channel_id=1, source_target_pairs={{0,8},{8,0},{16,24},{24,16},{1,9},{9,1},{17,25},{25,17},{2,10},{10... | collective-permute-start | bytes 3145736 | tf_op jit(solution)/shard_map/o1b/ppermute | solution.py:209
  177.6 47.9 %collective-permute-start.31 = (bf16[256,2048]{1,0:T(8,128)(2,1)S(1)}, bf16[256,2048]{1,0:T(8,128)(2,1)S(1)}, u32[]{:S(2)}, u32[]{:S(2)}) collective-permute-start(bf16[256,2048]{1,0:T(8,128)(2,1)S(1)} %copy-done.34), channel_id=1, source_target_pairs={{0,4},{1,3},{2,6},{3,1},{4,0},{5,7},{6,2},{7,5},{8,12},{9,11},{10,... | collective-permute-start | bytes 3145736 | tf_op jit(solution)/shard_map/o2b/ppermute | solution.py:197
  189.0 36.5 %collective-permute-start.30 = (bf16[128,2048]{1,0:T(8,128)(2,1)S(1)}, bf16[128,2048]{1,0:T(8,128)(2,1)S(1)}, u32[]{:S(2)}, u32[]{:S(2)}) collective-permute-start(bf16[128,2048]{1,0:T(8,128)(2,1)S(1)} %add_convert_fusion.12), channel_id=1, source_target_pairs={{0,8},{8,0},{16,24},{24,16},{1,9},{9,1},{17,25},{25,17},{2,10},{10... | collective-permute-start | bytes 1572872 | tf_op jit(solution)/shard_map/o3z/ppermute | solution.py:209
  227.8 26.6 %collective-permute-start.33 = (bf16[256,2048]{1,0:T(8,128)(2,1)}, bf16[256,2048]{1,0:T(8,128)(2,1)S(1)}, u32[]{:S(2)}, u32[]{:S(2)}) collective-permute-start(bf16[256,2048]{1,0:T(8,128)(2,1)} %get-tuple-element.112), channel_id=1, source_target_pairs={{0,4},{1,3},{2,6},{3,1},{4,0},{5,7},{6,2},{7,5},{8,12},{9,11},{10,... | collective-permute-start | bytes 3145736 | tf_op jit(solution)/shard_map/d2b/ppermute | solution.py:197
  229.8 28.3 %collective-permute-start.32 = (bf16[256,2048]{1,0:T(8,128)(2,1)}, bf16[256,2048]{1,0:T(8,128)(2,1)S(1)}, u32[]{:S(2)}, u32[]{:S(2)}) collective-permute-start(bf16[256,2048]{1,0:T(8,128)(2,1)} %get-tuple-element.109), channel_id=1, source_target_pairs={{0,8},{8,0},{16,24},{24,16},{1,9},{9,1},{17,25},{25,17},{2,10},{10... | collective-permute-start | bytes 3145736 | tf_op jit(solution)/shard_map/d1b/ppermute | solution.py:209
  241.3 33.5 %collective-permute-start.38 = (bf16[128,2048]{1,0:T(8,128)(2,1)S(1)}, bf16[128,2048]{1,0:T(8,128)(2,1)S(1)}, u32[]{:S(2)}, u32[]{:S(2)}) collective-permute-start(bf16[128,2048]{1,0:T(8,128)(2,1)S(1)} %add_convert_fusion.9), channel_id=1, source_target_pairs={{0,16},{8,24},{16,0},{24,8},{1,17},{9,25},{17,1},{25,9},{2,18},{10... | collective-permute-start | bytes 1572872 | tf_op jit(solution)/shard_map/o2z/ppermute | solution.py:209
  283.3 36.9 %collective-permute-start.39 = (bf16[256,2048]{1,0:T(8,128)(2,1)S(1)}, bf16[256,2048]{1,0:T(8,128)(2,1)S(1)}, u32[]{:S(2)}, u32[]{:S(2)}) collective-permute-start(bf16[256,2048]{1,0:T(8,128)(2,1)S(1)} %add_convert_fusion.1), channel_id=1, source_target_pairs={{0,4},{1,3},{2,6},{3,1},{4,0},{5,7},{6,2},{7,5},{8,12},{9,11},{10,... | collective-permute-start | bytes 3145736 | tf_op jit(solution)/shard_map/o0b/ppermute | solution.py:197
  292.3 30.0 %collective-permute-start.45 = (bf16[128,2048]{1,0:T(8,128)(2,1)S(1)}, bf16[128,2048]{1,0:T(8,128)(2,1)S(1)}, u32[]{:S(2)}, u32[]{:S(2)}) collective-permute-start(bf16[128,2048]{1,0:T(8,128)(2,1)S(1)} %add_convert_fusion.3), channel_id=1, source_target_pairs={{0,8},{8,0},{16,24},{24,16},{1,9},{9,1},{17,25},{25,17},{2,10},{10... | collective-permute-start | bytes 1572872 | tf_op jit(solution)/shard_map/d1z/ppermute | solution.py:209
  298.2 24.2 %collective-permute-start.46 = (bf16[128,2048]{1,0:T(8,128)(2,1)S(1)}, bf16[128,2048]{1,0:T(8,128)(2,1)S(1)}, u32[]{:S(2)}, u32[]{:S(2)}) collective-permute-start(bf16[128,2048]{1,0:T(8,128)(2,1)S(1)} %add_convert_fusion.2), channel_id=1, source_target_pairs={{0,16},{8,24},{16,0},{24,8},{1,17},{9,25},{17,1},{25,9},{2,18},{10... | collective-permute-start | bytes 1572872 | tf_op jit(solution)/shard_map/d2z/ppermute | solution.py:209
  (64 other events, 1276.1 us)

commit v5 on v4

--- a/solution.py
+++ b/solution.py
@@ -227,11 +227,8 @@
     ("o3b", ("g1z", "g2b", "g3z",)), ("g1b", ("F", "g1z", "g2b", "g3z",)), ("o1z", ()), ("g3b", ("o1a",)),
     ("o3a", ("g3a", "o1a",)), ("g1a", ("o3b", "g3a", "o1a",)), ("o2b", ("o1z", "o3b", "g3a",)),
     ("o1b", ("g1b", "o1z", "o3b", "g3a",)), ("o3z", ("g3b", "g1b", "o1z",)), ("B", ("o3a", "o1z",)),
-    ("o2a", ("B", "o1b", "o3z",)), ("d3b", ("o1b", "o3z", "o2b",)), ("d2b", ("o1b", "o3z", "o2b",)),
-    ("d1b", ("o1b", "o3z", "o2b",)), ("o2z", ()), ("d3a", ("o2a",)), ("d1a", ("d2b", "d3b", "o2a",)),
-    ("d2a", ("d3a", "o2z",)), ("d3z", ("o2z", "d2b",)), ("d0b", ("d1a", "d3a", "o2z",)),
-    ("o0b", ("d1b", "d1a", "d3a", "o2z",)), ("d2z", ("d1b", "d1a",)), ("d1z", ("d3z", "d2a", "d1b",)),
-    ("d0a", ("d3z", "d2a",)), ("o0a", ("d0b", "d3z", "d2a",)),
+    ("o2a", ("B",)), ("d3b", ()), ("d2b", ()), ("d1b", ()), ("o2z", ()), ("d3a", ()), ("d1a", ()), ("d2a", ()),
+    ("d3z", ()), ("d0b", ()), ("o0b", ()), ("d2z", ()), ("d1z", ()), ("d0a", ()), ("o0a", ()),
 )
 
 

time: 333 us -> 328 us (0.985)
  starting transfers between devices: 74.7 us -> 62.3 us
  waiting for transfers between devices: 182 us -> 190 us
    ppermute x16, waiting for transfers between devices: 54.5 us -> 75.9 us  [along_z(): return lax.ppermute(value, 'seq', [(i, i ^ k) for i in range(4)])]
    ppermute x31, waiting for transfers between devices: 128 us -> 114 us  [ep_permute(): return lax.ppermute(value, 'ep', [(i, partner(i)) for i in range(8)])]
    ppermute x31, starting transfers between devices: 40.9 us -> 32.4 us  [ep_permute(): return lax.ppermute(value, 'ep', [(i, partner(i)) for i in range(8)])]
    ppermute x16, starting transfers between devices: 29.8 us -> 25.7 us  [along_z(): return lax.ppermute(value, 'seq', [(i, i ^ k) for i in range(4)])]
where the time goes in v5:
time: 328 us
  waiting for transfers between devices  190 us (58%)
  starting transfers between devices  62.3 us (19%)
  Pallas kernels  58.3 us (18%)
  other arithmetic  11.3 us (3%)
  local copies, waits for them, and re-layouts  4.74 us (1%)
    ppermute x31, waiting for transfers between devices, ep_permute(): return lax.ppermute(value, 'ep', [(i, partner(i)) for i in range(8)])  114 us
    ppermute x16, waiting for transfers between devices, along_z(): return lax.ppermute(value, 'seq', [(i, i ^ k) for i in range(4)])  75.9 us
    pallas_call x2, Pallas kernels, run_experts(): pl.pallas_call(functools.partial(experts_kernel, forward, cap, groups), o...  58.3 us
    ppermute x31, starting transfers between devices, ep_permute(): return lax.ppermute(value, 'ep', [(i, partner(i)) for i in range(8)])  32.4 us
    ppermute x16, starting transfers between devices, along_z(): return lax.ppermute(value, 'seq', [(i, i ^ k) for i in range(4)])  25.7 us
  transfers between devices with their start and end apart: 48, of which 24 were waited for; matrix products, arithmetic and copies ran while one was open for 3% of the time, Pallas kernels for 18%

profile of v5, /device:TPU:0, one launch (start us, length us, event | category | flops | bytes accessed | tf_op | source)
XLA Modules:
  0.0 327.7 jit_solution(6253823729645370291)
XLA Ops:
  6.3 7.1 %collective-permute-done.2.refs_2_ = bf16[128,2048]{1,0:T(8,128)(2,1)S(1)} collective-permute-done((bf16[128,2048]{1,0:T(8,128)(2,1)S(1)}, bf16[128,2048]{1,0:T(8,128)(2,1)S(1)}, u32[]{:S(2)}, u32[]{:S(2)}) %collective-permute-start.2) | collective-permute-done | bytes 524320 | tf_op jit(solution)/shard_map/x0a/ppermute | solution.py:197
  13.4 5.6 %collective-permute-done.3.refs_2_ = bf16[128,2048]{1,0:T(8,128)(2,1)S(1)} collective-permute-done((bf16[128,2048]{1,0:T(8,128)(2,1)}, bf16[128,2048]{1,0:T(8,128)(2,1)S(1)}, u32[]{:S(2)}, u32[]{:S(2)}) %collective-permute-start.3) | collective-permute-done | bytes 524320 | tf_op jit(solution)/shard_map/g0a/ppermute | solution.py:197
  19.1 5.9 %collective-permute-done.4.refs_18_ = bf16[768,2048]{1,0:T(8,128)(2,1)S(1)} collective-permute-done((bf16[768,2048]{1,0:T(8,128)(2,1)}, bf16[768,2048]{1,0:T(8,128)(2,1)S(1)}, u32[]{:S(2)}, u32[]{:S(2)}) %collective-permute-start.4) | collective-permute-done | bytes 3145760 | tf_op jit(solution)/shard_map/w2/ppermute | solution.py:197
  32.2 18.6 %collective-permute-done.8.refs_4_ = bf16[128,2048]{1,0:T(8,128)(2,1)S(1)} collective-permute-done((bf16[128,2048]{1,0:T(8,128)(2,1)S(1)}, bf16[128,2048]{1,0:T(8,128)(2,1)S(1)}, u32[]{:S(2)}, u32[]{:S(2)}) %collective-permute-start.8) | collective-permute-done | bytes 524320 | tf_op jit(solution)/shard_map/x1z/ppermute | solution.py:209
  56.2 9.3 %collective-permute-done.5.refs_10_ = bf16[128,2048]{1,0:T(8,128)(2,1)S(1)} collective-permute-done((bf16[128,2048]{1,0:T(8,128)(2,1)S(1)}, bf16[128,2048]{1,0:T(8,128)(2,1)S(1)}, u32[]{:S(2)}, u32[]{:S(2)}) %collective-permute-start.5) | collective-permute-done | bytes 524320 | tf_op jit(solution)/shard_map/x3z/ppermute | solution.py:209
  67.9 3.4 %collective-permute-start.9 = (bf16[128,2048]{1,0:T(8,128)(2,1)S(1)}, bf16[128,2048]{1,0:T(8,128)(2,1)S(1)}, u32[]{:S(2)}, u32[]{:S(2)}) collective-permute-start(bf16[128,2048]{1,0:T(8,128)(2,1)S(1)} %copy-done.15), channel_id=1, source_target_pairs={{0,16},{8,24},{16,0},{24,8},{1,17},{9,25},{17,1},{25,9},{2,18},{10... | collective-permute-start | bytes 1572872 | tf_op jit(solution)/shard_map/g2z/ppermute | solution.py:209
  80.4 12.7 %collective-permute-done.9.refs_7_ = bf16[128,2048]{1,0:T(8,128)(2,1)S(1)} collective-permute-done((bf16[128,2048]{1,0:T(8,128)(2,1)S(1)}, bf16[128,2048]{1,0:T(8,128)(2,1)S(1)}, u32[]{:S(2)}, u32[]{:S(2)}) %collective-permute-start.9) | collective-permute-done | bytes 524320 | tf_op jit(solution)/shard_map/g2z/ppermute | solution.py:209
  96.1 4.2 %all-to-all-start = ((f32[32,1,256]{2,1,0:T(1,128)}), f32[32,1,256]{2,1,0:T(1,128)S(1)}, u32[]{:S(2)}, u32[]{:S(2)}) async-start(f32[32,1,256]{2,1,0:T(1,128)} %all_to_all.6), calls=%async_computation | async-start | bytes 65536 | tf_op jit(solution)/shard_map/tab/all_to_all | solution.py:324
  103.8 3.5 %collective-permute-done.15.refs_6_ = bf16[256,2048]{1,0:T(8,128)(2,1)} collective-permute-done((bf16[256,2048]{1,0:T(8,128)(2,1)}, bf16[256,2048]{1,0:T(8,128)(2,1)}, u32[]{:S(2)}, u32[]{:S(2)}) %collective-permute-start.15) | collective-permute-done | bytes 1048608 | tf_op jit(solution)/shard_map/x1b/ppermute | solution.py:209
  109.7 28.8 %F.1 = (bf16[128,2048]{1,0:T(8,128)(2,1)}, bf16[128,2048]{1,0:T(8,128)(2,1)}, bf16[256,2048]{1,0:T(8,128)(2,1)}, bf16[128,2048]{1,0:T(8,128)(2,1)}, bf16[128,204...) custom-call(s32[16]{0:T(128)} %stack.90.index_ref, ...), custom_call_target="tpu_custom_call" | custom-call | flops 14495514624 | bytes 40370176 | tf_op jit(solution)/shard_map/F/pallas_call | solution.py:166
  144.1 9.5 %collective-permute-done.25.refs_11_ = bf16[128,2048]{1,0:T(8,128)(2,1)S(1)} collective-permute-done((bf16[128,2048]{1,0:T(8,128)(2,1)}, bf16[128,2048]{1,0:T(8,128)(2,1)S(1)}, u32[]{:S(2)}, u32[]{:S(2)}) %collective-permute-start.25) | collective-permute-done | bytes 524320 | tf_op jit(solution)/shard_map/g3a/ppermute | solution.py:197
  153.5 11.2 %collective-permute-done.22 = bf16[128,2048]{1,0:T(8,128)(2,1)S(1)} collective-permute-done((bf16[128,2048]{1,0:T(8,128)(2,1)}, bf16[128,2048]{1,0:T(8,128)(2,1)S(1)}, u32[]{:S(2)}, u32[]{:S(2)}) %collective-permute-start.22) | collective-permute-done | bytes 524320 | tf_op jit(solution)/shard_map/o1a/ppermute | solution.py:197
  172.0 8.8 %collective-permute-done.23 = bf16[128,2048]{1,0:T(8,128)(2,1)S(1)} collective-permute-done((bf16[128,2048]{1,0:T(8,128)(2,1)S(1)}, bf16[128,2048]{1,0:T(8,128)(2,1)S(1)}, u32[]{:S(2)}, u32[]{:S(2)}) %collective-permute-start.23) | collective-permute-done | bytes 524320 | tf_op jit(solution)/shard_map/o1z/ppermute | solution.py:209
  184.9 4.7 %collective-permute-done.32.refs_12_ = bf16[256,2048]{1,0:T(8,128)(2,1)S(1)} collective-permute-done((bf16[256,2048]{1,0:T(8,128)(2,1)S(1)}, bf16[256,2048]{1,0:T(8,128)(2,1)S(1)}, u32[]{:S(2)}, u32[]{:S(2)}) %collective-permute-start.32) | collective-permute-done | bytes 1048608 | tf_op jit(solution)/shard_map/g3b/ppermute | solution.py:197
  189.5 6.6 %collective-permute-done.31.refs_5_ = bf16[128,2048]{1,0:T(8,128)(2,1)S(1)} collective-permute-done((bf16[128,2048]{1,0:T(8,128)(2,1)}, bf16[128,2048]{1,0:T(8,128)(2,1)S(1)}, u32[]{:S(2)}, u32[]{:S(2)}) %collective-permute-start.31) | collective-permute-done | bytes 524320 | tf_op jit(solution)/shard_map/g1a/ppermute | solution.py:197
  196.9 29.5 %B.1 = (bf16[128,2048]{1,0:T(8,128)(2,1)}, bf16[128,2048]{1,0:T(8,128)(2,1)}, bf16[256,2048]{1,0:T(8,128)(2,1)}, bf16[128,2048]{1,0:T(8,128)(2,1)}, bf16[128,204...) custom-call(s32[16]{0:T(128)} %stack.90.index_ref, ...), custom_call_target="tpu_custom_call" | custom-call | flops 14495514624 | bytes 40370176 | tf_op jit(solution)/shard_map/B/pallas_call | solution.py:166
  230.7 11.2 %collective-permute-done.39 = bf16[128,2048]{1,0:T(8,128)(2,1)S(1)} collective-permute-done((bf16[128,2048]{1,0:T(8,128)(2,1)}, bf16[128,2048]{1,0:T(8,128)(2,1)S(1)}, u32[]{:S(2)}, u32[]{:S(2)}) %collective-permute-start.39) | collective-permute-done | bytes 524320 | tf_op jit(solution)/shard_map/d1a/ppermute | solution.py:197
  242.8 16.9 %collective-permute-done.36 = bf16[256,2048]{1,0:T(8,128)(2,1)S(1)} collective-permute-done((bf16[256,2048]{1,0:T(8,128)(2,1)}, bf16[256,2048]{1,0:T(8,128)(2,1)S(1)}, u32[]{:S(2)}, u32[]{:S(2)}) %collective-permute-start.36) | collective-permute-done | bytes 1048608 | tf_op jit(solution)/shard_map/d1b/ppermute | solution.py:209
  264.7 12.0 %collective-permute-done.33 = bf16[128,2048]{1,0:T(8,128)(2,1)S(1)} collective-permute-done((bf16[128,2048]{1,0:T(8,128)(2,1)S(1)}, bf16[128,2048]{1,0:T(8,128)(2,1)S(1)}, u32[]{:S(2)}, u32[]{:S(2)}) %collective-permute-start.33) | collective-permute-done | bytes 524320 | tf_op jit(solution)/shard_map/o2a/ppermute | solution.py:197
  278.4 5.2 %collective-permute-done.44 = bf16[128,2048]{1,0:T(8,128)(2,1)S(1)} collective-permute-done((bf16[128,2048]{1,0:T(8,128)(2,1)S(1)}, bf16[128,2048]{1,0:T(8,128)(2,1)S(1)}, u32[]{:S(2)}, u32[]{:S(2)}) %collective-permute-start.44) | collective-permute-done | bytes 524320 | tf_op jit(solution)/shard_map/d3a/ppermute | solution.py:197
  288.9 18.3 %collective-permute-done.37 = bf16[256,2048]{1,0:T(8,128)(2,1)S(1)} collective-permute-done((bf16[256,2048]{1,0:T(8,128)(2,1)S(1)}, bf16[256,2048]{1,0:T(8,128)(2,1)S(1)}, u32[]{:S(2)}, u32[]{:S(2)}) %collective-permute-start.37) | collective-permute-done | bytes 1048608 | tf_op jit(solution)/shard_map/d0b/ppermute | solution.py:197
  309.9 6.5 %collective-permute-done.28 = bf16[128,2048]{1,0:T(8,128)(2,1)S(1)} collective-permute-done((bf16[128,2048]{1,0:T(8,128)(2,1)S(1)}, bf16[128,2048]{1,0:T(8,128)(2,1)S(1)}, u32[]{:S(2)}, u32[]{:S(2)}) %collective-permute-start.28) | collective-permute-done | bytes 524320 | tf_op jit(solution)/shard_map/o0a/ppermute | solution.py:197
  317.6 4.4 %collective-permute-done.38 = bf16[128,2048]{1,0:T(8,128)(2,1)S(1)} collective-permute-done((bf16[128,2048]{1,0:T(8,128)(2,1)S(1)}, bf16[128,2048]{1,0:T(8,128)(2,1)S(1)}, u32[]{:S(2)}, u32[]{:S(2)}) %collective-permute-start.38) | collective-permute-done | bytes 524320 | tf_op jit(solution)/shard_map/d0a/ppermute | solution.py:197
  322.0 3.6 %collective-permute-done.46 = bf16[128,2048]{1,0:T(8,128)(2,1)S(1)} collective-permute-done((bf16[128,2048]{1,0:T(8,128)(2,1)S(1)}, bf16[128,2048]{1,0:T(8,128)(2,1)S(1)}, u32[]{:S(2)}, u32[]{:S(2)}) %collective-permute-start.46) | collective-permute-done | bytes 524320 | tf_op jit(solution)/shard_map/d2z/ppermute | solution.py:209
  (192 shorter events, 79.1 us)
Async XLA Ops:
  25.0 30.6 %collective-permute-start.7 = (bf16[2048,768]{1,0:T(8,128)(2,1)}, bf16[2048,768]{1,0:T(8,128)(2,1)}, u32[]{:S(2)}, u32[]{:S(2)}) collective-permute-start(bf16[2048,768]{1,0:T(8,128)(2,1)} %bitcast.41), channel_id=1, source_target_pairs={{0,1},{1,0},{2,3},{3,2},{4,5},{5,4},{6,7},{7,6},{8,9},{9,8},{10,11... | collective-permute-start | bytes 9437192 | tf_op jit(solution)/shard_map/w1/ppermute | solution.py:197
  25.1 25.7 %collective-permute-start.8 = (bf16[128,2048]{1,0:T(8,128)(2,1)S(1)}, bf16[128,2048]{1,0:T(8,128)(2,1)S(1)}, u32[]{:S(2)}, u32[]{:S(2)}) collective-permute-start(bf16[128,2048]{1,0:T(8,128)(2,1)S(1)} %fusion.3.refs_1_), channel_id=1, source_target_pairs={{0,8},{8,0},{16,24},{24,16},{1,9},{9,1},{17,25},{25,17},{2,10},{10... | collective-permute-start | bytes 1572872 | tf_op jit(solution)/shard_map/x1z/ppermute | solution.py:209
  27.2 26.1 %collective-permute-start = (bf16[128,2048]{1,0:T(8,128)(2,1)S(1)}, bf16[128,2048]{1,0:T(8,128)(2,1)S(1)}, u32[]{:S(2)}, u32[]{:S(2)}) collective-permute-start(bf16[128,2048]{1,0:T(8,128)(2,1)S(1)} %fusion.3.refs_1_), channel_id=1, source_target_pairs={{0,16},{8,24},{16,0},{24,8},{1,17},{9,25},{17,1},{25,9},{2,18},{10... | collective-permute-start | bytes 1572872 | tf_op jit(solution)/shard_map/x2z/ppermute | solution.py:209
  29.9 26.3 %collective-permute-start.6 = (bf16[256,2048]{1,0:T(8,128)(2,1)S(1)}, bf16[256,2048]{1,0:T(8,128)(2,1)}, u32[]{:S(2)}, u32[]{:S(2)}) collective-permute-start(bf16[256,2048]{1,0:T(8,128)(2,1)S(1)} %pad_maximum_fusion), channel_id=1, source_target_pairs={{0,4},{1,3},{2,6},{3,1},{4,0},{5,7},{6,2},{7,5},{8,12},{9,11},{10,... | collective-permute-start | bytes 3145736 | tf_op jit(solution)/shard_map/x0b/ppermute | solution.py:197
  67.9 25.2 %collective-permute-start.9 = (bf16[128,2048]{1,0:T(8,128)(2,1)S(1)}, bf16[128,2048]{1,0:T(8,128)(2,1)S(1)}, u32[]{:S(2)}, u32[]{:S(2)}) collective-permute-start(bf16[128,2048]{1,0:T(8,128)(2,1)S(1)} %copy-done.15), channel_id=1, source_target_pairs={{0,16},{8,24},{16,0},{24,8},{1,17},{9,25},{17,1},{25,9},{2,18},{10... | collective-permute-start | bytes 1572872 | tf_op jit(solution)/shard_map/g2z/ppermute | solution.py:209
  71.2 36.0 %collective-permute-start.15 = (bf16[256,2048]{1,0:T(8,128)(2,1)}, bf16[256,2048]{1,0:T(8,128)(2,1)}, u32[]{:S(2)}, u32[]{:S(2)}) collective-permute-start(bf16[256,2048]{1,0:T(8,128)(2,1)} %collective-permute-done.6.refs_3_), channel_id=1, source_target_pairs={{0,8},{8,0},{16,24},{24,16},{1,9},{9,1},{17,25},{25,17},{2,10},{10... | collective-permute-start | bytes 3145736 | tf_op jit(solution)/shard_map/x1b/ppermute | solution.py:209
  73.1 34.2 %collective-permute-start.16 = (bf16[256,2048]{1,0:T(8,128)(2,1)S(1)}, bf16[256,2048]{1,0:T(8,128)(2,1)}, u32[]{:S(2)}, u32[]{:S(2)}) collective-permute-start(bf16[256,2048]{1,0:T(8,128)(2,1)S(1)} %pad_maximum_fusion.2), channel_id=1, source_target_pairs={{0,4},{1,3},{2,6},{3,1},{4,0},{5,7},{6,2},{7,5},{8,12},{9,11},{10,... | collective-permute-start | bytes 3145736 | tf_op jit(solution)/shard_map/x2b/ppermute | solution.py:197
  77.8 31.3 %collective-permute-start.17 = (bf16[256,2048]{1,0:T(8,128)(2,1)S(1)}, bf16[256,2048]{1,0:T(8,128)(2,1)}, u32[]{:S(2)}, u32[]{:S(2)}) collective-permute-start(bf16[256,2048]{1,0:T(8,128)(2,1)S(1)} %pad_maximum_fusion.3), channel_id=1, source_target_pairs={{0,4},{1,3},{2,6},{3,1},{4,0},{5,7},{6,2},{7,5},{8,12},{9,11},{10,... | collective-permute-start | bytes 3145736 | tf_op jit(solution)/shard_map/x3b/ppermute | solution.py:197
  100.3 38.2 %collective-permute-start.20 = (bf16[128,2048]{1,0:T(8,128)(2,1)S(1)}, bf16[128,2048]{1,0:T(8,128)(2,1)}, u32[]{:S(2)}, u32[]{:S(2)}) collective-permute-start(bf16[128,2048]{1,0:T(8,128)(2,1)S(1)} %collective-permute-done.9.refs_7_), channel_id=1, source_target_pairs={{0,8},{8,0},{16,24},{24,16},{1,9},{9,1},{17,25},{25,17},{2,10},{10... | collective-permute-start | bytes 1572872 | tf_op jit(solution)/shard_map/g3z/ppermute | solution.py:209
  107.3 31.3 %collective-permute-start.18 = (bf16[128,2048]{1,0:T(8,128)(2,1)S(1)}, bf16[128,2048]{1,0:T(8,128)(2,1)}, u32[]{:S(2)}, u32[]{:S(2)}) collective-permute-start(bf16[128,2048]{1,0:T(8,128)(2,1)S(1)} %copy-done.15), channel_id=1, source_target_pairs={{0,8},{8,0},{16,24},{24,16},{1,9},{9,1},{17,25},{25,17},{2,10},{10... | collective-permute-start | bytes 1572872 | tf_op jit(solution)/shard_map/g1z/ppermute | solution.py:209
  109.0 29.5 %collective-permute-start.19 = (bf16[256,2048]{1,0:T(8,128)(2,1)S(1)}, bf16[256,2048]{1,0:T(8,128)(2,1)}, u32[]{:S(2)}, u32[]{:S(2)}) collective-permute-start(bf16[256,2048]{1,0:T(8,128)(2,1)S(1)} %pad_maximum_fusion.4), channel_id=1, source_target_pairs={{0,4},{1,3},{2,6},{3,1},{4,0},{5,7},{6,2},{7,5},{8,12},{9,11},{10,... | collective-permute-start | bytes 3145736 | tf_op jit(solution)/shard_map/g2b/ppermute | solution.py:197
  139.9 24.8 %collective-permute-start.22 = (bf16[128,2048]{1,0:T(8,128)(2,1)}, bf16[128,2048]{1,0:T(8,128)(2,1)S(1)}, u32[]{:S(2)}, u32[]{:S(2)}) collective-permute-start(bf16[128,2048]{1,0:T(8,128)(2,1)} %get-tuple-element.80), channel_id=1, source_target_pairs={{0,2},{1,5},{2,0},{3,7},{4,6},{5,1},{6,4},{7,3},{8,10},{9,13},{10,... | collective-permute-start | bytes 1572872 | tf_op jit(solution)/shard_map/o1a/ppermute | solution.py:197
  140.6 29.1 %collective-permute-start.24 = (bf16[256,2048]{1,0:T(8,128)(2,1)}, bf16[256,2048]{1,0:T(8,128)(2,1)S(1)}, u32[]{:S(2)}, u32[]{:S(2)}) collective-permute-start(bf16[256,2048]{1,0:T(8,128)(2,1)} %get-tuple-element.82), channel_id=1, source_target_pairs={{0,4},{1,3},{2,6},{3,1},{4,0},{5,7},{6,2},{7,5},{8,12},{9,11},{10,... | collective-permute-start | bytes 3145736 | tf_op jit(solution)/shard_map/o3b/ppermute | solution.py:197
  142.7 38.2 %collective-permute-start.21 = (bf16[256,2048]{1,0:T(8,128)(2,1)S(1)}, bf16[256,2048]{1,0:T(8,128)(2,1)S(1)}, u32[]{:S(2)}, u32[]{:S(2)}) collective-permute-start(bf16[256,2048]{1,0:T(8,128)(2,1)S(1)} %copy-done.34), channel_id=1, source_target_pairs={{0,8},{8,0},{16,24},{24,16},{1,9},{9,1},{17,25},{25,17},{2,10},{10... | collective-permute-start | bytes 3145736 | tf_op jit(solution)/shard_map/g1b/ppermute | solution.py:209
  181.9 48.4 %collective-permute-start.26 = (bf16[256,2048]{1,0:T(8,128)(2,1)}, bf16[256,2048]{1,0:T(8,128)(2,1)S(1)}, u32[]{:S(2)}, u32[]{:S(2)}) collective-permute-start(bf16[256,2048]{1,0:T(8,128)(2,1)} %get-tuple-element.84), channel_id=1, source_target_pairs={{0,8},{8,0},{16,24},{24,16},{1,9},{9,1},{17,25},{25,17},{2,10},{10... | collective-permute-start | bytes 3145736 | tf_op jit(solution)/shard_map/o1b/ppermute | solution.py:209
  184.1 57.9 %collective-permute-start.29 = (bf16[256,2048]{1,0:T(8,128)(2,1)}, bf16[256,2048]{1,0:T(8,128)(2,1)S(1)}, u32[]{:S(2)}, u32[]{:S(2)}) collective-permute-start(bf16[256,2048]{1,0:T(8,128)(2,1)} %get-tuple-element.88), channel_id=1, source_target_pairs={{0,4},{1,3},{2,6},{3,1},{4,0},{5,7},{6,2},{7,5},{8,12},{9,11},{10,... | collective-permute-start | bytes 3145736 | tf_op jit(solution)/shard_map/o2b/ppermute | solution.py:197
  228.2 36.0 %collective-permute-start.34 = (bf16[128,2048]{1,0:T(8,128)(2,1)S(1)}, bf16[128,2048]{1,0:T(8,128)(2,1)S(1)}, u32[]{:S(2)}, u32[]{:S(2)}) collective-permute-start(bf16[128,2048]{1,0:T(8,128)(2,1)S(1)} %add_convert_fusion.10), channel_id=1, source_target_pairs={{0,8},{8,0},{16,24},{24,16},{1,9},{9,1},{17,25},{25,17},{2,10},{10... | collective-permute-start | bytes 1572872 | tf_op jit(solution)/shard_map/o3z/ppermute | solution.py:209
  228.7 30.9 %collective-permute-start.36 = (bf16[256,2048]{1,0:T(8,128)(2,1)}, bf16[256,2048]{1,0:T(8,128)(2,1)S(1)}, u32[]{:S(2)}, u32[]{:S(2)}) collective-permute-start(bf16[256,2048]{1,0:T(8,128)(2,1)} %get-tuple-element.101), channel_id=1, source_target_pairs={{0,8},{8,0},{16,24},{24,16},{1,9},{9,1},{17,25},{25,17},{2,10},{10... | collective-permute-start | bytes 3145736 | tf_op jit(solution)/shard_map/d1b/ppermute | solution.py:209
  230.2 33.1 %collective-permute-start.41 = (bf16[256,2048]{1,0:T(8,128)(2,1)S(1)}, bf16[256,2048]{1,0:T(8,128)(2,1)S(1)}, u32[]{:S(2)}, u32[]{:S(2)}) collective-permute-start(bf16[256,2048]{1,0:T(8,128)(2,1)S(1)} %copy-done.35), channel_id=1, source_target_pairs={{0,4},{1,3},{2,6},{3,1},{4,0},{5,7},{6,2},{7,5},{8,12},{9,11},{10,... | collective-permute-start | bytes 3145736 | tf_op jit(solution)/shard_map/d2b/ppermute | solution.py:197
  242.0 75.6 %collective-permute-start.40 = (bf16[128,2048]{1,0:T(8,128)(2,1)S(1)}, bf16[128,2048]{1,0:T(8,128)(2,1)S(1)}, u32[]{:S(2)}, u32[]{:S(2)}) collective-permute-start(bf16[128,2048]{1,0:T(8,128)(2,1)S(1)} %add_convert_fusion.6), channel_id=1, source_target_pairs={{0,8},{8,0},{16,24},{24,16},{1,9},{9,1},{17,25},{25,17},{2,10},{10... | collective-permute-start | bytes 1572872 | tf_op jit(solution)/shard_map/d1z/ppermute | solution.py:209
  259.7 27.3 %collective-permute-start.27 = (bf16[256,2048]{1,0:T(8,128)(2,1)S(1)}, bf16[256,2048]{1,0:T(8,128)(2,1)S(1)}, u32[]{:S(2)}, u32[]{:S(2)}) collective-permute-start(bf16[256,2048]{1,0:T(8,128)(2,1)S(1)} %add_convert_fusion.1), channel_id=1, source_target_pairs={{0,4},{1,3},{2,6},{3,1},{4,0},{5,7},{6,2},{7,5},{8,12},{9,11},{10,... | collective-permute-start | bytes 3145736 | tf_op jit(solution)/shard_map/o0b/ppermute | solution.py:197
  264.2 43.0 %collective-permute-start.37 = (bf16[256,2048]{1,0:T(8,128)(2,1)S(1)}, bf16[256,2048]{1,0:T(8,128)(2,1)S(1)}, u32[]{:S(2)}, u32[]{:S(2)}) collective-permute-start(bf16[256,2048]{1,0:T(8,128)(2,1)S(1)} %add_convert_fusion), channel_id=1, source_target_pairs={{0,4},{1,3},{2,6},{3,1},{4,0},{5,7},{6,2},{7,5},{8,12},{9,11},{10,... | collective-permute-start | bytes 3145736 | tf_op jit(solution)/shard_map/d0b/ppermute | solution.py:197
  276.7 31.6 %collective-permute-start.42 = (bf16[128,2048]{1,0:T(8,128)(2,1)S(1)}, bf16[128,2048]{1,0:T(8,128)(2,1)S(1)}, u32[]{:S(2)}, u32[]{:S(2)}) collective-permute-start(bf16[128,2048]{1,0:T(8,128)(2,1)S(1)} %add_convert_fusion.5), channel_id=1, source_target_pairs={{0,2},{1,5},{2,0},{3,7},{4,6},{5,1},{6,4},{7,3},{8,10},{9,13},{10,... | collective-permute-start | bytes 1572872 | tf_op jit(solution)/shard_map/d2a/ppermute | solution.py:197
  283.6 26.3 %collective-permute-start.35 = (bf16[128,2048]{1,0:T(8,128)(2,1)S(1)}, bf16[128,2048]{1,0:T(8,128)(2,1)S(1)}, u32[]{:S(2)}, u32[]{:S(2)}) collective-permute-start(bf16[128,2048]{1,0:T(8,128)(2,1)S(1)} %add_convert_fusion.9), channel_id=1, source_target_pairs={{0,16},{8,24},{16,0},{24,8},{1,17},{9,25},{17,1},{25,9},{2,18},{10... | collective-permute-start | bytes 1572872 | tf_op jit(solution)/shard_map/o2z/ppermute | solution.py:209
  (66 other events, 1220.4 us)

commit v6 on v5

--- a/solution.py
+++ b/solution.py
@@ -222,13 +222,13 @@
     ("x2a", ("w1", "x1z",)), ("x1b", ("w1", "x1z", "x2z",)), ("g2z", ("x3z", "x0b", "w1", "x1z",)),
     ("tab", ("g0b", "x3z", "x0b", "w1", "x1z",)), ("x3a", ("x1a", "g0b", "x0b", "w1",)),
     ("x2b", ("x1a", "g0b", "x3z", "x0b",)), ("x3b", ("x2a",)), ("g2a", ("x3a", "x2a",)),
-    ("g3z", ("x3a", "x2a",)), ("g1z", ("x1b", "x2b", "g2z", "x3a",)), ("g2b", ("x1b", "x2b",)),
-    ("F", ("g2a",)), ("o1a", ("g1z", "g2b", "g3z",)), ("g3a", ("F", "g1z", "g2b",)),
-    ("o3b", ("g1z", "g2b", "g3z",)), ("g1b", ("F", "g1z", "g2b", "g3z",)), ("o1z", ()), ("g3b", ("o1a",)),
-    ("o3a", ("g3a", "o1a",)), ("g1a", ("o3b", "g3a", "o1a",)), ("o2b", ("o1z", "o3b", "g3a",)),
-    ("o1b", ("g1b", "o1z", "o3b", "g3a",)), ("o3z", ("g3b", "g1b", "o1z",)), ("B", ("o3a", "o1z",)),
-    ("o2a", ("B",)), ("d3b", ()), ("d2b", ()), ("d1b", ()), ("o2z", ()), ("d3a", ()), ("d1a", ()), ("d2a", ()),
-    ("d3z", ()), ("d0b", ()), ("o0b", ()), ("d2z", ()), ("d1z", ()), ("d0a", ()), ("o0a", ()),
+    ("g3z", ("x3a", "x2a",)), ("g1z", ("x1b", "x2b", "g2z", "x3a",)), ("g2b", ("x1b", "x2b",)), ("F", ()),
+    ("o1a", ("g2b",)), ("g3a", ("F", "g1z", "g2b",)), ("o3b", ("g1z", "g2b", "g3z",)),
+    ("g1b", ("F", "g1z", "g2b", "g3z",)), ("o1z", ()), ("g3b", ("o1a",)), ("o3a", ("g3a", "o1a",)),
+    ("g1a", ("o3b", "g3a", "o1a",)), ("o2b", ("o1z", "o3b", "g3a",)), ("o1b", ("g1b", "o1z", "o3b", "g3a",)),
+    ("o3z", ("g3b", "g1b", "o1z",)), ("B", ("o3a", "o1z",)), ("o2a", ("B",)), ("d3b", ()), ("d2b", ()),
+    ("d1b", ()), ("o2z", ()), ("d3a", ()), ("d1a", ()), ("d2a", ()), ("d3z", ()), ("d0b", ()), ("o0b", ()),
+    ("d2z", ()), ("d1z", ()), ("d0a", ()), ("o0a", ()),
 )
 
 

time: 328 us -> 328 us (level)
  transfers between devices with their start and end apart: 48 -> 48, of which waited for: 24 -> 23; matrix products, arithmetic and copies ran while one was open for 3% -> 3% of each run, Pallas kernels for 18% -> 18%
where the time goes in v6:
time: 328 us
  waiting for transfers between devices  190 us (58%)
  starting transfers between devices  62 us (19%)
  Pallas kernels  58.3 us (18%)
  other arithmetic  11.3 us (3%)
  local copies, waits for them, and re-layouts  4.74 us (1%)
    ppermute x31, waiting for transfers between devices, ep_permute(): return lax.ppermute(value, 'ep', [(i, partner(i)) for i in range(8)])  112 us
    ppermute x16, waiting for transfers between devices, along_z(): return lax.ppermute(value, 'seq', [(i, i ^ k) for i in range(4)])  77.7 us
    pallas_call x2, Pallas kernels, run_experts(): pl.pallas_call(functools.partial(experts_kernel, forward, cap, groups), o...  58.3 us
    ppermute x31, starting transfers between devices, ep_permute(): return lax.ppermute(value, 'ep', [(i, partner(i)) for i in range(8)])  32.4 us
    ppermute x16, starting transfers between devices, along_z(): return lax.ppermute(value, 'seq', [(i, i ^ k) for i in range(4)])  25.3 us
  transfers between devices with their start and end apart: 48, of which 23 were waited for; matrix products, arithmetic and copies ran while one was open for 3% of the time, Pallas kernels for 18%

profile of v6, /device:TPU:0, one launch (start us, length us, event | category | flops | bytes accessed | tf_op | source)
XLA Modules:
  0.0 327.7 jit_solution(5469862504040284435)
XLA Ops:
  6.3 7.1 %collective-permute-done.2.refs_2_ = bf16[128,2048]{1,0:T(8,128)(2,1)S(1)} collective-permute-done((bf16[128,2048]{1,0:T(8,128)(2,1)S(1)}, bf16[128,2048]{1,0:T(8,128)(2,1)S(1)}, u32[]{:S(2)}, u32[]{:S(2)}) %collective-permute-start.2) | collective-permute-done | bytes 524320 | tf_op jit(solution)/shard_map/x0a/ppermute | solution.py:197
  13.4 5.6 %collective-permute-done.refs_2_ = bf16[128,2048]{1,0:T(8,128)(2,1)S(1)} collective-permute-done((bf16[128,2048]{1,0:T(8,128)(2,1)}, bf16[128,2048]{1,0:T(8,128)(2,1)S(1)}, u32[]{:S(2)}, u32[]{:S(2)}) %collective-permute-start) | collective-permute-done | bytes 524320 | tf_op jit(solution)/shard_map/g0a/ppermute | solution.py:197
  19.1 5.9 %collective-permute-done.5.refs_18_ = bf16[768,2048]{1,0:T(8,128)(2,1)S(1)} collective-permute-done((bf16[768,2048]{1,0:T(8,128)(2,1)}, bf16[768,2048]{1,0:T(8,128)(2,1)S(1)}, u32[]{:S(2)}, u32[]{:S(2)}) %collective-permute-start.5) | collective-permute-done | bytes 3145760 | tf_op jit(solution)/shard_map/w2/ppermute | solution.py:197
  32.2 18.6 %collective-permute-done.9.refs_4_ = bf16[128,2048]{1,0:T(8,128)(2,1)S(1)} collective-permute-done((bf16[128,2048]{1,0:T(8,128)(2,1)S(1)}, bf16[128,2048]{1,0:T(8,128)(2,1)S(1)}, u32[]{:S(2)}, u32[]{:S(2)}) %collective-permute-start.9) | collective-permute-done | bytes 524320 | tf_op jit(solution)/shard_map/x1z/ppermute | solution.py:209
  56.2 9.3 %collective-permute-done.6.refs_10_ = bf16[128,2048]{1,0:T(8,128)(2,1)S(1)} collective-permute-done((bf16[128,2048]{1,0:T(8,128)(2,1)S(1)}, bf16[128,2048]{1,0:T(8,128)(2,1)S(1)}, u32[]{:S(2)}, u32[]{:S(2)}) %collective-permute-start.6) | collective-permute-done | bytes 524320 | tf_op jit(solution)/shard_map/x3z/ppermute | solution.py:209
  67.9 3.4 %collective-permute-start.16 = (bf16[128,2048]{1,0:T(8,128)(2,1)S(1)}, bf16[128,2048]{1,0:T(8,128)(2,1)S(1)}, u32[]{:S(2)}, u32[]{:S(2)}) collective-permute-start(bf16[128,2048]{1,0:T(8,128)(2,1)S(1)} %copy-done.15), channel_id=1, source_target_pairs={{0,16},{8,24},{16,0},{24,8},{1,17},{9,25},{17,1},{25,9},{2,18},{10... | collective-permute-start | bytes 1572872 | tf_op jit(solution)/shard_map/g2z/ppermute | solution.py:209
  80.4 12.7 %collective-permute-done.16.refs_7_ = bf16[128,2048]{1,0:T(8,128)(2,1)S(1)} collective-permute-done((bf16[128,2048]{1,0:T(8,128)(2,1)S(1)}, bf16[128,2048]{1,0:T(8,128)(2,1)S(1)}, u32[]{:S(2)}, u32[]{:S(2)}) %collective-permute-start.16) | collective-permute-done | bytes 524320 | tf_op jit(solution)/shard_map/g2z/ppermute | solution.py:209
  96.1 4.2 %all-to-all-start = ((f32[32,1,256]{2,1,0:T(1,128)}), f32[32,1,256]{2,1,0:T(1,128)S(1)}, u32[]{:S(2)}, u32[]{:S(2)}) async-start(f32[32,1,256]{2,1,0:T(1,128)} %all_to_all.6), calls=%async_computation | async-start | bytes 65536 | tf_op jit(solution)/shard_map/tab/all_to_all | solution.py:324
  102.0 5.3 %collective-permute-done.11.refs_6_ = bf16[256,2048]{1,0:T(8,128)(2,1)} collective-permute-done((bf16[256,2048]{1,0:T(8,128)(2,1)}, bf16[256,2048]{1,0:T(8,128)(2,1)}, u32[]{:S(2)}, u32[]{:S(2)}) %collective-permute-start.11) | collective-permute-done | bytes 1048608 | tf_op jit(solution)/shard_map/x1b/ppermute | solution.py:209
  109.7 28.8 %F.1 = (bf16[128,2048]{1,0:T(8,128)(2,1)}, bf16[128,2048]{1,0:T(8,128)(2,1)}, bf16[256,2048]{1,0:T(8,128)(2,1)}, bf16[128,2048]{1,0:T(8,128)(2,1)}, bf16[128,204...) custom-call(s32[16]{0:T(128)} %stack.90.index_ref, ...), custom_call_target="tpu_custom_call" | custom-call | flops 14495514624 | bytes 40370176 | tf_op jit(solution)/shard_map/F/pallas_call | solution.py:166
  144.1 9.5 %collective-permute-done.25.refs_11_ = bf16[128,2048]{1,0:T(8,128)(2,1)S(1)} collective-permute-done((bf16[128,2048]{1,0:T(8,128)(2,1)}, bf16[128,2048]{1,0:T(8,128)(2,1)S(1)}, u32[]{:S(2)}, u32[]{:S(2)}) %collective-permute-start.25) | collective-permute-done | bytes 524320 | tf_op jit(solution)/shard_map/g3a/ppermute | solution.py:197
  153.5 11.2 %collective-permute-done.22 = bf16[128,2048]{1,0:T(8,128)(2,1)S(1)} collective-permute-done((bf16[128,2048]{1,0:T(8,128)(2,1)}, bf16[128,2048]{1,0:T(8,128)(2,1)S(1)}, u32[]{:S(2)}, u32[]{:S(2)}) %collective-permute-start.22) | collective-permute-done | bytes 524320 | tf_op jit(solution)/shard_map/o1a/ppermute | solution.py:197
  172.0 8.8 %collective-permute-done.23 = bf16[128,2048]{1,0:T(8,128)(2,1)S(1)} collective-permute-done((bf16[128,2048]{1,0:T(8,128)(2,1)S(1)}, bf16[128,2048]{1,0:T(8,128)(2,1)S(1)}, u32[]{:S(2)}, u32[]{:S(2)}) %collective-permute-start.23) | collective-permute-done | bytes 524320 | tf_op jit(solution)/shard_map/o1z/ppermute | solution.py:209
  184.8 4.7 %collective-permute-done.32.refs_12_ = bf16[256,2048]{1,0:T(8,128)(2,1)S(1)} collective-permute-done((bf16[256,2048]{1,0:T(8,128)(2,1)S(1)}, bf16[256,2048]{1,0:T(8,128)(2,1)S(1)}, u32[]{:S(2)}, u32[]{:S(2)}) %collective-permute-start.32) | collective-permute-done | bytes 1048608 | tf_op jit(solution)/shard_map/g3b/ppermute | solution.py:197
  189.5 6.5 %collective-permute-done.31.refs_5_ = bf16[128,2048]{1,0:T(8,128)(2,1)S(1)} collective-permute-done((bf16[128,2048]{1,0:T(8,128)(2,1)}, bf16[128,2048]{1,0:T(8,128)(2,1)S(1)}, u32[]{:S(2)}, u32[]{:S(2)}) %collective-permute-start.31) | collective-permute-done | bytes 524320 | tf_op jit(solution)/shard_map/g1a/ppermute | solution.py:197
  196.9 29.5 %B.1 = (bf16[128,2048]{1,0:T(8,128)(2,1)}, bf16[128,2048]{1,0:T(8,128)(2,1)}, bf16[256,2048]{1,0:T(8,128)(2,1)}, bf16[128,2048]{1,0:T(8,128)(2,1)}, bf16[128,204...) custom-call(s32[16]{0:T(128)} %stack.90.index_ref, ...), custom_call_target="tpu_custom_call" | custom-call | flops 14495514624 | bytes 40370176 | tf_op jit(solution)/shard_map/B/pallas_call | solution.py:166
  230.7 11.2 %collective-permute-done.39 = bf16[128,2048]{1,0:T(8,128)(2,1)S(1)} collective-permute-done((bf16[128,2048]{1,0:T(8,128)(2,1)}, bf16[128,2048]{1,0:T(8,128)(2,1)S(1)}, u32[]{:S(2)}, u32[]{:S(2)}) %collective-permute-start.39) | collective-permute-done | bytes 524320 | tf_op jit(solution)/shard_map/d1a/ppermute | solution.py:197
  242.8 16.9 %collective-permute-done.36 = bf16[256,2048]{1,0:T(8,128)(2,1)S(1)} collective-permute-done((bf16[256,2048]{1,0:T(8,128)(2,1)}, bf16[256,2048]{1,0:T(8,128)(2,1)S(1)}, u32[]{:S(2)}, u32[]{:S(2)}) %collective-permute-start.36) | collective-permute-done | bytes 1048608 | tf_op jit(solution)/shard_map/d1b/ppermute | solution.py:209
  264.7 12.0 %collective-permute-done.33 = bf16[128,2048]{1,0:T(8,128)(2,1)S(1)} collective-permute-done((bf16[128,2048]{1,0:T(8,128)(2,1)S(1)}, bf16[128,2048]{1,0:T(8,128)(2,1)S(1)}, u32[]{:S(2)}, u32[]{:S(2)}) %collective-permute-start.33) | collective-permute-done | bytes 524320 | tf_op jit(solution)/shard_map/o2a/ppermute | solution.py:197
  278.4 5.2 %collective-permute-done.44 = bf16[128,2048]{1,0:T(8,128)(2,1)S(1)} collective-permute-done((bf16[128,2048]{1,0:T(8,128)(2,1)S(1)}, bf16[128,2048]{1,0:T(8,128)(2,1)S(1)}, u32[]{:S(2)}, u32[]{:S(2)}) %collective-permute-start.44) | collective-permute-done | bytes 524320 | tf_op jit(solution)/shard_map/d3a/ppermute | solution.py:197
  288.9 18.3 %collective-permute-done.37 = bf16[256,2048]{1,0:T(8,128)(2,1)S(1)} collective-permute-done((bf16[256,2048]{1,0:T(8,128)(2,1)S(1)}, bf16[256,2048]{1,0:T(8,128)(2,1)S(1)}, u32[]{:S(2)}, u32[]{:S(2)}) %collective-permute-start.37) | collective-permute-done | bytes 1048608 | tf_op jit(solution)/shard_map/d0b/ppermute | solution.py:197
  309.9 6.5 %collective-permute-done.28 = bf16[128,2048]{1,0:T(8,128)(2,1)S(1)} collective-permute-done((bf16[128,2048]{1,0:T(8,128)(2,1)S(1)}, bf16[128,2048]{1,0:T(8,128)(2,1)S(1)}, u32[]{:S(2)}, u32[]{:S(2)}) %collective-permute-start.28) | collective-permute-done | bytes 524320 | tf_op jit(solution)/shard_map/o0a/ppermute | solution.py:197
  317.6 4.4 %collective-permute-done.38 = bf16[128,2048]{1,0:T(8,128)(2,1)S(1)} collective-permute-done((bf16[128,2048]{1,0:T(8,128)(2,1)S(1)}, bf16[128,2048]{1,0:T(8,128)(2,1)S(1)}, u32[]{:S(2)}, u32[]{:S(2)}) %collective-permute-start.38) | collective-permute-done | bytes 524320 | tf_op jit(solution)/shard_map/d0a/ppermute | solution.py:197
  322.0 3.6 %collective-permute-done.46 = bf16[128,2048]{1,0:T(8,128)(2,1)S(1)} collective-permute-done((bf16[128,2048]{1,0:T(8,128)(2,1)S(1)}, bf16[128,2048]{1,0:T(8,128)(2,1)S(1)}, u32[]{:S(2)}, u32[]{:S(2)}) %collective-permute-start.46) | collective-permute-done | bytes 524320 | tf_op jit(solution)/shard_map/d2z/ppermute | solution.py:209
  (192 shorter events, 77.2 us)
Async XLA Ops:
  25.0 30.6 %collective-permute-start.8 = (bf16[2048,768]{1,0:T(8,128)(2,1)}, bf16[2048,768]{1,0:T(8,128)(2,1)}, u32[]{:S(2)}, u32[]{:S(2)}) collective-permute-start(bf16[2048,768]{1,0:T(8,128)(2,1)} %bitcast.41), channel_id=1, source_target_pairs={{0,1},{1,0},{2,3},{3,2},{4,5},{5,4},{6,7},{7,6},{8,9},{9,8},{10,11... | collective-permute-start | bytes 9437192 | tf_op jit(solution)/shard_map/w1/ppermute | solution.py:197
  25.1 25.7 %collective-permute-start.9 = (bf16[128,2048]{1,0:T(8,128)(2,1)S(1)}, bf16[128,2048]{1,0:T(8,128)(2,1)S(1)}, u32[]{:S(2)}, u32[]{:S(2)}) collective-permute-start(bf16[128,2048]{1,0:T(8,128)(2,1)S(1)} %fusion.3.refs_1_), channel_id=1, source_target_pairs={{0,8},{8,0},{16,24},{24,16},{1,9},{9,1},{17,25},{25,17},{2,10},{10... | collective-permute-start | bytes 1572872 | tf_op jit(solution)/shard_map/x1z/ppermute | solution.py:209
  27.2 26.1 %collective-permute-start.4 = (bf16[128,2048]{1,0:T(8,128)(2,1)S(1)}, bf16[128,2048]{1,0:T(8,128)(2,1)S(1)}, u32[]{:S(2)}, u32[]{:S(2)}) collective-permute-start(bf16[128,2048]{1,0:T(8,128)(2,1)S(1)} %fusion.3.refs_1_), channel_id=1, source_target_pairs={{0,16},{8,24},{16,0},{24,8},{1,17},{9,25},{17,1},{25,9},{2,18},{10... | collective-permute-start | bytes 1572872 | tf_op jit(solution)/shard_map/x2z/ppermute | solution.py:209
  29.9 26.3 %collective-permute-start.7 = (bf16[256,2048]{1,0:T(8,128)(2,1)S(1)}, bf16[256,2048]{1,0:T(8,128)(2,1)}, u32[]{:S(2)}, u32[]{:S(2)}) collective-permute-start(bf16[256,2048]{1,0:T(8,128)(2,1)S(1)} %pad_maximum_fusion.1), channel_id=1, source_target_pairs={{0,4},{1,3},{2,6},{3,1},{4,0},{5,7},{6,2},{7,5},{8,12},{9,11},{10,... | collective-permute-start | bytes 3145736 | tf_op jit(solution)/shard_map/x0b/ppermute | solution.py:197
  67.9 25.2 %collective-permute-start.16 = (bf16[128,2048]{1,0:T(8,128)(2,1)S(1)}, bf16[128,2048]{1,0:T(8,128)(2,1)S(1)}, u32[]{:S(2)}, u32[]{:S(2)}) collective-permute-start(bf16[128,2048]{1,0:T(8,128)(2,1)S(1)} %copy-done.15), channel_id=1, source_target_pairs={{0,16},{8,24},{16,0},{24,8},{1,17},{9,25},{17,1},{25,9},{2,18},{10... | collective-permute-start | bytes 1572872 | tf_op jit(solution)/shard_map/g2z/ppermute | solution.py:209
  71.2 36.0 %collective-permute-start.11 = (bf16[256,2048]{1,0:T(8,128)(2,1)}, bf16[256,2048]{1,0:T(8,128)(2,1)}, u32[]{:S(2)}, u32[]{:S(2)}) collective-permute-start(bf16[256,2048]{1,0:T(8,128)(2,1)} %collective-permute-done.7.refs_3_), channel_id=1, source_target_pairs={{0,8},{8,0},{16,24},{24,16},{1,9},{9,1},{17,25},{25,17},{2,10},{10... | collective-permute-start | bytes 3145736 | tf_op jit(solution)/shard_map/x1b/ppermute | solution.py:209
  73.1 34.2 %collective-permute-start.13 = (bf16[256,2048]{1,0:T(8,128)(2,1)S(1)}, bf16[256,2048]{1,0:T(8,128)(2,1)}, u32[]{:S(2)}, u32[]{:S(2)}) collective-permute-start(bf16[256,2048]{1,0:T(8,128)(2,1)S(1)} %pad_maximum_fusion.2), channel_id=1, source_target_pairs={{0,4},{1,3},{2,6},{3,1},{4,0},{5,7},{6,2},{7,5},{8,12},{9,11},{10,... | collective-permute-start | bytes 3145736 | tf_op jit(solution)/shard_map/x2b/ppermute | solution.py:197
  77.8 31.3 %collective-permute-start.15 = (bf16[256,2048]{1,0:T(8,128)(2,1)S(1)}, bf16[256,2048]{1,0:T(8,128)(2,1)}, u32[]{:S(2)}, u32[]{:S(2)}) collective-permute-start(bf16[256,2048]{1,0:T(8,128)(2,1)S(1)} %pad_maximum_fusion.3), channel_id=1, source_target_pairs={{0,4},{1,3},{2,6},{3,1},{4,0},{5,7},{6,2},{7,5},{8,12},{9,11},{10,... | collective-permute-start | bytes 3145736 | tf_op jit(solution)/shard_map/x3b/ppermute | solution.py:197
  100.3 38.2 %collective-permute-start.20 = (bf16[128,2048]{1,0:T(8,128)(2,1)S(1)}, bf16[128,2048]{1,0:T(8,128)(2,1)}, u32[]{:S(2)}, u32[]{:S(2)}) collective-permute-start(bf16[128,2048]{1,0:T(8,128)(2,1)S(1)} %collective-permute-done.16.refs_7_), channel_id=1, source_target_pairs={{0,8},{8,0},{16,24},{24,16},{1,9},{9,1},{17,25},{25,17},{2,10},{10... | collective-permute-start | bytes 1572872 | tf_op jit(solution)/shard_map/g3z/ppermute | solution.py:209
  107.3 31.3 %collective-permute-start.17 = (bf16[128,2048]{1,0:T(8,128)(2,1)S(1)}, bf16[128,2048]{1,0:T(8,128)(2,1)}, u32[]{:S(2)}, u32[]{:S(2)}) collective-permute-start(bf16[128,2048]{1,0:T(8,128)(2,1)S(1)} %copy-done.15), channel_id=1, source_target_pairs={{0,8},{8,0},{16,24},{24,16},{1,9},{9,1},{17,25},{25,17},{2,10},{10... | collective-permute-start | bytes 1572872 | tf_op jit(solution)/shard_map/g1z/ppermute | solution.py:209
  109.0 29.5 %collective-permute-start.19 = (bf16[256,2048]{1,0:T(8,128)(2,1)S(1)}, bf16[256,2048]{1,0:T(8,128)(2,1)}, u32[]{:S(2)}, u32[]{:S(2)}) collective-permute-start(bf16[256,2048]{1,0:T(8,128)(2,1)S(1)} %pad_maximum_fusion.4), channel_id=1, source_target_pairs={{0,4},{1,3},{2,6},{3,1},{4,0},{5,7},{6,2},{7,5},{8,12},{9,11},{10,... | collective-permute-start | bytes 3145736 | tf_op jit(solution)/shard_map/g2b/ppermute | solution.py:197
  139.9 24.8 %collective-permute-start.22 = (bf16[128,2048]{1,0:T(8,128)(2,1)}, bf16[128,2048]{1,0:T(8,128)(2,1)S(1)}, u32[]{:S(2)}, u32[]{:S(2)}) collective-permute-start(bf16[128,2048]{1,0:T(8,128)(2,1)} %get-tuple-element.78), channel_id=1, source_target_pairs={{0,2},{1,5},{2,0},{3,7},{4,6},{5,1},{6,4},{7,3},{8,10},{9,13},{10,... | collective-permute-start | bytes 1572872 | tf_op jit(solution)/shard_map/o1a/ppermute | solution.py:197
  140.6 29.1 %collective-permute-start.24 = (bf16[256,2048]{1,0:T(8,128)(2,1)}, bf16[256,2048]{1,0:T(8,128)(2,1)S(1)}, u32[]{:S(2)}, u32[]{:S(2)}) collective-permute-start(bf16[256,2048]{1,0:T(8,128)(2,1)} %get-tuple-element.80), channel_id=1, source_target_pairs={{0,4},{1,3},{2,6},{3,1},{4,0},{5,7},{6,2},{7,5},{8,12},{9,11},{10,... | collective-permute-start | bytes 3145736 | tf_op jit(solution)/shard_map/o3b/ppermute | solution.py:197
  142.7 38.2 %collective-permute-start.21 = (bf16[256,2048]{1,0:T(8,128)(2,1)S(1)}, bf16[256,2048]{1,0:T(8,128)(2,1)S(1)}, u32[]{:S(2)}, u32[]{:S(2)}) collective-permute-start(bf16[256,2048]{1,0:T(8,128)(2,1)S(1)} %copy-done.34), channel_id=1, source_target_pairs={{0,8},{8,0},{16,24},{24,16},{1,9},{9,1},{17,25},{25,17},{2,10},{10... | collective-permute-start | bytes 3145736 | tf_op jit(solution)/shard_map/g1b/ppermute | solution.py:209
  181.9 48.4 %collective-permute-start.26 = (bf16[256,2048]{1,0:T(8,128)(2,1)}, bf16[256,2048]{1,0:T(8,128)(2,1)S(1)}, u32[]{:S(2)}, u32[]{:S(2)}) collective-permute-start(bf16[256,2048]{1,0:T(8,128)(2,1)} %get-tuple-element.82), channel_id=1, source_target_pairs={{0,8},{8,0},{16,24},{24,16},{1,9},{9,1},{17,25},{25,17},{2,10},{10... | collective-permute-start | bytes 3145736 | tf_op jit(solution)/shard_map/o1b/ppermute | solution.py:209
  183.7 58.3 %collective-permute-start.29 = (bf16[256,2048]{1,0:T(8,128)(2,1)}, bf16[256,2048]{1,0:T(8,128)(2,1)S(1)}, u32[]{:S(2)}, u32[]{:S(2)}) collective-permute-start(bf16[256,2048]{1,0:T(8,128)(2,1)} %get-tuple-element.86), channel_id=1, source_target_pairs={{0,4},{1,3},{2,6},{3,1},{4,0},{5,7},{6,2},{7,5},{8,12},{9,11},{10,... | collective-permute-start | bytes 3145736 | tf_op jit(solution)/shard_map/o2b/ppermute | solution.py:197
  228.2 36.0 %collective-permute-start.34 = (bf16[128,2048]{1,0:T(8,128)(2,1)S(1)}, bf16[128,2048]{1,0:T(8,128)(2,1)S(1)}, u32[]{:S(2)}, u32[]{:S(2)}) collective-permute-start(bf16[128,2048]{1,0:T(8,128)(2,1)S(1)} %add_convert_fusion.10), channel_id=1, source_target_pairs={{0,8},{8,0},{16,24},{24,16},{1,9},{9,1},{17,25},{25,17},{2,10},{10... | collective-permute-start | bytes 1572872 | tf_op jit(solution)/shard_map/o3z/ppermute | solution.py:209
  228.7 31.0 %collective-permute-start.36 = (bf16[256,2048]{1,0:T(8,128)(2,1)}, bf16[256,2048]{1,0:T(8,128)(2,1)S(1)}, u32[]{:S(2)}, u32[]{:S(2)}) collective-permute-start(bf16[256,2048]{1,0:T(8,128)(2,1)} %get-tuple-element.99), channel_id=1, source_target_pairs={{0,8},{8,0},{16,24},{24,16},{1,9},{9,1},{17,25},{25,17},{2,10},{10... | collective-permute-start | bytes 3145736 | tf_op jit(solution)/shard_map/d1b/ppermute | solution.py:209
  230.2 33.1 %collective-permute-start.41 = (bf16[256,2048]{1,0:T(8,128)(2,1)S(1)}, bf16[256,2048]{1,0:T(8,128)(2,1)S(1)}, u32[]{:S(2)}, u32[]{:S(2)}) collective-permute-start(bf16[256,2048]{1,0:T(8,128)(2,1)S(1)} %copy-done.35), channel_id=1, source_target_pairs={{0,4},{1,3},{2,6},{3,1},{4,0},{5,7},{6,2},{7,5},{8,12},{9,11},{10,... | collective-permute-start | bytes 3145736 | tf_op jit(solution)/shard_map/d2b/ppermute | solution.py:197
  242.0 75.6 %collective-permute-start.40 = (bf16[128,2048]{1,0:T(8,128)(2,1)S(1)}, bf16[128,2048]{1,0:T(8,128)(2,1)S(1)}, u32[]{:S(2)}, u32[]{:S(2)}) collective-permute-start(bf16[128,2048]{1,0:T(8,128)(2,1)S(1)} %add_convert_fusion.6), channel_id=1, source_target_pairs={{0,8},{8,0},{16,24},{24,16},{1,9},{9,1},{17,25},{25,17},{2,10},{10... | collective-permute-start | bytes 1572872 | tf_op jit(solution)/shard_map/d1z/ppermute | solution.py:209
  259.7 27.3 %collective-permute-start.27 = (bf16[256,2048]{1,0:T(8,128)(2,1)S(1)}, bf16[256,2048]{1,0:T(8,128)(2,1)S(1)}, u32[]{:S(2)}, u32[]{:S(2)}) collective-permute-start(bf16[256,2048]{1,0:T(8,128)(2,1)S(1)} %add_convert_fusion.1), channel_id=1, source_target_pairs={{0,4},{1,3},{2,6},{3,1},{4,0},{5,7},{6,2},{7,5},{8,12},{9,11},{10,... | collective-permute-start | bytes 3145736 | tf_op jit(solution)/shard_map/o0b/ppermute | solution.py:197
  264.2 43.0 %collective-permute-start.37 = (bf16[256,2048]{1,0:T(8,128)(2,1)S(1)}, bf16[256,2048]{1,0:T(8,128)(2,1)S(1)}, u32[]{:S(2)}, u32[]{:S(2)}) collective-permute-start(bf16[256,2048]{1,0:T(8,128)(2,1)S(1)} %add_convert_fusion), channel_id=1, source_target_pairs={{0,4},{1,3},{2,6},{3,1},{4,0},{5,7},{6,2},{7,5},{8,12},{9,11},{10,... | collective-permute-start | bytes 3145736 | tf_op jit(solution)/shard_map/d0b/ppermute | solution.py:197
  276.7 31.6 %collective-permute-start.42 = (bf16[128,2048]{1,0:T(8,128)(2,1)S(1)}, bf16[128,2048]{1,0:T(8,128)(2,1)S(1)}, u32[]{:S(2)}, u32[]{:S(2)}) collective-permute-start(bf16[128,2048]{1,0:T(8,128)(2,1)S(1)} %add_convert_fusion.5), channel_id=1, source_target_pairs={{0,2},{1,5},{2,0},{3,7},{4,6},{5,1},{6,4},{7,3},{8,10},{9,13},{10,... | collective-permute-start | bytes 1572872 | tf_op jit(solution)/shard_map/d2a/ppermute | solution.py:197
  283.6 26.3 %collective-permute-start.35 = (bf16[128,2048]{1,0:T(8,128)(2,1)S(1)}, bf16[128,2048]{1,0:T(8,128)(2,1)S(1)}, u32[]{:S(2)}, u32[]{:S(2)}) collective-permute-start(bf16[128,2048]{1,0:T(8,128)(2,1)S(1)} %add_convert_fusion.9), channel_id=1, source_target_pairs={{0,16},{8,24},{16,0},{24,8},{1,17},{9,25},{17,1},{25,9},{2,18},{10... | collective-permute-start | bytes 1572872 | tf_op jit(solution)/shard_map/o2z/ppermute | solution.py:209
  (66 other events, 1223.9 us)
